TPU v7x, 512 devices: a whole 4x4x16 slice. The times are simulated.
512 devices in a mesh: expert: 64 (over x, z), tensor: 8 (over y, core).
Axes of the slice: x: 4, y: 4, z: 16, core: 2. Of those that a mesh axis runs over, the one named last changes fastest.
Arguments:
- tokens: bfloat16 [1024, 7168], P('expert', 'tensor'), may hold values from -6 to 6
- expert_ids: int32 [1024, 8], P('expert'), may hold values from 0 to 31, as said below
- route_weights: float32 [1024, 8], P('expert'), may hold values from 0.05 to 1
- gate_weight: bfloat16 [64, 512, 7168], P('expert', 'tensor'), may hold values from -0.0625 to 0.0625
- up_weight: bfloat16 [64, 512, 7168], P('expert', 'tensor'), may hold values from -0.0625 to 0.0625
- down_weight: bfloat16 [64, 512, 7168], P('expert', 'tensor'), may hold values from -0.1875 to 0.1875
Outputs:
- mixed: bfloat16 [1024, 7168], P('expert', 'tensor')
Inputs may be any that keep to these rules, and one draw needn't show every extreme that they name: `expert_ids`: each row holds 8 different experts. One expert, the same for all tokens, is named by exactly 4 of the 16 tokens of every block of 16 consecutive tokens; every other expert by at most 4 tokens of a block.
All inputs are finite; a program needn't handle non-finite values.
Results may differ from a plain program's by a relative error of at most 0.015.
Values may be sent and summed in bfloat16 or wider, within the bound.
No kernel may reach another device: no remote copies, remote signals or barrier semaphores. Data moves between devices by JAX's collectives and lax.ppermute only.
A program may use at most 64 MiB of HBM per device.

v0:
```python
import jax
import jax.numpy as jnp
from jax import lax
from jax.experimental import pallas as pl
from jax.experimental.pallas import tpu as pltpu
from jax.sharding import PartitionSpec as P

F32 = jnp.float32
BF16 = jnp.bfloat16


def slot_onehot(ids, lanes, capacity, copies):
    tok_count, per_token = ids.shape
    lane = lax.broadcasted_iota(jnp.int32, (tok_count, lanes), 1)
    expert = lane // (capacity * copies)
    hit = jnp.zeros((tok_count, lanes), F32)
    for j in range(per_token):
        hit = hit + jnp.where(ids[:, j : j + 1] == expert, 1.0, 0.0)
    row = lax.broadcasted_iota(jnp.int32, (tok_count, tok_count), 0)
    col = lax.broadcasted_iota(jnp.int32, (tok_count, tok_count), 1)
    lower = jnp.where(col < row, 1.0, 0.0).astype(BF16)
    earlier = jnp.dot(lower, hit.astype(BF16), preferred_element_type=F32)
    slot = (lane % capacity).astype(F32)
    return jnp.where((hit > 0.5) & (earlier == slot), 1.0, 0.0), expert


def pack_kernel(capacity, copies, ids_ref, tok_ref, out_ref):
    lanes = out_ref.shape[0]
    select, _ = slot_onehot(ids_ref[...], lanes, capacity, copies)
    out_ref[...] = lax.dot_general(
        select.astype(BF16), tok_ref[...], (((0,), (0,)), ((), ())), preferred_element_type=F32
    ).astype(BF16)


def mix_kernel(capacity, copies, ids_ref, route_ref, mix_ref):
    lanes = mix_ref.shape[1]
    ids = ids_ref[...]
    route = route_ref[...]
    select, expert = slot_onehot(ids, lanes, capacity, copies)
    weight = jnp.zeros(select.shape, F32)
    for j in range(ids.shape[1]):
        weight = weight + jnp.where(ids[:, j : j + 1] == expert, route[:, j : j + 1], 0.0)
    mix_ref[...] = select * weight


def combine_kernel(mix_ref, rows_ref, out_ref):
    mix = mix_ref[...]
    high = mix.astype(BF16)
    low = (mix - high.astype(F32)).astype(BF16)
    rows = rows_ref[...]
    total = jnp.dot(high, rows, preferred_element_type=F32)
    total = total + jnp.dot(low, rows, preferred_element_type=F32)
    out_ref[...] = total.astype(BF16)


CORES = 2
VMEM_BYTES = 16 * 2**20


def moved_by(index, groups, ring, core, sign=1):
    rings = groups // CORES
    place = lax.rem(index // CORES + sign * ring + rings, rings)
    return place * CORES + lax.rem(lax.rem(index, CORES) + core, CORES)


def shift_pairs(groups, ring, core):
    rings = groups // CORES
    return [
        (i, (i // CORES + ring) % rings * CORES + (i + core) % CORES) for i in range(groups)
    ]


def cut_kernel(wide, gate_ref, up_ref, *outs):
    rings = len(outs)
    units = gate_ref.shape[0]
    chip = lax.axis_index("tensor") // CORES
    for ring, out in enumerate(outs):
        target = lax.rem(chip + ring, rings)
        cols = pl.ds(pl.multiple_of(target * wide, 128), wide)
        out[:units, :] = gate_ref[:, cols]
        out[units:, :] = up_ref[:, cols]


def chip_blocks(gate, up, width, groups):
    wide, rings = CORES * width, groups // CORES
    shape = jax.ShapeDtypeStruct((2 * gate.shape[0], wide), BF16)
    first, *rest = pl.pallas_call(
        lambda *refs: cut_kernel(wide, *refs),
        out_shape=[shape] * rings,
        compiler_params=pltpu.CompilerParams(vmem_limit_bytes=VMEM_BYTES),
        name="cut",
    )(gate, up)
    return [first] + [
        lax.ppermute(block, "tensor", shift_pairs(groups, ring + 1, 0))
        for ring, block in enumerate(rest)
    ]


def half_product(block_ref, rows_ref, half):
    width = rows_ref.shape[1]
    cols = pl.ds(pl.multiple_of(half * width, 128), width)
    return lax.dot_general(
        block_ref[:, cols], rows_ref[...], (((1,), (1,)), ((), ())), preferred_element_type=F32
    )


def near_kernel(rows_ref, *refs):
    *blocks, out_ref = refs
    chip, core = lax.axis_index("tensor") // CORES, lax.rem(lax.axis_index("tensor"), CORES)
    for ring, block in enumerate(blocks):
        source = lax.rem(chip - ring + len(blocks), len(blocks))
        out_ref[source] = half_product(block, rows_ref, core)


def far_kernel(rows_ref, near_ref, *refs):
    *blocks, out_ref = refs
    chip, core = lax.axis_index("tensor") // CORES, lax.rem(lax.axis_index("tensor"), CORES)
    for ring, block in enumerate(blocks):
        source = lax.rem(chip - ring + len(blocks), len(blocks))
        out_ref[source] = (near_ref[source] + half_product(block, rows_ref, 1 - core)).astype(BF16)


def hidden_kernel(partial_ref, out_ref):
    groups, units, _ = out_ref.shape
    act = partial_ref[0].astype(F32)
    for g in range(1, partial_ref.shape[0]):
        act = act + partial_ref[g].astype(F32)
    gate, up = act[:units], act[units:]
    hidden = (jax.nn.silu(gate) * up).astype(BF16)
    for g in range(groups):
        out_ref[g] = hidden


def chip_cut_kernel(wide, weight_ref, *outs):
    rings = len(outs)
    chip = lax.axis_index("tensor") // CORES
    for ring, out in enumerate(outs):
        target = lax.rem(chip + ring, rings)
        out[...] = weight_ref[:, pl.ds(pl.multiple_of(target * wide, 128), wide)]


def core_cut_kernel(*refs):
    *blocks, near_ref, far_ref = refs
    core = lax.rem(lax.axis_index("tensor"), CORES)
    units = blocks[0].shape[0]
    width = near_ref.shape[1]
    for ring, block in enumerate(blocks):
        rows = pl.ds(ring * units, units)
        near_ref[rows, :] = block[:, pl.ds(pl.multiple_of(core * width, 128), width)]
        far_ref[rows, :] = block[:, pl.ds(pl.multiple_of((1 - core) * width, 128), width)]


def down_columns(weight, width, groups):
    units = weight.shape[0]
    rings, wide = groups // CORES, CORES * width
    first, *rest = pl.pallas_call(
        lambda *refs: chip_cut_kernel(wide, *refs),
        out_shape=[jax.ShapeDtypeStruct((units, wide), BF16)] * rings,
        compiler_params=pltpu.CompilerParams(vmem_limit_bytes=VMEM_BYTES),
        name="chip_cut",
    )(weight)
    for ring in range(1, rings):
        rest[ring - 1] = lax.ppermute(
            rest[ring - 1], "tensor", shift_pairs(groups, ring, 0)
        )
    near, far = pl.pallas_call(
        core_cut_kernel,
        out_shape=[jax.ShapeDtypeStruct((rings * units, width), BF16)] * 2,
        compiler_params=pltpu.CompilerParams(vmem_limit_bytes=VMEM_BYTES),
        name="core_cut",
    )(first, *rest)
    return near, lax.ppermute(far, "tensor", shift_pairs(groups, 0, 1))


def down_kernel(hidden_ref, near_ref, far_ref, out_ref, held):
    groups, units, _ = hidden_ref.shape
    me = lax.axis_index("tensor")
    for core in range(CORES):
        for ring in range(groups // CORES):
            source = moved_by(me, groups, ring, core, sign=-1)
            held[core, pl.ds(ring * units, units), :] = hidden_ref[source]
    dims = (((0,), (0,)), ((), ()))
    total = lax.dot_general(held[0], near_ref[...], dims, preferred_element_type=F32)
    total = total + lax.dot_general(held[1], far_ref[...], dims, preferred_element_type=F32)
    out_ref[...] = total.astype(BF16)


def body(tokens, expert_ids, route_weights, gate_weight, up_weight, down_weight):
    devices_wide = lax.axis_size("expert")
    groups = lax.axis_size("tensor")
    experts = devices_wide // 2
    tok_count, per_token = expert_ids.shape
    width = tokens.shape[1]
    units = gate_weight.shape[1]
    capacity = min(tok_count, tok_count * per_token // experts)
    arrived_count = devices_wide * capacity

    packed = pl.pallas_call(
        lambda *refs: pack_kernel(capacity, 2, *refs),
        out_shape=jax.ShapeDtypeStruct((arrived_count, width), BF16),
        compiler_params=pltpu.CompilerParams(vmem_limit_bytes=VMEM_BYTES),
        name="pack",
    )(expert_ids, tokens)
    mix = pl.pallas_call(
        lambda *refs: mix_kernel(capacity, 2, *refs),
        out_shape=jax.ShapeDtypeStruct((tok_count, arrived_count), F32),
        compiler_params=pltpu.CompilerParams(vmem_limit_bytes=VMEM_BYTES),
        name="mix",
    )(expert_ids, route_weights)

    blocks = chip_blocks(gate_weight[0], up_weight[0], width, groups)
    arrived = lax.all_to_all(
        packed.reshape(devices_wide, capacity, width), "expert", 0, 0, tiled=True
    )
    arrived = arrived.reshape(arrived_count, width)
    down_near, down_far = down_columns(down_weight[0], width, groups)

    partner = lax.ppermute(arrived, "tensor", shift_pairs(groups, 0, 1))
    rings = groups // CORES
    near = pl.pallas_call(
        near_kernel,
        out_shape=jax.ShapeDtypeStruct((rings, 2 * units, arrived_count), F32),
        compiler_params=pltpu.CompilerParams(vmem_limit_bytes=VMEM_BYTES),
        cost_estimate=pl.CostEstimate(flops=10**9, bytes_accessed=10**6, transcendentals=0),
        name="near",
    )(arrived, *blocks)
    partial = pl.pallas_call(
        far_kernel,
        out_shape=jax.ShapeDtypeStruct((rings, 2 * units, arrived_count), BF16),
        compiler_params=pltpu.CompilerParams(vmem_limit_bytes=VMEM_BYTES),
        name="far",
    )(partner, near, *blocks)
    same_core = [list(range(core, groups, CORES)) for core in range(CORES)]
    partial = lax.all_to_all(
        partial, "tensor", 0, 0, axis_index_groups=same_core, tiled=True
    )
    hidden = pl.pallas_call(
        hidden_kernel,
        out_shape=jax.ShapeDtypeStruct((groups, units, arrived_count), BF16),
        compiler_params=pltpu.CompilerParams(vmem_limit_bytes=VMEM_BYTES),
        name="hidden",
    )(partial)
    hidden, mix = lax.optimization_barrier((hidden, mix))
    hidden = lax.all_to_all(hidden, "tensor", 0, 0, tiled=True)
    half_out = pl.pallas_call(
        down_kernel,
        out_shape=jax.ShapeDtypeStruct((arrived_count, width), BF16),
        scratch_shapes=[pltpu.VMEM((2, groups // 2 * units, arrived_count), BF16)],
        compiler_params=pltpu.CompilerParams(vmem_limit_bytes=VMEM_BYTES),
        name="down",
    )(hidden, down_near, down_far)
    returned = lax.all_to_all(
        half_out.reshape(devices_wide, capacity, width), "expert", 0, 0, tiled=True
    ).reshape(arrived_count, width)
    return pl.pallas_call(
        combine_kernel,
        out_shape=jax.ShapeDtypeStruct((tok_count, width), BF16),
        compiler_params=pltpu.CompilerParams(vmem_limit_bytes=VMEM_BYTES),
        name="combine",
    )(mix, returned)


def solution(mesh):
    placed = (
        P("expert", "tensor"),
        P("expert", None),
        P("expert", None),
        P("expert", "tensor", None),
        P("expert", "tensor", None),
        P("expert", "tensor", None),
    )
    def step(*args):
        return body(*args)

    step = jax.shard_map(
        step, mesh=mesh, in_specs=placed, out_specs=P("expert", "tensor"), check_vma=False
    )
    return step
```

profile of v0, /device:TPU:6, one launch (start us, length us, event | category | flops | bytes accessed | tf_op | source)
XLA Modules:
  0.0 139.2 jit_solution(13848698787396756270)
XLA Ops:
  0.0 0.8 copy.7.refs_0_
  0.8 0.7 copy-done.7
  1.5 0.5 pack.1
  2.0 0.0 copy-start
  2.0 0.9 reshape.12
  2.9 19.1 %all-to-all-start = ((bf16[64,4,896]{2,1,0:T(4,128)(2,1)}), bf16[64,4,896]{2,1,0:T(4,128)(2,1)}, u32[]{:S(2)}, u32[]{:S(2)}) async-start(bf16[64,4,896]{2,1,0:T(4,128)(2,1)} %reshape.12), calls=%async_computation | async-start | bytes 917504 | tf_op jit(solution)/shard_map/all_to_all | solution.py:212
  22.0 0.0 copy-done
  22.1 0.9 chip_cut.1
  22.9 0.7 copy-done.8
  23.6 3.5 %collective-permute-start.4 = (bf16[64,1792]{1,0:T(8,128)(2,1)}, bf16[64,1792]{1,0:T(8,128)(2,1)S(1)}, u32[]{:S(2)}, u32[]{:S(2)}) collective-permute-start(bf16[64,1792]{1,0:T(8,128)(2,1)} %get-tuple-element.24), channel_id=1, source_target_pairs={{0,2},{1,3},{2,4},{3,5},{4,6},{5,7},{6,0},{7,1},{8,10},{9,11},{10,... | collective-permute-start | bytes 688136 | tf_op jit(solution)/shard_map/ppermute | solution.py:163
  27.1 4.8 %collective-permute-start.5 = (bf16[64,1792]{1,0:T(8,128)(2,1)}, bf16[64,1792]{1,0:T(8,128)(2,1)S(1)}, u32[]{:S(2)}, u32[]{:S(2)}) collective-permute-start(bf16[64,1792]{1,0:T(8,128)(2,1)} %get-tuple-element.25), channel_id=1, source_target_pairs={{0,4},{1,5},{2,6},{3,7},{4,0},{5,1},{6,2},{7,3},{8,12},{9,13},{10,... | collective-permute-start | bytes 688136 | tf_op jit(solution)/shard_map/ppermute | solution.py:163
  31.9 0.0 copy-done.1
  31.9 0.0 copy-done.2
  31.9 1.2 cut.1
  33.1 0.8 copy-done.3
  33.9 1.9 %collective-permute-start.1 = (bf16[128,1792]{1,0:T(8,128)(2,1)}, bf16[128,1792]{1,0:T(8,128)(2,1)S(1)}, u32[]{:S(2)}, u32[]{:S(2)}) collective-permute-start(bf16[128,1792]{1,0:T(8,128)(2,1)} %get-tuple-element.18), channel_id=1, source_target_pairs={{0,2},{1,3},{2,4},{3,5},{4,6},{5,7},{6,0},{7,1},{8,10},{9,11},{10,... | collective-permute-start | bytes 1376264 | tf_op jit(solution)/shard_map/ppermute | solution.py:94
  35.8 4.7 %collective-permute-start.2 = (bf16[128,1792]{1,0:T(8,128)(2,1)}, bf16[128,1792]{1,0:T(8,128)(2,1)S(1)}, u32[]{:S(2)}, u32[]{:S(2)}) collective-permute-start(bf16[128,1792]{1,0:T(8,128)(2,1)} %get-tuple-element.19), channel_id=1, source_target_pairs={{0,4},{1,5},{2,6},{3,7},{4,0},{5,1},{6,2},{7,3},{8,12},{9,13},{10,... | collective-permute-start | bytes 1376264 | tf_op jit(solution)/shard_map/ppermute | solution.py:94
  40.6 2.5 %collective-permute-start.3 = (bf16[128,1792]{1,0:T(8,128)(2,1)}, bf16[128,1792]{1,0:T(8,128)(2,1)S(1)}, u32[]{:S(2)}, u32[]{:S(2)}) collective-permute-start(bf16[128,1792]{1,0:T(8,128)(2,1)} %get-tuple-element.20), channel_id=1, source_target_pairs={{0,6},{1,7},{2,0},{3,1},{4,2},{5,3},{6,4},{7,5},{8,14},{9,15},{10,... | collective-permute-start | bytes 1376264 | tf_op jit(solution)/shard_map/ppermute | solution.py:94
  43.1 7.7 %all-to-all-done = bf16[64,4,896]{2,1,0:T(4,128)(2,1)} async-done(((bf16[64,4,896]{2,1,0:T(4,128)(2,1)}), bf16[64,4,896]{2,1,0:T(4,128)(2,1)}, u32[]{:S(2)}, u32[]{:S(2)}) %all-to-all-start) | async-done | bytes 458784 | tf_op jit(solution)/shard_map/all_to_all | solution.py:212
  50.8 1.1 reshape.13.rows_ref
  51.9 0.0 collective-permute-done.4.refs_1_
  51.9 1.9 %collective-permute-start = (bf16[256,896]{1,0:T(8,128)(2,1)S(1)}, bf16[256,896]{1,0:T(8,128)(2,1)S(1)}, u32[]{:S(2)}, u32[]{:S(2)}) collective-permute-start(bf16[256,896]{1,0:T(8,128)(2,1)S(1)} %reshape.13.rows_ref), channel_id=1, source_target_pairs={{0,1},{1,0},{2,3},{3,2},{4,5},{5,4},{6,7},{7,6},{8,9},{9,8},{10,11... | collective-permute-start | bytes 1376264 | tf_op jit(solution)/shard_map/ppermute | solution.py:218
  53.8 0.0 collective-permute-done.5.refs_2_
  53.9 0.7 copy-done.5
  54.5 4.9 %collective-permute-start.6 = (bf16[64,1792]{1,0:T(8,128)(2,1)S(1)}, bf16[64,1792]{1,0:T(8,128)(2,1)S(1)}, u32[]{:S(2)}, u32[]{:S(2)}) collective-permute-start(bf16[64,1792]{1,0:T(8,128)(2,1)S(1)} %copy-done.9), channel_id=1, source_target_pairs={{0,6},{1,7},{2,0},{3,1},{4,2},{5,3},{6,4},{7,5},{8,14},{9,15},{10,... | collective-permute-start | bytes 688136 | tf_op jit(solution)/shard_map/ppermute | solution.py:163
  59.5 6.2 %collective-permute-done.6.refs_3_ = bf16[64,1792]{1,0:T(8,128)(2,1)S(1)} collective-permute-done((bf16[64,1792]{1,0:T(8,128)(2,1)S(1)}, bf16[64,1792]{1,0:T(8,128)(2,1)S(1)}, u32[]{:S(2)}, u32[]{:S(2)}) %collective-permute-start.6) | collective-permute-done | bytes 229408 | tf_op jit(solution)/shard_map/ppermute | solution.py:163
  65.6 0.9 copy-done.6
  66.6 0.8 core_cut.1
  67.4 1.9 %collective-permute-start.7 = (bf16[256,896]{1,0:T(8,128)(2,1)}, bf16[256,896]{1,0:T(8,128)(2,1)S(1)}, u32[]{:S(2)}, u32[]{:S(2)}) collective-permute-start(bf16[256,896]{1,0:T(8,128)(2,1)} %get-tuple-element.28), channel_id=1, source_target_pairs={{0,1},{1,0},{2,3},{3,2},{4,5},{5,4},{6,7},{7,6},{8,9},{9,8},{10,11... | collective-permute-start | bytes 1376264 | tf_op jit(solution)/shard_map/ppermute | solution.py:172
  69.3 0.0 collective-permute-done.1.refs_1_
  69.3 0.0 collective-permute-done.2.refs_2_
  69.4 0.0 collective-permute-done.3.refs_3_
  69.4 0.7 near.1.near_ref
  70.1 0.0 collective-permute-done.rows_ref
  70.1 1.4 %far.1 = bf16[4,128,256]{2,1,0:T(8,128)(2,1)} custom-call(bf16[256,896]{1,0:T(8,128)(2,1)S(1)} %collective-permute-done.rows_ref, f32[4,128,256]{2,1,0:T(8,128)S(1)} %near.1.near_ref, bf16[128,1792]{1,0:T(8,128)(2,1)S(1)} %copy-done.4, bf16[128,1792]{1,0:T(8,128)(2,1)S(1)} %collective-permute-done.1.refs_1_, ...), custom_call_target="tpu_custom_call" | custom-call | tf_op jit(solution)/shard_map/far/pallas_call | solution.py:227
  71.5 4.4 %all-to-all-start.1 = ((bf16[4,128,256]{2,1,0:T(8,128)(2,1)}), bf16[4,128,256]{2,1,0:T(8,128)(2,1)S(1)}, u32[]{:S(2)}, u32[]{:S(2)}) async-start(bf16[4,128,256]{2,1,0:T(8,128)(2,1)} %far.1), calls=%async_computation.1 | async-start | bytes 524288 | tf_op jit(solution)/shard_map/all_to_all | solution.py:234
  76.0 0.1 copy.9.refs_1_
  76.0 0.2 mix.1.mix_ref
  76.3 7.0 %all-to-all-done.1.partial_ref = bf16[4,128,256]{2,1,0:T(8,128)(2,1)S(1)} async-done(((bf16[4,128,256]{2,1,0:T(8,128)(2,1)}), bf16[4,128,256]{2,1,0:T(8,128)(2,1)S(1)}, u32[]{:S(2)}, u32[]{:S(2)}) %all-to-all-start.1) | async-done | bytes 262176 | tf_op jit(solution)/shard_map/all_to_all | solution.py:234
  83.3 0.7 hidden.1
  84.0 3.4 %all-to-all-start.2 = ((bf16[8,64,256]{2,1,0:T(8,128)(2,1)}), bf16[8,64,256]{2,1,0:T(8,128)(2,1)S(1)}, u32[]{:S(2)}, u32[]{:S(2)}) async-start(bf16[8,64,256]{2,1,0:T(8,128)(2,1)} %hidden.1), calls=%async_computation.2 | async-start | bytes 524288 | tf_op jit(solution)/shard_map/all_to_all | solution.py:244
  87.4 0.0 collective-permute-done.7.far_ref
  87.5 7.4 %all-to-all-done.2.hidden_ref = bf16[8,64,256]{2,1,0:T(8,128)(2,1)S(1)} async-done(((bf16[8,64,256]{2,1,0:T(8,128)(2,1)}), bf16[8,64,256]{2,1,0:T(8,128)(2,1)S(1)}, u32[]{:S(2)}, u32[]{:S(2)}) %all-to-all-start.2) | async-done | bytes 262176 | tf_op jit(solution)/shard_map/all_to_all | solution.py:244
  94.9 0.5 down.1
  95.4 0.1 reshape.14
  95.5 42.8 %all_to_all.20 = bf16[64,4,896]{2,1,0:T(4,128)(2,1)S(1)} all-to-all(bf16[64,4,896]{2,1,0:T(4,128)(2,1)S(1)} %reshape.14), channel_id=1, replica_groups=mesh['expert'=64,'tensor'=8] {'expert'}, dimensions={0} | all-to-all | bytes 917504 | tf_op jit(solution)/shard_map/all_to_all | solution.py:252
  138.3 0.1 reshape.15.rows_ref
  138.4 0.9 combine.1
  (13 shorter events, 0.0 us)
Async XLA Ops:
  0.8 0.7 copy-start.7
  2.0 20.0 %copy-start = (bf16[1,64,7168]{2,1,0:T(8,128)(2,1)S(1)}, bf16[1,64,7168]{2,1,0:T(8,128)(2,1)}, u32[]{:S(2)}) copy-start(bf16[1,64,7168]{2,1,0:T(8,128)(2,1)} %param.11) | copy-start | bytes 2752516
  2.9 29.0 %copy-start.1 = (bf16[1,64,7168]{2,1,0:T(8,128)(2,1)S(1)}, bf16[1,64,7168]{2,1,0:T(8,128)(2,1)}, u32[]{:S(2)}) copy-start(bf16[1,64,7168]{2,1,0:T(8,128)(2,1)} %param.9) | copy-start | bytes 2752516
  2.9 29.0 %copy-start.2 = (bf16[1,64,7168]{2,1,0:T(8,128)(2,1)S(1)}, bf16[1,64,7168]{2,1,0:T(8,128)(2,1)}, u32[]{:S(2)}) copy-start(bf16[1,64,7168]{2,1,0:T(8,128)(2,1)} %param.10) | copy-start | bytes 2752516
  2.9 47.8 %all-to-all-start = ((bf16[64,4,896]{2,1,0:T(4,128)(2,1)}), bf16[64,4,896]{2,1,0:T(4,128)(2,1)}, u32[]{:S(2)}, u32[]{:S(2)}) async-start(bf16[64,4,896]{2,1,0:T(4,128)(2,1)} %reshape.12), calls=%async_computation | async-start | bytes 917504 | tf_op jit(solution)/shard_map/all_to_all | solution.py:212
  22.9 0.7 copy-start.8
  23.6 28.3 %collective-permute-start.4 = (bf16[64,1792]{1,0:T(8,128)(2,1)}, bf16[64,1792]{1,0:T(8,128)(2,1)S(1)}, u32[]{:S(2)}, u32[]{:S(2)}) collective-permute-start(bf16[64,1792]{1,0:T(8,128)(2,1)} %get-tuple-element.24), channel_id=1, source_target_pairs={{0,2},{1,3},{2,4},{3,5},{4,6},{5,7},{6,0},{7,1},{8,10},{9,11},{10,... | collective-permute-start | bytes 688136 | tf_op jit(solution)/shard_map/ppermute | solution.py:163
  27.1 26.8 %collective-permute-start.5 = (bf16[64,1792]{1,0:T(8,128)(2,1)}, bf16[64,1792]{1,0:T(8,128)(2,1)S(1)}, u32[]{:S(2)}, u32[]{:S(2)}) collective-permute-start(bf16[64,1792]{1,0:T(8,128)(2,1)} %get-tuple-element.25), channel_id=1, source_target_pairs={{0,4},{1,5},{2,6},{3,7},{4,0},{5,1},{6,2},{7,3},{8,12},{9,13},{10,... | collective-permute-start | bytes 688136 | tf_op jit(solution)/shard_map/ppermute | solution.py:163
  33.1 0.8 copy-start.3
  33.9 35.4 %collective-permute-start.1 = (bf16[128,1792]{1,0:T(8,128)(2,1)}, bf16[128,1792]{1,0:T(8,128)(2,1)S(1)}, u32[]{:S(2)}, u32[]{:S(2)}) collective-permute-start(bf16[128,1792]{1,0:T(8,128)(2,1)} %get-tuple-element.18), channel_id=1, source_target_pairs={{0,2},{1,3},{2,4},{3,5},{4,6},{5,7},{6,0},{7,1},{8,10},{9,11},{10,... | collective-permute-start | bytes 1376264 | tf_op jit(solution)/shard_map/ppermute | solution.py:94
  35.8 33.5 %collective-permute-start.2 = (bf16[128,1792]{1,0:T(8,128)(2,1)}, bf16[128,1792]{1,0:T(8,128)(2,1)S(1)}, u32[]{:S(2)}, u32[]{:S(2)}) collective-permute-start(bf16[128,1792]{1,0:T(8,128)(2,1)} %get-tuple-element.19), channel_id=1, source_target_pairs={{0,4},{1,5},{2,6},{3,7},{4,0},{5,1},{6,2},{7,3},{8,12},{9,13},{10,... | collective-permute-start | bytes 1376264 | tf_op jit(solution)/shard_map/ppermute | solution.py:94
  40.5 14.0 %copy-start.9 = (bf16[64,1792]{1,0:T(8,128)(2,1)S(1)}, bf16[64,1792]{1,0:T(8,128)(2,1)}, u32[]{:S(2)}) copy-start(bf16[64,1792]{1,0:T(8,128)(2,1)} %copy-done.8) | copy-start | bytes 688132
  40.6 28.8 %collective-permute-start.3 = (bf16[128,1792]{1,0:T(8,128)(2,1)}, bf16[128,1792]{1,0:T(8,128)(2,1)S(1)}, u32[]{:S(2)}, u32[]{:S(2)}) collective-permute-start(bf16[128,1792]{1,0:T(8,128)(2,1)} %get-tuple-element.20), channel_id=1, source_target_pairs={{0,6},{1,7},{2,0},{3,1},{4,2},{5,3},{6,4},{7,5},{8,14},{9,15},{10,... | collective-permute-start | bytes 1376264 | tf_op jit(solution)/shard_map/ppermute | solution.py:94
  51.9 18.2 %collective-permute-start = (bf16[256,896]{1,0:T(8,128)(2,1)S(1)}, bf16[256,896]{1,0:T(8,128)(2,1)S(1)}, u32[]{:S(2)}, u32[]{:S(2)}) collective-permute-start(bf16[256,896]{1,0:T(8,128)(2,1)S(1)} %reshape.13.rows_ref), channel_id=1, source_target_pairs={{0,1},{1,0},{2,3},{3,2},{4,5},{5,4},{6,7},{7,6},{8,9},{9,8},{10,11... | collective-permute-start | bytes 1376264 | tf_op jit(solution)/shard_map/ppermute | solution.py:218
  53.9 0.7 copy-start.5
  54.5 11.1 %collective-permute-start.6 = (bf16[64,1792]{1,0:T(8,128)(2,1)S(1)}, bf16[64,1792]{1,0:T(8,128)(2,1)S(1)}, u32[]{:S(2)}, u32[]{:S(2)}) collective-permute-start(bf16[64,1792]{1,0:T(8,128)(2,1)S(1)} %copy-done.9), channel_id=1, source_target_pairs={{0,6},{1,7},{2,0},{3,1},{4,2},{5,3},{6,4},{7,5},{8,14},{9,15},{10,... | collective-permute-start | bytes 688136 | tf_op jit(solution)/shard_map/ppermute | solution.py:163
  65.6 0.9 copy-start.6
  66.6 2.8 %copy-start.4 = (bf16[128,1792]{1,0:T(8,128)(2,1)S(1)}, bf16[128,1792]{1,0:T(8,128)(2,1)}, u32[]{:S(2)}) copy-start(bf16[128,1792]{1,0:T(8,128)(2,1)} %copy-done.3) | copy-start | bytes 1376260
  67.4 20.0 %collective-permute-start.7 = (bf16[256,896]{1,0:T(8,128)(2,1)}, bf16[256,896]{1,0:T(8,128)(2,1)S(1)}, u32[]{:S(2)}, u32[]{:S(2)}) collective-permute-start(bf16[256,896]{1,0:T(8,128)(2,1)} %get-tuple-element.28), channel_id=1, source_target_pairs={{0,1},{1,0},{2,3},{3,2},{4,5},{5,4},{6,7},{7,6},{8,9},{9,8},{10,11... | collective-permute-start | bytes 1376264 | tf_op jit(solution)/shard_map/ppermute | solution.py:172
  71.5 4.4 %copy-start.10 = (f32[16,8]{0,1:T(8,128)S(1)}, f32[16,8]{0,1:T(8,128)}, u32[]{:S(2)}) copy-start(f32[16,8]{0,1:T(8,128)} %param.8) | copy-start | bytes 1540
  71.5 11.7 %all-to-all-start.1 = ((bf16[4,128,256]{2,1,0:T(8,128)(2,1)}), bf16[4,128,256]{2,1,0:T(8,128)(2,1)S(1)}, u32[]{:S(2)}, u32[]{:S(2)}) async-start(bf16[4,128,256]{2,1,0:T(8,128)(2,1)} %far.1), calls=%async_computation.1 | async-start | bytes 524288 | tf_op jit(solution)/shard_map/all_to_all | solution.py:234
  84.0 10.8 %all-to-all-start.2 = ((bf16[8,64,256]{2,1,0:T(8,128)(2,1)}), bf16[8,64,256]{2,1,0:T(8,128)(2,1)S(1)}, u32[]{:S(2)}, u32[]{:S(2)}) async-start(bf16[8,64,256]{2,1,0:T(8,128)(2,1)} %hidden.1), calls=%async_computation.2 | async-start | bytes 524288 | tf_op jit(solution)/shard_map/all_to_all | solution.py:244
where the time goes:
time: 140 us; the launch traced here: 139 us
  starting transfers between devices  53 us (38%)
  blocking collectives  42.8 us (31%)
  waiting for transfers between devices  28.4 us (20%)
  Pallas kernels  7.88 us (6%)
  local copies, waits for them, and re-layouts  6.92 us (5%)
    all_to_all x1, blocking collectives, body(): lax.all_to_all(half_out.reshape(devices_wide, capacity, width), 'expert',...  42.8 us
    all_to_all x1, starting transfers between devices, body(): lax.all_to_all(packed.reshape(devices_wide, capacity, width), 'expert', 0...  19.1 us
    ppermute x3, starting transfers between devices, down_columns(): lax.ppermute(rest[ring - 1], 'tensor', shift_pairs(groups, ring, 0))  13.2 us
    ppermute x3, starting transfers between devices, chip_blocks(): lax.ppermute(block, 'tensor', shift_pairs(groups, ring + 1, 0))  9.1 us
    all_to_all x1, waiting for transfers between devices, body(): lax.all_to_all(packed.reshape(devices_wide, capacity, width), 'expert', 0...  7.72 us
    all_to_all x1, waiting for transfers between devices, body(): hidden = lax.all_to_all(hidden, 'tensor', 0, 0, tiled=True)  7.42 us
    all_to_all x1, waiting for transfers between devices, body(): lax.all_to_all(partial, 'tensor', 0, 0, axis_index_groups=same_core, tile...  7.02 us
    ppermute x3, waiting for transfers between devices, down_columns(): lax.ppermute(rest[ring - 1], 'tensor', shift_pairs(groups, ring, 0))  6.18 us
  transfers between devices with their start and end apart: 11, of which 4 were waited for; matrix products, arithmetic and copies ran while one was open for 1% of the time, Pallas kernels for 4%

commit v1 on v0

--- a/solution.py
+++ b/solution.py
@@ -9,37 +9,35 @@
 BF16 = jnp.bfloat16
 
 
-def slot_onehot(ids, lanes, capacity, copies):
-    tok_count, per_token = ids.shape
-    lane = lax.broadcasted_iota(jnp.int32, (tok_count, lanes), 1)
-    expert = lane // (capacity * copies)
-    hit = jnp.zeros((tok_count, lanes), F32)
+def slot_onehot(ids, slots, capacity, copies):
+    per_token, tok_count = ids.shape
+    slot = lax.broadcasted_iota(jnp.int32, (slots, tok_count), 0)
+    expert = slot // (capacity * copies)
+    hit = jnp.zeros((slots, tok_count), F32)
     for j in range(per_token):
-        hit = hit + jnp.where(ids[:, j : j + 1] == expert, 1.0, 0.0)
+        hit = hit + jnp.where(ids[j : j + 1, :] == expert, 1.0, 0.0)
     row = lax.broadcasted_iota(jnp.int32, (tok_count, tok_count), 0)
     col = lax.broadcasted_iota(jnp.int32, (tok_count, tok_count), 1)
-    lower = jnp.where(col < row, 1.0, 0.0).astype(BF16)
-    earlier = jnp.dot(lower, hit.astype(BF16), preferred_element_type=F32)
-    slot = (lane % capacity).astype(F32)
-    return jnp.where((hit > 0.5) & (earlier == slot), 1.0, 0.0), expert
-
-
-def pack_kernel(capacity, copies, ids_ref, tok_ref, out_ref):
-    lanes = out_ref.shape[0]
-    select, _ = slot_onehot(ids_ref[...], lanes, capacity, copies)
-    out_ref[...] = lax.dot_general(
-        select.astype(BF16), tok_ref[...], (((0,), (0,)), ((), ())), preferred_element_type=F32
-    ).astype(BF16)
+    before = jnp.where(row < col, 1.0, 0.0).astype(BF16)
+    earlier = jnp.dot(hit.astype(BF16), before, preferred_element_type=F32)
+    rank = (slot % capacity).astype(F32)
+    return jnp.where((hit > 0.5) & (earlier == rank), 1.0, 0.0), expert
+
+
+def pack_kernel(copies, ids_ref, tok_ref, out_ref):
+    peers, capacity, width = out_ref.shape
+    select, _ = slot_onehot(ids_ref[...], peers * capacity, capacity, copies)
+    packed = jnp.dot(select.astype(BF16), tok_ref[...], preferred_element_type=F32)
+    out_ref[...] = packed.reshape(peers, capacity, width).astype(BF16)
 
 
 def mix_kernel(capacity, copies, ids_ref, route_ref, mix_ref):
-    lanes = mix_ref.shape[1]
     ids = ids_ref[...]
     route = route_ref[...]
-    select, expert = slot_onehot(ids, lanes, capacity, copies)
+    select, expert = slot_onehot(ids, mix_ref.shape[0], capacity, copies)
     weight = jnp.zeros(select.shape, F32)
-    for j in range(ids.shape[1]):
-        weight = weight + jnp.where(ids[:, j : j + 1] == expert, route[:, j : j + 1], 0.0)
+    for j in range(ids.shape[0]):
+        weight = weight + jnp.where(ids[j : j + 1, :] == expert, route[j : j + 1, :], 0.0)
     mix_ref[...] = select * weight
 
 
@@ -48,13 +46,14 @@
     high = mix.astype(BF16)
     low = (mix - high.astype(F32)).astype(BF16)
     rows = rows_ref[...]
-    total = jnp.dot(high, rows, preferred_element_type=F32)
-    total = total + jnp.dot(low, rows, preferred_element_type=F32)
+    dims = (((0,), (0,)), ((), ()))
+    total = lax.dot_general(high, rows, dims, preferred_element_type=F32)
+    total = total + lax.dot_general(low, rows, dims, preferred_element_type=F32)
     out_ref[...] = total.astype(BF16)
 
 
 CORES = 2
-VMEM_BYTES = 16 * 2**20
+VMEM_BYTES = 10 * 2**20
 
 
 def moved_by(index, groups, ring, core, sign=1):
@@ -87,7 +86,6 @@
     first, *rest = pl.pallas_call(
         lambda *refs: cut_kernel(wide, *refs),
         out_shape=[shape] * rings,
-        compiler_params=pltpu.CompilerParams(vmem_limit_bytes=VMEM_BYTES),
         name="cut",
     )(gate, up)
     return [first] + [
@@ -156,7 +154,6 @@
     first, *rest = pl.pallas_call(
         lambda *refs: chip_cut_kernel(wide, *refs),
         out_shape=[jax.ShapeDtypeStruct((units, wide), BF16)] * rings,
-        compiler_params=pltpu.CompilerParams(vmem_limit_bytes=VMEM_BYTES),
         name="chip_cut",
     )(weight)
     for ring in range(1, rings):
@@ -195,23 +192,21 @@
     capacity = min(tok_count, tok_count * per_token // experts)
     arrived_count = devices_wide * capacity
 
+    ids = expert_ids.T
     packed = pl.pallas_call(
-        lambda *refs: pack_kernel(capacity, 2, *refs),
-        out_shape=jax.ShapeDtypeStruct((arrived_count, width), BF16),
-        compiler_params=pltpu.CompilerParams(vmem_limit_bytes=VMEM_BYTES),
+        lambda *refs: pack_kernel(2, *refs),
+        out_shape=jax.ShapeDtypeStruct((devices_wide, capacity, width), BF16),
         name="pack",
-    )(expert_ids, tokens)
+    )(ids, tokens)
     mix = pl.pallas_call(
         lambda *refs: mix_kernel(capacity, 2, *refs),
-        out_shape=jax.ShapeDtypeStruct((tok_count, arrived_count), F32),
+        out_shape=jax.ShapeDtypeStruct((arrived_count, tok_count), F32),
         compiler_params=pltpu.CompilerParams(vmem_limit_bytes=VMEM_BYTES),
         name="mix",
-    )(expert_ids, route_weights)
+    )(ids, route_weights.T)
 
     blocks = chip_blocks(gate_weight[0], up_weight[0], width, groups)
-    arrived = lax.all_to_all(
-        packed.reshape(devices_wide, capacity, width), "expert", 0, 0, tiled=True
-    )
+    arrived = lax.all_to_all(packed, "expert", 0, 0, tiled=True)
     arrived = arrived.reshape(arrived_count, width)
     down_near, down_far = down_columns(down_weight[0], width, groups)
 

time: 140 us -> 139 us (level)
  local copies, waits for them, and re-layouts: 6.92 us -> 0.34 us
  Pallas kernels: 7.88 us -> 12.3 us
  waiting for transfers between devices: 28.4 us -> 30.1 us
    unnamed x24 -> x10, local copies, waits for them, and re-layouts: 4.68 us -> 0.02 us
    ppermute x3, waiting for transfers between devices: 6.18 us -> 9.25 us  [down_columns(): lax.ppermute(rest[ring - 1], 'tensor', shift_pairs(groups, ring, 0))]
    pallas_call x1, Pallas kernels: 1.21 us -> 2.83 us  [chip_blocks(): pl.pallas_call(lambda *refs: cut_kernel(wide, *refs), out_shape=[shape] *...]
    pallas_call x1, Pallas kernels: 0.52 us -> 1.97 us  [body(): pl.pallas_call(lambda *refs: pack_kernel(2, *refs), out_shape=jax.ShapeDt...]
  transfers between devices with their start and end apart: 11 -> 11, of which waited for: 4 -> 4; matrix products, arithmetic and copies ran while one was open for 1% -> 0% of each run, Pallas kernels for 4% -> 6%
where the time goes in v1:
time: 139 us; the launch traced here: 138 us
  starting transfers between devices  52.4 us (38%)
  blocking collectives  43.2 us (31%)
  waiting for transfers between devices  30.1 us (22%)
  Pallas kernels  12.3 us (9%)
    all_to_all x1, blocking collectives, body(): lax.all_to_all(half_out.reshape(devices_wide, capacity, width), 'expert',...  43.2 us
    all_to_all x1, starting transfers between devices, body(): arrived = lax.all_to_all(packed, 'expert', 0, 0, tiled=True)  18.8 us
    ppermute x3, starting transfers between devices, down_columns(): lax.ppermute(rest[ring - 1], 'tensor', shift_pairs(groups, ring, 0))  13.2 us
    ppermute x3, waiting for transfers between devices, down_columns(): lax.ppermute(rest[ring - 1], 'tensor', shift_pairs(groups, ring, 0))  9.25 us
    ppermute x3, starting transfers between devices, chip_blocks(): lax.ppermute(block, 'tensor', shift_pairs(groups, ring + 1, 0))  9.1 us
    all_to_all x1, waiting for transfers between devices, body(): hidden = lax.all_to_all(hidden, 'tensor', 0, 0, tiled=True)  7.42 us
    all_to_all x1, waiting for transfers between devices, body(): lax.all_to_all(partial, 'tensor', 0, 0, axis_index_groups=same_core, tile...  7.05 us
    all_to_all x1, waiting for transfers between devices, body(): arrived = lax.all_to_all(packed, 'expert', 0, 0, tiled=True)  6.33 us
  transfers between devices with their start and end apart: 11, of which 4 were waited for; matrix products, arithmetic and copies ran while one was open for 0% of the time, Pallas kernels for 6%

profile of v1, /device:TPU:6, one launch (start us, length us, event | category | flops | bytes accessed | tf_op | source)
XLA Modules:
  0.0 138.5 jit_solution(18393742299720771934)
XLA Ops:
  0.0 2.0 %pack.1 = bf16[64,4,896]{2,1,0:T(4,128)(2,1)} custom-call(s32[8,16]{1,0:T(8,128)} %bitcast.5, bf16[16,896]{1,0:T(8,128)(2,1)} %refs_1_.1), custom_call_target="tpu_custom_call" | custom-call | tf_op jit(solution)/shard_map/pack/pallas_call | solution.py:196
  2.0 18.8 %all-to-all-start = ((bf16[64,4,896]{2,1,0:T(4,128)(2,1)}), bf16[64,4,896]{2,1,0:T(4,128)(2,1)S(1)}, u32[]{:S(2)}, u32[]{:S(2)}) async-start(bf16[64,4,896]{2,1,0:T(4,128)(2,1)} %pack.1), calls=%async_computation | async-start | bytes 917504 | tf_op jit(solution)/shard_map/all_to_all | solution.py:209
  20.8 2.2 %chip_cut.1 = (bf16[64,1792]{1,0:T(8,128)(2,1)}, bf16[64,1792]{1,0:T(8,128)(2,1)}, bf16[64,1792]{1,0:T(8,128)(2,1)}, bf16[64,1792]{1,0:T(8,128)(2,1)}) custom-call(bf16[64,7168]{1,0:T(8,128)(2,1)} %bitcast.8), custom_call_target="tpu_custom_call" | custom-call | tf_op jit(solution)/shard_map/chip_cut/pallas_call | solution.py:154
  23.0 3.5 %collective-permute-start.4 = (bf16[64,1792]{1,0:T(8,128)(2,1)}, bf16[64,1792]{1,0:T(8,128)(2,1)S(1)}, u32[]{:S(2)}, u32[]{:S(2)}) collective-permute-start(bf16[64,1792]{1,0:T(8,128)(2,1)} %get-tuple-element.24), channel_id=1, source_target_pairs={{0,2},{1,3},{2,4},{3,5},{4,6},{5,7},{6,0},{7,1},{8,10},{9,11},{10,... | collective-permute-start | bytes 688136 | tf_op jit(solution)/shard_map/ppermute | solution.py:160
  26.4 4.8 %collective-permute-start.5 = (bf16[64,1792]{1,0:T(8,128)(2,1)}, bf16[64,1792]{1,0:T(8,128)(2,1)S(1)}, u32[]{:S(2)}, u32[]{:S(2)}) collective-permute-start(bf16[64,1792]{1,0:T(8,128)(2,1)} %get-tuple-element.25), channel_id=1, source_target_pairs={{0,4},{1,5},{2,6},{3,7},{4,0},{5,1},{6,2},{7,3},{8,12},{9,13},{10,... | collective-permute-start | bytes 688136 | tf_op jit(solution)/shard_map/ppermute | solution.py:160
  31.3 2.8 %cut.1 = (bf16[128,1792]{1,0:T(8,128)(2,1)}, bf16[128,1792]{1,0:T(8,128)(2,1)}, bf16[128,1792]{1,0:T(8,128)(2,1)}, bf16[128,1792]{1,0:T(8,128)(2,1)}) custom-call(bf16[64,7168]{1,0:T(8,128)(2,1)} %bitcast.9, bf16[64,7168]{1,0:T(8,128)(2,1)} %bitcast.10), custom_call_target="tpu_custom_call" | custom-call | tf_op jit(solution)/shard_map/cut/pallas_call | solution.py:86
  34.1 1.9 %collective-permute-start.1 = (bf16[128,1792]{1,0:T(8,128)(2,1)}, bf16[128,1792]{1,0:T(8,128)(2,1)S(1)}, u32[]{:S(2)}, u32[]{:S(2)}) collective-permute-start(bf16[128,1792]{1,0:T(8,128)(2,1)} %get-tuple-element.18), channel_id=1, source_target_pairs={{0,2},{1,3},{2,4},{3,5},{4,6},{5,7},{6,0},{7,1},{8,10},{9,11},{10,... | collective-permute-start | bytes 1376264 | tf_op jit(solution)/shard_map/ppermute | solution.py:92
  36.0 4.7 %collective-permute-start.2 = (bf16[128,1792]{1,0:T(8,128)(2,1)}, bf16[128,1792]{1,0:T(8,128)(2,1)S(1)}, u32[]{:S(2)}, u32[]{:S(2)}) collective-permute-start(bf16[128,1792]{1,0:T(8,128)(2,1)} %get-tuple-element.19), channel_id=1, source_target_pairs={{0,4},{1,5},{2,6},{3,7},{4,0},{5,1},{6,2},{7,3},{8,12},{9,13},{10,... | collective-permute-start | bytes 1376264 | tf_op jit(solution)/shard_map/ppermute | solution.py:92
  40.7 0.0 copy-start.4
  40.7 0.0 copy-start.1
  40.7 2.5 %collective-permute-start.3 = (bf16[128,1792]{1,0:T(8,128)(2,1)}, bf16[128,1792]{1,0:T(8,128)(2,1)S(1)}, u32[]{:S(2)}, u32[]{:S(2)}) collective-permute-start(bf16[128,1792]{1,0:T(8,128)(2,1)} %get-tuple-element.20), channel_id=1, source_target_pairs={{0,6},{1,7},{2,0},{3,1},{4,2},{5,3},{6,4},{7,5},{8,14},{9,15},{10,... | collective-permute-start | bytes 1376264 | tf_op jit(solution)/shard_map/ppermute | solution.py:92
  43.2 6.3 %all-to-all-done = bf16[64,4,896]{2,1,0:T(4,128)(2,1)S(1)} async-done(((bf16[64,4,896]{2,1,0:T(4,128)(2,1)}), bf16[64,4,896]{2,1,0:T(4,128)(2,1)S(1)}, u32[]{:S(2)}, u32[]{:S(2)}) %all-to-all-start) | async-done | bytes 458784 | tf_op jit(solution)/shard_map/all_to_all | solution.py:209
  49.6 0.1 reshape.9.rows_ref
  49.7 0.0 collective-permute-done.4.refs_1_
  49.7 1.9 %collective-permute-start = (bf16[256,896]{1,0:T(8,128)(2,1)S(1)}, bf16[256,896]{1,0:T(8,128)(2,1)S(1)}, u32[]{:S(2)}, u32[]{:S(2)}) collective-permute-start(bf16[256,896]{1,0:T(8,128)(2,1)S(1)} %reshape.9.rows_ref), channel_id=1, source_target_pairs={{0,1},{1,0},{2,3},{3,2},{4,5},{5,4},{6,7},{7,6},{8,9},{9,8},{10,11... | collective-permute-start | bytes 1376264 | tf_op jit(solution)/shard_map/ppermute | solution.py:213
  51.6 0.0 collective-permute-done.5.refs_2_
  51.6 0.0 copy-done.4
  51.6 4.9 %collective-permute-start.6 = (bf16[64,1792]{1,0:T(8,128)(2,1)S(1)}, bf16[64,1792]{1,0:T(8,128)(2,1)S(1)}, u32[]{:S(2)}, u32[]{:S(2)}) collective-permute-start(bf16[64,1792]{1,0:T(8,128)(2,1)S(1)} %copy-done.4), channel_id=1, source_target_pairs={{0,6},{1,7},{2,0},{3,1},{4,2},{5,3},{6,4},{7,5},{8,14},{9,15},{10,... | collective-permute-start | bytes 688136 | tf_op jit(solution)/shard_map/ppermute | solution.py:160
  56.6 9.2 %collective-permute-done.6.refs_3_ = bf16[64,1792]{1,0:T(8,128)(2,1)S(1)} collective-permute-done((bf16[64,1792]{1,0:T(8,128)(2,1)S(1)}, bf16[64,1792]{1,0:T(8,128)(2,1)S(1)}, u32[]{:S(2)}, u32[]{:S(2)}) %collective-permute-start.6) | collective-permute-done | bytes 229408 | tf_op jit(solution)/shard_map/ppermute | solution.py:160
  65.8 0.0 copy-done.1
  65.8 0.0 copy-start
  65.8 0.8 core_cut.1
  66.7 1.9 %collective-permute-start.7 = (bf16[256,896]{1,0:T(8,128)(2,1)}, bf16[256,896]{1,0:T(8,128)(2,1)S(1)}, u32[]{:S(2)}, u32[]{:S(2)}) collective-permute-start(bf16[256,896]{1,0:T(8,128)(2,1)} %get-tuple-element.28), channel_id=1, source_target_pairs={{0,1},{1,0},{2,3},{3,2},{4,5},{5,4},{6,7},{7,6},{8,9},{9,8},{10,11... | collective-permute-start | bytes 1376264 | tf_op jit(solution)/shard_map/ppermute | solution.py:169
  68.6 0.0 collective-permute-done.1.refs_1_
  68.6 0.0 collective-permute-done.2.refs_2_
  68.6 0.0 collective-permute-done.3.refs_3_
  68.6 0.0 copy-done
  68.6 0.7 near.1.near_ref
  69.3 0.0 collective-permute-done.rows_ref
  69.3 1.4 %far.1 = bf16[4,128,256]{2,1,0:T(8,128)(2,1)} custom-call(bf16[256,896]{1,0:T(8,128)(2,1)S(1)} %collective-permute-done.rows_ref, f32[4,128,256]{2,1,0:T(8,128)S(1)} %near.1.near_ref, bf16[128,1792]{1,0:T(8,128)(2,1)S(1)} %copy-done, bf16[128,1792]{1,0:T(8,128)(2,1)S(1)} %collective-permute-done.1.refs_1_, ...), custom_call_target="tpu_custom_call" | custom-call | tf_op jit(solution)/shard_map/far/pallas_call | solution.py:222
  70.8 0.0 copy-start.2
  70.8 0.0 copy-start.3
  70.8 4.0 %all-to-all-start.1 = ((bf16[4,128,256]{2,1,0:T(8,128)(2,1)}), bf16[4,128,256]{2,1,0:T(8,128)(2,1)S(1)}, u32[]{:S(2)}, u32[]{:S(2)}) async-start(bf16[4,128,256]{2,1,0:T(8,128)(2,1)} %far.1), calls=%async_computation.1 | async-start | bytes 524288 | tf_op jit(solution)/shard_map/all_to_all | solution.py:229
  74.8 0.0 copy-done.2
  74.8 0.0 copy-done.3
  74.8 0.2 mix.1.mix_ref
  75.1 7.1 %all-to-all-done.1.partial_ref = bf16[4,128,256]{2,1,0:T(8,128)(2,1)S(1)} async-done(((bf16[4,128,256]{2,1,0:T(8,128)(2,1)}), bf16[4,128,256]{2,1,0:T(8,128)(2,1)S(1)}, u32[]{:S(2)}, u32[]{:S(2)}) %all-to-all-start.1) | async-done | bytes 262176 | tf_op jit(solution)/shard_map/all_to_all | solution.py:229
  82.1 0.7 hidden.1
  82.9 3.4 %all-to-all-start.2 = ((bf16[8,64,256]{2,1,0:T(8,128)(2,1)}), bf16[8,64,256]{2,1,0:T(8,128)(2,1)S(1)}, u32[]{:S(2)}, u32[]{:S(2)}) async-start(bf16[8,64,256]{2,1,0:T(8,128)(2,1)} %hidden.1), calls=%async_computation.2 | async-start | bytes 524288 | tf_op jit(solution)/shard_map/all_to_all | solution.py:239
  86.3 0.0 collective-permute-done.7.far_ref
  86.3 7.4 %all-to-all-done.2.hidden_ref = bf16[8,64,256]{2,1,0:T(8,128)(2,1)S(1)} async-done(((bf16[8,64,256]{2,1,0:T(8,128)(2,1)}), bf16[8,64,256]{2,1,0:T(8,128)(2,1)S(1)}, u32[]{:S(2)}, u32[]{:S(2)}) %all-to-all-start.2) | async-done | bytes 262176 | tf_op jit(solution)/shard_map/all_to_all | solution.py:239
  93.7 0.5 down.1
  94.2 0.1 reshape.10
  94.3 43.2 %all_to_all.20 = bf16[64,4,896]{2,1,0:T(4,128)(2,1)S(1)} all-to-all(bf16[64,4,896]{2,1,0:T(4,128)(2,1)S(1)} %reshape.10), channel_id=1, replica_groups=mesh['expert'=64,'tensor'=8] {'expert'}, dimensions={0} | all-to-all | bytes 917504 | tf_op jit(solution)/shard_map/all_to_all | solution.py:247
  137.5 0.1 reshape.11.rows_ref
  137.6 0.9 combine.1
Async XLA Ops:
  2.0 47.6 %all-to-all-start = ((bf16[64,4,896]{2,1,0:T(4,128)(2,1)}), bf16[64,4,896]{2,1,0:T(4,128)(2,1)S(1)}, u32[]{:S(2)}, u32[]{:S(2)}) async-start(bf16[64,4,896]{2,1,0:T(4,128)(2,1)} %pack.1), calls=%async_computation | async-start | bytes 917504 | tf_op jit(solution)/shard_map/all_to_all | solution.py:209
  23.0 26.7 %collective-permute-start.4 = (bf16[64,1792]{1,0:T(8,128)(2,1)}, bf16[64,1792]{1,0:T(8,128)(2,1)S(1)}, u32[]{:S(2)}, u32[]{:S(2)}) collective-permute-start(bf16[64,1792]{1,0:T(8,128)(2,1)} %get-tuple-element.24), channel_id=1, source_target_pairs={{0,2},{1,3},{2,4},{3,5},{4,6},{5,7},{6,0},{7,1},{8,10},{9,11},{10,... | collective-permute-start | bytes 688136 | tf_op jit(solution)/shard_map/ppermute | solution.py:160
  26.4 25.2 %collective-permute-start.5 = (bf16[64,1792]{1,0:T(8,128)(2,1)}, bf16[64,1792]{1,0:T(8,128)(2,1)S(1)}, u32[]{:S(2)}, u32[]{:S(2)}) collective-permute-start(bf16[64,1792]{1,0:T(8,128)(2,1)} %get-tuple-element.25), channel_id=1, source_target_pairs={{0,4},{1,5},{2,6},{3,7},{4,0},{5,1},{6,2},{7,3},{8,12},{9,13},{10,... | collective-permute-start | bytes 688136 | tf_op jit(solution)/shard_map/ppermute | solution.py:160
  34.1 34.5 %collective-permute-start.1 = (bf16[128,1792]{1,0:T(8,128)(2,1)}, bf16[128,1792]{1,0:T(8,128)(2,1)S(1)}, u32[]{:S(2)}, u32[]{:S(2)}) collective-permute-start(bf16[128,1792]{1,0:T(8,128)(2,1)} %get-tuple-element.18), channel_id=1, source_target_pairs={{0,2},{1,3},{2,4},{3,5},{4,6},{5,7},{6,0},{7,1},{8,10},{9,11},{10,... | collective-permute-start | bytes 1376264 | tf_op jit(solution)/shard_map/ppermute | solution.py:92
  36.0 32.6 %collective-permute-start.2 = (bf16[128,1792]{1,0:T(8,128)(2,1)}, bf16[128,1792]{1,0:T(8,128)(2,1)S(1)}, u32[]{:S(2)}, u32[]{:S(2)}) collective-permute-start(bf16[128,1792]{1,0:T(8,128)(2,1)} %get-tuple-element.19), channel_id=1, source_target_pairs={{0,4},{1,5},{2,6},{3,7},{4,0},{5,1},{6,2},{7,3},{8,12},{9,13},{10,... | collective-permute-start | bytes 1376264 | tf_op jit(solution)/shard_map/ppermute | solution.py:92
  40.7 10.9 %copy-start.4 = (bf16[64,1792]{1,0:T(8,128)(2,1)S(1)}, bf16[64,1792]{1,0:T(8,128)(2,1)}, u32[]{:S(2)}) copy-start(bf16[64,1792]{1,0:T(8,128)(2,1)} %get-tuple-element.26) | copy-start | bytes 688132
  40.7 25.1 %copy-start.1 = (bf16[64,1792]{1,0:T(8,128)(2,1)S(1)}, bf16[64,1792]{1,0:T(8,128)(2,1)}, u32[]{:S(2)}) copy-start(bf16[64,1792]{1,0:T(8,128)(2,1)} %get-tuple-element.23.refs_0_) | copy-start | bytes 688132
  40.7 27.9 %collective-permute-start.3 = (bf16[128,1792]{1,0:T(8,128)(2,1)}, bf16[128,1792]{1,0:T(8,128)(2,1)S(1)}, u32[]{:S(2)}, u32[]{:S(2)}) collective-permute-start(bf16[128,1792]{1,0:T(8,128)(2,1)} %get-tuple-element.20), channel_id=1, source_target_pairs={{0,6},{1,7},{2,0},{3,1},{4,2},{5,3},{6,4},{7,5},{8,14},{9,15},{10,... | collective-permute-start | bytes 1376264 | tf_op jit(solution)/shard_map/ppermute | solution.py:92
  49.7 19.7 %collective-permute-start = (bf16[256,896]{1,0:T(8,128)(2,1)S(1)}, bf16[256,896]{1,0:T(8,128)(2,1)S(1)}, u32[]{:S(2)}, u32[]{:S(2)}) collective-permute-start(bf16[256,896]{1,0:T(8,128)(2,1)S(1)} %reshape.9.rows_ref), channel_id=1, source_target_pairs={{0,1},{1,0},{2,3},{3,2},{4,5},{5,4},{6,7},{7,6},{8,9},{9,8},{10,11... | collective-permute-start | bytes 1376264 | tf_op jit(solution)/shard_map/ppermute | solution.py:213
  51.6 14.2 %collective-permute-start.6 = (bf16[64,1792]{1,0:T(8,128)(2,1)S(1)}, bf16[64,1792]{1,0:T(8,128)(2,1)S(1)}, u32[]{:S(2)}, u32[]{:S(2)}) collective-permute-start(bf16[64,1792]{1,0:T(8,128)(2,1)S(1)} %copy-done.4), channel_id=1, source_target_pairs={{0,6},{1,7},{2,0},{3,1},{4,2},{5,3},{6,4},{7,5},{8,14},{9,15},{10,... | collective-permute-start | bytes 688136 | tf_op jit(solution)/shard_map/ppermute | solution.py:160
  65.8 2.8 %copy-start = (bf16[128,1792]{1,0:T(8,128)(2,1)S(1)}, bf16[128,1792]{1,0:T(8,128)(2,1)}, u32[]{:S(2)}) copy-start(bf16[128,1792]{1,0:T(8,128)(2,1)} %get-tuple-element.17.refs_0_) | copy-start | bytes 1376260
  66.7 19.6 %collective-permute-start.7 = (bf16[256,896]{1,0:T(8,128)(2,1)}, bf16[256,896]{1,0:T(8,128)(2,1)S(1)}, u32[]{:S(2)}, u32[]{:S(2)}) collective-permute-start(bf16[256,896]{1,0:T(8,128)(2,1)} %get-tuple-element.28), channel_id=1, source_target_pairs={{0,1},{1,0},{2,3},{3,2},{4,5},{5,4},{6,7},{7,6},{8,9},{9,8},{10,11... | collective-permute-start | bytes 1376264 | tf_op jit(solution)/shard_map/ppermute | solution.py:169
  70.8 4.0 %copy-start.2 = (s32[16,8]{0,1:T(8,128)S(1)}, s32[16,8]{0,1:T(8,128)}, u32[]{:S(2)}) copy-start(s32[16,8]{0,1:T(8,128)} %param.7) | copy-start | bytes 1540
  70.8 4.0 %copy-start.3 = (f32[16,8]{0,1:T(8,128)S(1)}, f32[16,8]{0,1:T(8,128)}, u32[]{:S(2)}) copy-start(f32[16,8]{0,1:T(8,128)} %param.8) | copy-start | bytes 1540
  70.8 11.3 %all-to-all-start.1 = ((bf16[4,128,256]{2,1,0:T(8,128)(2,1)}), bf16[4,128,256]{2,1,0:T(8,128)(2,1)S(1)}, u32[]{:S(2)}, u32[]{:S(2)}) async-start(bf16[4,128,256]{2,1,0:T(8,128)(2,1)} %far.1), calls=%async_computation.1 | async-start | bytes 524288 | tf_op jit(solution)/shard_map/all_to_all | solution.py:229
  82.9 10.8 %all-to-all-start.2 = ((bf16[8,64,256]{2,1,0:T(8,128)(2,1)}), bf16[8,64,256]{2,1,0:T(8,128)(2,1)S(1)}, u32[]{:S(2)}, u32[]{:S(2)}) async-start(bf16[8,64,256]{2,1,0:T(8,128)(2,1)} %hidden.1), calls=%async_computation.2 | async-start | bytes 524288 | tf_op jit(solution)/shard_map/all_to_all | solution.py:239

commit v2 on v1

--- a/solution.py
+++ b/solution.py
@@ -69,29 +69,53 @@
     ]
 
 
-def cut_kernel(wide, gate_ref, up_ref, *outs):
+def cut_kernel(wide, gate_ref, up_ref, *refs):
+    *outs, held, taken, given = refs
     rings = len(outs)
     units = gate_ref.shape[0]
     chip = lax.axis_index("tensor") // CORES
-    for ring, out in enumerate(outs):
-        target = lax.rem(chip + ring, rings)
-        cols = pl.ds(pl.multiple_of(target * wide, 128), wide)
-        out[:units, :] = gate_ref[:, cols]
-        out[units:, :] = up_ref[:, cols]
+    order = [ring % rings for ring in range(1, rings + 1)]
+    reads, writes = {}, {}
+    for ring in order:
+        cols = pl.ds(pl.multiple_of(lax.rem(chip + ring, rings) * wide, 128), wide)
+        for part, weight in enumerate((gate_ref, up_ref)):
+            reads[ring, part] = pltpu.make_async_copy(
+                weight.at[:, cols],
+                held.at[ring, pl.ds(part * units, units), :],
+                taken.at[ring, part],
+            )
+            reads[ring, part].start()
+    for ring in order:
+        reads[ring, 0].wait()
+        reads[ring, 1].wait()
+        writes[ring] = pltpu.make_async_copy(held.at[ring], outs[ring], given.at[ring])
+        writes[ring].start()
+    for ring in order:
+        writes[ring].wait()
 
 
 def chip_blocks(gate, up, width, groups):
     wide, rings = CORES * width, groups // CORES
     shape = jax.ShapeDtypeStruct((2 * gate.shape[0], wide), BF16)
-    first, *rest = pl.pallas_call(
+    whole = pl.BlockSpec(memory_space=pl.ANY)
+    blocks = pl.pallas_call(
         lambda *refs: cut_kernel(wide, *refs),
         out_shape=[shape] * rings,
+        in_specs=[whole] * 2,
+        out_specs=[whole] * rings,
+        scratch_shapes=[
+            pltpu.VMEM((rings, *shape.shape), BF16),
+            pltpu.SemaphoreType.DMA((rings, 2)),
+            pltpu.SemaphoreType.DMA((rings,)),
+        ],
         name="cut",
     )(gate, up)
-    return [first] + [
-        lax.ppermute(block, "tensor", shift_pairs(groups, ring + 1, 0))
-        for ring, block in enumerate(rest)
-    ]
+    blocks = list(blocks)
+    for ring in range(1, rings):
+        blocks[ring] = lax.ppermute(
+            blocks[ring], "tensor", shift_pairs(groups, ring, 0)
+        )
+    return blocks
 
 
 def half_product(block_ref, rows_ref, half):
@@ -129,56 +153,82 @@
         out_ref[g] = hidden
 
 
-def chip_cut_kernel(wide, weight_ref, *outs):
-    rings = len(outs)
+def split_kernel(weight_ref, keep_ref, send_ref, held, taken, given):
+    rings, _, width = keep_ref.shape
+    core = lax.rem(lax.axis_index("tensor"), CORES)
+    reads = []
+    for side in (1, 0):
+        lane = lax.rem(core + side, CORES)
+        for ring in range(rings):
+            cols = pl.ds(pl.multiple_of((ring * CORES + lane) * width, 128), width)
+            reads.append(
+                pltpu.make_async_copy(
+                    weight_ref.at[:, cols], held.at[side, ring], taken.at[side, ring]
+                )
+            )
+            reads[-1].start()
+    writes = []
+    for place, (side, out) in enumerate(((1, send_ref), (0, keep_ref))):
+        for read in reads[place * rings : (place + 1) * rings]:
+            read.wait()
+        writes.append(pltpu.make_async_copy(held.at[side], out, given.at[side]))
+        writes[-1].start()
+    for write in writes:
+        write.wait()
+
+
+def join_kernel(keep_ref, took_ref, *outs):
+    rings, units, _ = keep_ref.shape
     chip = lax.axis_index("tensor") // CORES
     for ring, out in enumerate(outs):
         target = lax.rem(chip + ring, rings)
-        out[...] = weight_ref[:, pl.ds(pl.multiple_of(target * wide, 128), wide)]
-
-
-def core_cut_kernel(*refs):
-    *blocks, near_ref, far_ref = refs
-    core = lax.rem(lax.axis_index("tensor"), CORES)
-    units = blocks[0].shape[0]
-    width = near_ref.shape[1]
-    for ring, block in enumerate(blocks):
-        rows = pl.ds(ring * units, units)
-        near_ref[rows, :] = block[:, pl.ds(pl.multiple_of(core * width, 128), width)]
-        far_ref[rows, :] = block[:, pl.ds(pl.multiple_of((1 - core) * width, 128), width)]
-
-
-def down_columns(weight, width, groups):
+        out[:units, :] = keep_ref[target]
+        out[units:, :] = took_ref[target]
+
+
+def down_blocks(weight, width, groups):
     units = weight.shape[0]
-    rings, wide = groups // CORES, CORES * width
-    first, *rest = pl.pallas_call(
-        lambda *refs: chip_cut_kernel(wide, *refs),
-        out_shape=[jax.ShapeDtypeStruct((units, wide), BF16)] * rings,
-        name="chip_cut",
+    rings = groups // CORES
+    whole = pl.BlockSpec(memory_space=pl.ANY)
+    keep, send = pl.pallas_call(
+        split_kernel,
+        out_shape=[jax.ShapeDtypeStruct((rings, units, width), BF16)] * 2,
+        in_specs=[whole],
+        out_specs=[whole] * 2,
+        scratch_shapes=[
+            pltpu.VMEM((CORES, rings, units, width), BF16),
+            pltpu.SemaphoreType.DMA((CORES, rings)),
+            pltpu.SemaphoreType.DMA((CORES,)),
+        ],
+        name="split",
     )(weight)
+    took = lax.ppermute(send, "tensor", shift_pairs(groups, 0, 1))
+    blocks = pl.pallas_call(
+        join_kernel,
+        out_shape=[jax.ShapeDtypeStruct((CORES * units, width), BF16)] * rings,
+        name="join",
+    )(keep, took)
+    blocks = list(blocks)
     for ring in range(1, rings):
-        rest[ring - 1] = lax.ppermute(
-            rest[ring - 1], "tensor", shift_pairs(groups, ring, 0)
+        blocks[ring] = lax.ppermute(
+            blocks[ring], "tensor", shift_pairs(groups, ring, 0)
         )
-    near, far = pl.pallas_call(
-        core_cut_kernel,
-        out_shape=[jax.ShapeDtypeStruct((rings * units, width), BF16)] * 2,
-        compiler_params=pltpu.CompilerParams(vmem_limit_bytes=VMEM_BYTES),
-        name="core_cut",
-    )(first, *rest)
-    return near, lax.ppermute(far, "tensor", shift_pairs(groups, 0, 1))
-
-
-def down_kernel(hidden_ref, near_ref, far_ref, out_ref, held):
+    return blocks
+
+
+def down_kernel(hidden_ref, *refs):
+    *blocks, out_ref, held = refs
     groups, units, _ = hidden_ref.shape
     me = lax.axis_index("tensor")
-    for core in range(CORES):
-        for ring in range(groups // CORES):
+    total = None
+    for ring, block in enumerate(blocks):
+        for core in range(CORES):
             source = moved_by(me, groups, ring, core, sign=-1)
-            held[core, pl.ds(ring * units, units), :] = hidden_ref[source]
-    dims = (((0,), (0,)), ((), ()))
-    total = lax.dot_general(held[0], near_ref[...], dims, preferred_element_type=F32)
-    total = total + lax.dot_general(held[1], far_ref[...], dims, preferred_element_type=F32)
+            held[ring, pl.ds(core * units, units), :] = hidden_ref[source]
+        term = lax.dot_general(
+            held[ring], block[...], (((0,), (0,)), ((), ())), preferred_element_type=F32
+        )
+        total = term if total is None else total + term
     out_ref[...] = total.astype(BF16)
 
 
@@ -208,7 +258,7 @@
     blocks = chip_blocks(gate_weight[0], up_weight[0], width, groups)
     arrived = lax.all_to_all(packed, "expert", 0, 0, tiled=True)
     arrived = arrived.reshape(arrived_count, width)
-    down_near, down_far = down_columns(down_weight[0], width, groups)
+    down = down_blocks(down_weight[0], width, groups)
 
     partner = lax.ppermute(arrived, "tensor", shift_pairs(groups, 0, 1))
     rings = groups // CORES
@@ -240,10 +290,10 @@
     half_out = pl.pallas_call(
         down_kernel,
         out_shape=jax.ShapeDtypeStruct((arrived_count, width), BF16),
-        scratch_shapes=[pltpu.VMEM((2, groups // 2 * units, arrived_count), BF16)],
+        scratch_shapes=[pltpu.VMEM((rings, CORES * units, arrived_count), BF16)],
         compiler_params=pltpu.CompilerParams(vmem_limit_bytes=VMEM_BYTES),
         name="down",
-    )(hidden, down_near, down_far)
+    )(hidden, *down)
     returned = lax.all_to_all(
         half_out.reshape(devices_wide, capacity, width), "expert", 0, 0, tiled=True
     ).reshape(arrived_count, width)

time: 139 us -> 130 us (0.935)
  waiting for transfers between devices: 30.1 us -> 22.2 us
  blocking collectives: 43.2 us -> 37.6 us
  starting transfers between devices: 52.4 us -> 54.7 us
    all_to_all x1, waiting for transfers between devices: 6.33 us -> 14.7 us  [body(): arrived = lax.all_to_all(packed, 'expert', 0, 0, tiled=True)]
    ppermute x7, waiting for transfers between devices: 9.26 us -> 1.75 us  [the longest x3 1.74 us: down_blocks(): lax.ppermute(blocks[ring], 'tensor', shift_pairs(groups, ring, 0))]
    all_to_all x1, waiting for transfers between devices: 7.05 us -> 0.01 us  [body(): lax.all_to_all(partial, 'tensor', 0, 0, axis_index_groups=same_core, tile...]
    all_to_all x1, blocking collectives: 43.2 us -> 37.6 us  [body(): lax.all_to_all(half_out.reshape(devices_wide, capacity, width), 'expert',...]
    all_to_all x1, waiting for transfers between devices: 7.42 us -> 5.69 us  [body(): hidden = lax.all_to_all(hidden, 'tensor', 0, 0, tiled=True)]
    ppermute x7, starting transfers between devices: 24.2 us -> 25.8 us  [the longest x3 11.9 us: down_blocks(): lax.ppermute(blocks[ring], 'tensor', shift_pairs(groups, ring, 0))]
  transfers between devices with their start and end apart: 11 -> 11, of which waited for: 4 -> 4; matrix products, arithmetic and copies ran while one was open for 0% -> 0% of each run, Pallas kernels for 6% -> 8%
where the time goes in v2:
time: 130 us; the launch traced here: 129 us
  starting transfers between devices  54.7 us (42%)
  blocking collectives  37.6 us (29%)
  waiting for transfers between devices  22.2 us (17%)
  Pallas kernels  13.5 us (10%)
    all_to_all x1, blocking collectives, body(): lax.all_to_all(half_out.reshape(devices_wide, capacity, width), 'expert',...  37.6 us
    all_to_all x1, starting transfers between devices, body(): arrived = lax.all_to_all(packed, 'expert', 0, 0, tiled=True)  18.8 us
    all_to_all x1, waiting for transfers between devices, body(): arrived = lax.all_to_all(packed, 'expert', 0, 0, tiled=True)  14.7 us
    ppermute x3, starting transfers between devices, down_blocks(): lax.ppermute(blocks[ring], 'tensor', shift_pairs(groups, ring, 0))  11.9 us
    ppermute x3, starting transfers between devices, chip_blocks(): lax.ppermute(blocks[ring], 'tensor', shift_pairs(groups, ring, 0))  11.5 us
    all_to_all x1, waiting for transfers between devices, body(): hidden = lax.all_to_all(hidden, 'tensor', 0, 0, tiled=True)  5.69 us
    all_to_all x1, starting transfers between devices, body(): lax.all_to_all(partial, 'tensor', 0, 0, axis_index_groups=same_core, tile...  4.6 us
    all_to_all x1, starting transfers between devices, body(): hidden = lax.all_to_all(hidden, 'tensor', 0, 0, tiled=True)  3.54 us
  transfers between devices with their start and end apart: 11, of which 4 were waited for; matrix products, arithmetic and copies ran while one was open for 0% of the time, Pallas kernels for 8%

profile of v2, /device:TPU:6, one launch (start us, length us, event | category | flops | bytes accessed | tf_op | source)
XLA Modules:
  0.0 129.2 jit_solution(5958901720967439408)
XLA Ops:
  0.0 2.0 %pack.1 = bf16[64,4,896]{2,1,0:T(4,128)(2,1)} custom-call(s32[8,16]{1,0:T(8,128)} %bitcast.5, bf16[16,896]{1,0:T(8,128)(2,1)} %refs_1_.1), custom_call_target="tpu_custom_call" | custom-call | tf_op jit(solution)/shard_map/pack/pallas_call | solution.py:246
  2.0 18.8 %all-to-all-start = ((bf16[64,4,896]{2,1,0:T(4,128)(2,1)}), bf16[64,4,896]{2,1,0:T(4,128)(2,1)S(1)}, u32[]{:S(2)}, u32[]{:S(2)}) async-start(bf16[64,4,896]{2,1,0:T(4,128)(2,1)} %pack.1), calls=%async_computation | async-start | bytes 917504 | tf_op jit(solution)/shard_map/all_to_all | solution.py:259
  20.8 2.5 %cut.1 = (bf16[128,1792]{1,0:T(8,128)(2,1)}, bf16[128,1792]{1,0:T(8,128)(2,1)}, bf16[128,1792]{1,0:T(8,128)(2,1)}, bf16[128,1792]{1,0:T(8,128)(2,1)}) custom-call(bf16[64,7168]{1,0:T(8,128)(2,1)} %bitcast.8, bf16[64,7168]{1,0:T(8,128)(2,1)} %bitcast.9), custom_call_target="tpu_custom_call" | custom-call | tf_op jit(solution)/shard_map/cut/pallas_call | solution.py:101
  23.3 3.5 %collective-permute-start.1 = (bf16[128,1792]{1,0:T(8,128)(2,1)}, bf16[128,1792]{1,0:T(8,128)(2,1)S(1)}, u32[]{:S(2)}, u32[]{:S(2)}) collective-permute-start(bf16[128,1792]{1,0:T(8,128)(2,1)} %get-tuple-element.18), channel_id=1, source_target_pairs={{0,2},{1,3},{2,4},{3,5},{4,6},{5,7},{6,0},{7,1},{8,10},{9,11},{10,... | collective-permute-start | bytes 1376264 | tf_op jit(solution)/shard_map/ppermute | solution.py:115
  26.7 4.8 %collective-permute-start.2 = (bf16[128,1792]{1,0:T(8,128)(2,1)}, bf16[128,1792]{1,0:T(8,128)(2,1)S(1)}, u32[]{:S(2)}, u32[]{:S(2)}) collective-permute-start(bf16[128,1792]{1,0:T(8,128)(2,1)} %get-tuple-element.19), channel_id=1, source_target_pairs={{0,4},{1,5},{2,6},{3,7},{4,0},{5,1},{6,2},{7,3},{8,12},{9,13},{10,... | collective-permute-start | bytes 1376264 | tf_op jit(solution)/shard_map/ppermute | solution.py:115
  31.6 3.3 %collective-permute-start.3 = (bf16[128,1792]{1,0:T(8,128)(2,1)}, bf16[128,1792]{1,0:T(8,128)(2,1)S(1)}, u32[]{:S(2)}, u32[]{:S(2)}) collective-permute-start(bf16[128,1792]{1,0:T(8,128)(2,1)} %get-tuple-element.20), channel_id=1, source_target_pairs={{0,6},{1,7},{2,0},{3,1},{4,2},{5,3},{6,4},{7,5},{8,14},{9,15},{10,... | collective-permute-start | bytes 1376264 | tf_op jit(solution)/shard_map/ppermute | solution.py:115
  34.8 14.7 %all-to-all-done = bf16[64,4,896]{2,1,0:T(4,128)(2,1)S(1)} async-done(((bf16[64,4,896]{2,1,0:T(4,128)(2,1)}), bf16[64,4,896]{2,1,0:T(4,128)(2,1)S(1)}, u32[]{:S(2)}, u32[]{:S(2)}) %all-to-all-start) | async-done | bytes 458784 | tf_op jit(solution)/shard_map/all_to_all | solution.py:259
  49.6 0.1 reshape.9.rows_ref
  49.7 1.9 %collective-permute-start = (bf16[256,896]{1,0:T(8,128)(2,1)S(1)}, bf16[256,896]{1,0:T(8,128)(2,1)S(1)}, u32[]{:S(2)}, u32[]{:S(2)}) collective-permute-start(bf16[256,896]{1,0:T(8,128)(2,1)S(1)} %reshape.9.rows_ref), channel_id=1, source_target_pairs={{0,1},{1,0},{2,3},{3,2},{4,5},{5,4},{6,7},{7,6},{8,9},{9,8},{10,11... | collective-permute-start | bytes 1376264 | tf_op jit(solution)/shard_map/ppermute | solution.py:263
  51.6 0.0 copy-start
  51.6 2.2 %split.1 = (bf16[4,64,896]{2,1,0:T(8,128)(2,1)}, bf16[4,64,896]{2,1,0:T(8,128)(2,1)}) custom-call(bf16[64,7168]{1,0:T(8,128)(2,1)} %bitcast.10), custom_call_target="tpu_custom_call" | custom-call | tf_op jit(solution)/shard_map/split/pallas_call | solution.py:193
  53.8 2.4 %collective-permute-start.4 = (bf16[4,64,896]{2,1,0:T(8,128)(2,1)}, bf16[4,64,896]{2,1,0:T(8,128)(2,1)S(1)}, u32[]{:S(2)}, u32[]{:S(2)}) collective-permute-start(bf16[4,64,896]{2,1,0:T(8,128)(2,1)} %get-tuple-element.24), channel_id=1, source_target_pairs={{0,1},{1,0},{2,3},{3,2},{4,5},{5,4},{6,7},{7,6},{8,9},{9,8},{10,11... | collective-permute-start | bytes 1376264 | tf_op jit(solution)/shard_map/ppermute | solution.py:205
  56.2 0.0 collective-permute-done.1.refs_1_
  56.2 0.0 collective-permute-done.2.refs_2_
  56.2 0.0 collective-permute-done.3.refs_3_
  56.2 0.0 copy-done
  56.2 0.7 near.1.near_ref
  57.0 0.0 collective-permute-done.rows_ref
  57.0 1.5 %far.1 = bf16[4,128,256]{2,1,0:T(8,128)(2,1)} custom-call(bf16[256,896]{1,0:T(8,128)(2,1)S(1)} %collective-permute-done.rows_ref, f32[4,128,256]{2,1,0:T(8,128)S(1)} %near.1.near_ref, bf16[128,1792]{1,0:T(8,128)(2,1)S(1)} %copy-done, bf16[128,1792]{1,0:T(8,128)(2,1)S(1)} %collective-permute-done.1.refs_1_, ...), custom_call_target="tpu_custom_call" | custom-call | tf_op jit(solution)/shard_map/far/pallas_call | solution.py:272
  58.4 0.0 copy-start.2
  58.4 0.0 copy-start.3
  58.4 4.6 %all-to-all-start.1 = ((bf16[4,128,256]{2,1,0:T(8,128)(2,1)}), bf16[4,128,256]{2,1,0:T(8,128)(2,1)S(1)}, u32[]{:S(2)}, u32[]{:S(2)}) async-start(bf16[4,128,256]{2,1,0:T(8,128)(2,1)} %far.1), calls=%async_computation.1 | async-start | bytes 524288 | tf_op jit(solution)/shard_map/all_to_all | solution.py:279
  63.0 0.0 copy-done.2
  63.0 0.0 copy-done.3
  63.0 0.2 mix.1.mix_ref
  63.3 0.0 collective-permute-done.4.took_ref
  63.3 0.0 copy-start.4
  63.3 0.8 copy-done.4
  64.1 2.2 %join.1 = (bf16[128,896]{1,0:T(8,128)(2,1)}, bf16[128,896]{1,0:T(8,128)(2,1)}, bf16[128,896]{1,0:T(8,128)(2,1)}, bf16[128,896]{1,0:T(8,128)(2,1)}) custom-call(bf16[4,64,896]{2,1,0:T(8,128)(2,1)} %get-tuple-element.23.keep_ref, bf16[4,64,896]{2,1,0:T(8,128)(2,1)} %copy-done.4), custom_call_target="tpu_custom_call" | custom-call | tf_op jit(solution)/shard_map/join/pallas_call | solution.py:206
  66.2 3.9 %collective-permute-start.5 = (bf16[128,896]{1,0:T(8,128)(2,1)}, bf16[128,896]{1,0:T(8,128)(2,1)S(1)}, u32[]{:S(2)}, u32[]{:S(2)}) collective-permute-start(bf16[128,896]{1,0:T(8,128)(2,1)} %get-tuple-element.26), channel_id=1, source_target_pairs={{0,2},{1,3},{2,4},{3,5},{4,6},{5,7},{6,0},{7,1},{8,10},{9,11},{10,... | collective-permute-start | bytes 688136 | tf_op jit(solution)/shard_map/ppermute | solution.py:213
  70.1 4.6 %collective-permute-start.6 = (bf16[128,896]{1,0:T(8,128)(2,1)}, bf16[128,896]{1,0:T(8,128)(2,1)S(1)}, u32[]{:S(2)}, u32[]{:S(2)}) collective-permute-start(bf16[128,896]{1,0:T(8,128)(2,1)} %get-tuple-element.27), channel_id=1, source_target_pairs={{0,4},{1,5},{2,6},{3,7},{4,0},{5,1},{6,2},{7,3},{8,12},{9,13},{10,... | collective-permute-start | bytes 688136 | tf_op jit(solution)/shard_map/ppermute | solution.py:213
  74.7 3.4 %collective-permute-start.7 = (bf16[128,896]{1,0:T(8,128)(2,1)}, bf16[128,896]{1,0:T(8,128)(2,1)S(1)}, u32[]{:S(2)}, u32[]{:S(2)}) collective-permute-start(bf16[128,896]{1,0:T(8,128)(2,1)} %get-tuple-element.28), channel_id=1, source_target_pairs={{0,6},{1,7},{2,0},{3,1},{4,2},{5,3},{6,4},{7,5},{8,14},{9,15},{10,... | collective-permute-start | bytes 688136 | tf_op jit(solution)/shard_map/ppermute | solution.py:213
  78.1 0.0 all-to-all-done.1.partial_ref
  78.1 0.7 hidden.1
  78.9 0.0 copy-start.1
  78.9 3.5 %all-to-all-start.2 = ((bf16[8,64,256]{2,1,0:T(8,128)(2,1)}), bf16[8,64,256]{2,1,0:T(8,128)(2,1)S(1)}, u32[]{:S(2)}, u32[]{:S(2)}) async-start(bf16[8,64,256]{2,1,0:T(8,128)(2,1)} %hidden.1), calls=%async_computation.2 | async-start | bytes 524288 | tf_op jit(solution)/shard_map/all_to_all | solution.py:289
  82.4 0.0 collective-permute-done.5.refs_1_
  82.4 0.4 collective-permute-done.6.refs_2_
  82.8 1.3 %collective-permute-done.7.refs_3_ = bf16[128,896]{1,0:T(8,128)(2,1)S(1)} collective-permute-done((bf16[128,896]{1,0:T(8,128)(2,1)}, bf16[128,896]{1,0:T(8,128)(2,1)S(1)}, u32[]{:S(2)}, u32[]{:S(2)}) %collective-permute-start.7) | collective-permute-done | bytes 229408 | tf_op jit(solution)/shard_map/ppermute | solution.py:213
  84.2 5.7 %all-to-all-done.2.hidden_ref = bf16[8,64,256]{2,1,0:T(8,128)(2,1)S(1)} async-done(((bf16[8,64,256]{2,1,0:T(8,128)(2,1)}), bf16[8,64,256]{2,1,0:T(8,128)(2,1)S(1)}, u32[]{:S(2)}, u32[]{:S(2)}) %all-to-all-start.2) | async-done | bytes 262176 | tf_op jit(solution)/shard_map/all_to_all | solution.py:289
  89.9 0.0 copy-done.1
  89.9 0.7 down.1
  90.5 0.1 reshape.10
  90.6 37.6 %all_to_all.20 = bf16[64,4,896]{2,1,0:T(4,128)(2,1)S(1)} all-to-all(bf16[64,4,896]{2,1,0:T(4,128)(2,1)S(1)} %reshape.10), channel_id=1, replica_groups=mesh['expert'=64,'tensor'=8] {'expert'}, dimensions={0} | all-to-all | bytes 917504 | tf_op jit(solution)/shard_map/all_to_all | solution.py:297
  128.2 0.1 reshape.11.rows_ref
  128.3 0.9 combine.1
Async XLA Ops:
  2.0 47.6 %all-to-all-start = ((bf16[64,4,896]{2,1,0:T(4,128)(2,1)}), bf16[64,4,896]{2,1,0:T(4,128)(2,1)S(1)}, u32[]{:S(2)}, u32[]{:S(2)}) async-start(bf16[64,4,896]{2,1,0:T(4,128)(2,1)} %pack.1), calls=%async_computation | async-start | bytes 917504 | tf_op jit(solution)/shard_map/all_to_all | solution.py:259
  23.3 32.9 %collective-permute-start.1 = (bf16[128,1792]{1,0:T(8,128)(2,1)}, bf16[128,1792]{1,0:T(8,128)(2,1)S(1)}, u32[]{:S(2)}, u32[]{:S(2)}) collective-permute-start(bf16[128,1792]{1,0:T(8,128)(2,1)} %get-tuple-element.18), channel_id=1, source_target_pairs={{0,2},{1,3},{2,4},{3,5},{4,6},{5,7},{6,0},{7,1},{8,10},{9,11},{10,... | collective-permute-start | bytes 1376264 | tf_op jit(solution)/shard_map/ppermute | solution.py:115
  26.7 29.5 %collective-permute-start.2 = (bf16[128,1792]{1,0:T(8,128)(2,1)}, bf16[128,1792]{1,0:T(8,128)(2,1)S(1)}, u32[]{:S(2)}, u32[]{:S(2)}) collective-permute-start(bf16[128,1792]{1,0:T(8,128)(2,1)} %get-tuple-element.19), channel_id=1, source_target_pairs={{0,4},{1,5},{2,6},{3,7},{4,0},{5,1},{6,2},{7,3},{8,12},{9,13},{10,... | collective-permute-start | bytes 1376264 | tf_op jit(solution)/shard_map/ppermute | solution.py:115
  31.6 24.7 %collective-permute-start.3 = (bf16[128,1792]{1,0:T(8,128)(2,1)}, bf16[128,1792]{1,0:T(8,128)(2,1)S(1)}, u32[]{:S(2)}, u32[]{:S(2)}) collective-permute-start(bf16[128,1792]{1,0:T(8,128)(2,1)} %get-tuple-element.20), channel_id=1, source_target_pairs={{0,6},{1,7},{2,0},{3,1},{4,2},{5,3},{6,4},{7,5},{8,14},{9,15},{10,... | collective-permute-start | bytes 1376264 | tf_op jit(solution)/shard_map/ppermute | solution.py:115
  49.7 7.3 %collective-permute-start = (bf16[256,896]{1,0:T(8,128)(2,1)S(1)}, bf16[256,896]{1,0:T(8,128)(2,1)S(1)}, u32[]{:S(2)}, u32[]{:S(2)}) collective-permute-start(bf16[256,896]{1,0:T(8,128)(2,1)S(1)} %reshape.9.rows_ref), channel_id=1, source_target_pairs={{0,1},{1,0},{2,3},{3,2},{4,5},{5,4},{6,7},{7,6},{8,9},{9,8},{10,11... | collective-permute-start | bytes 1376264 | tf_op jit(solution)/shard_map/ppermute | solution.py:263
  51.6 4.6 %copy-start = (bf16[128,1792]{1,0:T(8,128)(2,1)S(1)}, bf16[128,1792]{1,0:T(8,128)(2,1)}, u32[]{:S(2)}) copy-start(bf16[128,1792]{1,0:T(8,128)(2,1)} %get-tuple-element.17.refs_0_) | copy-start | bytes 1376260
  53.8 9.5 %collective-permute-start.4 = (bf16[4,64,896]{2,1,0:T(8,128)(2,1)}, bf16[4,64,896]{2,1,0:T(8,128)(2,1)S(1)}, u32[]{:S(2)}, u32[]{:S(2)}) collective-permute-start(bf16[4,64,896]{2,1,0:T(8,128)(2,1)} %get-tuple-element.24), channel_id=1, source_target_pairs={{0,1},{1,0},{2,3},{3,2},{4,5},{5,4},{6,7},{7,6},{8,9},{9,8},{10,11... | collective-permute-start | bytes 1376264 | tf_op jit(solution)/shard_map/ppermute | solution.py:205
  58.4 4.6 %copy-start.2 = (s32[16,8]{0,1:T(8,128)S(1)}, s32[16,8]{0,1:T(8,128)}, u32[]{:S(2)}) copy-start(s32[16,8]{0,1:T(8,128)} %param.7) | copy-start | bytes 1540
  58.4 4.6 %copy-start.3 = (f32[16,8]{0,1:T(8,128)S(1)}, f32[16,8]{0,1:T(8,128)}, u32[]{:S(2)}) copy-start(f32[16,8]{0,1:T(8,128)} %param.8) | copy-start | bytes 1540
  58.4 19.7 %all-to-all-start.1 = ((bf16[4,128,256]{2,1,0:T(8,128)(2,1)}), bf16[4,128,256]{2,1,0:T(8,128)(2,1)S(1)}, u32[]{:S(2)}, u32[]{:S(2)}) async-start(bf16[4,128,256]{2,1,0:T(8,128)(2,1)} %far.1), calls=%async_computation.1 | async-start | bytes 524288 | tf_op jit(solution)/shard_map/all_to_all | solution.py:279
  63.3 0.8 copy-start.4
  66.2 16.2 %collective-permute-start.5 = (bf16[128,896]{1,0:T(8,128)(2,1)}, bf16[128,896]{1,0:T(8,128)(2,1)S(1)}, u32[]{:S(2)}, u32[]{:S(2)}) collective-permute-start(bf16[128,896]{1,0:T(8,128)(2,1)} %get-tuple-element.26), channel_id=1, source_target_pairs={{0,2},{1,3},{2,4},{3,5},{4,6},{5,7},{6,0},{7,1},{8,10},{9,11},{10,... | collective-permute-start | bytes 688136 | tf_op jit(solution)/shard_map/ppermute | solution.py:213
  70.1 12.7 %collective-permute-start.6 = (bf16[128,896]{1,0:T(8,128)(2,1)}, bf16[128,896]{1,0:T(8,128)(2,1)S(1)}, u32[]{:S(2)}, u32[]{:S(2)}) collective-permute-start(bf16[128,896]{1,0:T(8,128)(2,1)} %get-tuple-element.27), channel_id=1, source_target_pairs={{0,4},{1,5},{2,6},{3,7},{4,0},{5,1},{6,2},{7,3},{8,12},{9,13},{10,... | collective-permute-start | bytes 688136 | tf_op jit(solution)/shard_map/ppermute | solution.py:213
  74.7 9.4 %collective-permute-start.7 = (bf16[128,896]{1,0:T(8,128)(2,1)}, bf16[128,896]{1,0:T(8,128)(2,1)S(1)}, u32[]{:S(2)}, u32[]{:S(2)}) collective-permute-start(bf16[128,896]{1,0:T(8,128)(2,1)} %get-tuple-element.28), channel_id=1, source_target_pairs={{0,6},{1,7},{2,0},{3,1},{4,2},{5,3},{6,4},{7,5},{8,14},{9,15},{10,... | collective-permute-start | bytes 688136 | tf_op jit(solution)/shard_map/ppermute | solution.py:213
  78.9 11.0 %copy-start.1 = (bf16[128,896]{1,0:T(8,128)(2,1)S(1)}, bf16[128,896]{1,0:T(8,128)(2,1)}, u32[]{:S(2)}) copy-start(bf16[128,896]{1,0:T(8,128)(2,1)} %get-tuple-element.25.refs_0_) | copy-start | bytes 688132
  78.9 11.0 %all-to-all-start.2 = ((bf16[8,64,256]{2,1,0:T(8,128)(2,1)}), bf16[8,64,256]{2,1,0:T(8,128)(2,1)S(1)}, u32[]{:S(2)}, u32[]{:S(2)}) async-start(bf16[8,64,256]{2,1,0:T(8,128)(2,1)} %hidden.1), calls=%async_computation.2 | async-start | bytes 524288 | tf_op jit(solution)/shard_map/all_to_all | solution.py:289

commit v3 on v1

--- a/solution.py
+++ b/solution.py
@@ -24,11 +24,18 @@
     return jnp.where((hit > 0.5) & (earlier == rank), 1.0, 0.0), expert
 
 
-def pack_kernel(copies, ids_ref, tok_ref, out_ref):
+def pack_kernel(copies, ring, ids_ref, tok_ref, gate_ref, up_ref, out_ref, block_ref, *refs):
+    held, taken, given = refs
+    reads = cut_reads(ring, (gate_ref, up_ref), held, taken)
     peers, capacity, width = out_ref.shape
     select, _ = slot_onehot(ids_ref[...], peers * capacity, capacity, copies)
     packed = jnp.dot(select.astype(BF16), tok_ref[...], preferred_element_type=F32)
+    for read in reads:
+        read.wait()
+    write = pltpu.make_async_copy(held, block_ref, given)
+    write.start()
     out_ref[...] = packed.reshape(peers, capacity, width).astype(BF16)
+    write.wait()
 
 
 def mix_kernel(capacity, copies, ids_ref, route_ref, mix_ref):
@@ -69,29 +76,56 @@
     ]
 
 
-def cut_kernel(wide, gate_ref, up_ref, *outs):
-    rings = len(outs)
-    units = gate_ref.shape[0]
+def cut_reads(ring, weights, held, taken):
+    wide = held.shape[1]
+    units, full = weights[0].shape
+    rings = full // wide
     chip = lax.axis_index("tensor") // CORES
-    for ring, out in enumerate(outs):
-        target = lax.rem(chip + ring, rings)
-        cols = pl.ds(pl.multiple_of(target * wide, 128), wide)
-        out[:units, :] = gate_ref[:, cols]
-        out[units:, :] = up_ref[:, cols]
-
-
-def chip_blocks(gate, up, width, groups):
-    wide, rings = CORES * width, groups // CORES
-    shape = jax.ShapeDtypeStruct((2 * gate.shape[0], wide), BF16)
-    first, *rest = pl.pallas_call(
-        lambda *refs: cut_kernel(wide, *refs),
-        out_shape=[shape] * rings,
+    cols = pl.ds(pl.multiple_of(lax.rem(chip + ring, rings) * wide, 128), wide)
+    reads = []
+    for part, weight in enumerate(weights):
+        reads.append(
+            pltpu.make_async_copy(
+                weight.at[:, cols], held.at[pl.ds(part * units, units), :], taken.at[part]
+            )
+        )
+        reads[-1].start()
+    return reads
+
+
+def cut_kernel(rings, parts, *refs):
+    weights, refs = refs[:parts], refs[parts:]
+    *outs, held, taken, given = refs
+    reads = [
+        cut_reads(ring, weights, held.at[place], taken.at[place])
+        for place, ring in enumerate(rings)
+    ]
+    writes = []
+    for place, out in enumerate(outs):
+        for read in reads[place]:
+            read.wait()
+        writes.append(pltpu.make_async_copy(held.at[place], out, given.at[place]))
+        writes[-1].start()
+    for write in writes:
+        write.wait()
+
+
+def cut(rings, weights, wide):
+    parts, units = len(weights), weights[0].shape[0]
+    shape = jax.ShapeDtypeStruct((parts * units, wide), BF16)
+    whole = pl.BlockSpec(memory_space=pl.ANY)
+    return pl.pallas_call(
+        lambda *refs: cut_kernel(rings, parts, *refs),
+        out_shape=[shape] * len(rings),
+        in_specs=[whole] * parts,
+        out_specs=[whole] * len(rings),
+        scratch_shapes=[
+            pltpu.VMEM((len(rings), *shape.shape), BF16),
+            pltpu.SemaphoreType.DMA((len(rings), parts)),
+            pltpu.SemaphoreType.DMA((len(rings),)),
+        ],
         name="cut",
-    )(gate, up)
-    return [first] + [
-        lax.ppermute(block, "tensor", shift_pairs(groups, ring + 1, 0))
-        for ring, block in enumerate(rest)
-    ]
+    )(*weights)
 
 
 def half_product(block_ref, rows_ref, half):
@@ -129,14 +163,6 @@
         out_ref[g] = hidden
 
 
-def chip_cut_kernel(wide, weight_ref, *outs):
-    rings = len(outs)
-    chip = lax.axis_index("tensor") // CORES
-    for ring, out in enumerate(outs):
-        target = lax.rem(chip + ring, rings)
-        out[...] = weight_ref[:, pl.ds(pl.multiple_of(target * wide, 128), wide)]
-
-
 def core_cut_kernel(*refs):
     *blocks, near_ref, far_ref = refs
     core = lax.rem(lax.axis_index("tensor"), CORES)
@@ -150,22 +176,20 @@
 
 def down_columns(weight, width, groups):
     units = weight.shape[0]
-    rings, wide = groups // CORES, CORES * width
-    first, *rest = pl.pallas_call(
-        lambda *refs: chip_cut_kernel(wide, *refs),
-        out_shape=[jax.ShapeDtypeStruct((units, wide), BF16)] * rings,
-        name="chip_cut",
-    )(weight)
+    rings = groups // CORES
+    order = (1, 2, 3, 0)
+    cuts = cut(order, (weight,), CORES * width)
+    blocks = dict(zip(order, cuts))
     for ring in range(1, rings):
-        rest[ring - 1] = lax.ppermute(
-            rest[ring - 1], "tensor", shift_pairs(groups, ring, 0)
+        blocks[ring] = lax.ppermute(
+            blocks[ring], "tensor", shift_pairs(groups, ring, 0)
         )
     near, far = pl.pallas_call(
         core_cut_kernel,
         out_shape=[jax.ShapeDtypeStruct((rings * units, width), BF16)] * 2,
         compiler_params=pltpu.CompilerParams(vmem_limit_bytes=VMEM_BYTES),
         name="core_cut",
-    )(first, *rest)
+    )(*[blocks[ring] for ring in range(rings)])
     return near, lax.ppermute(far, "tensor", shift_pairs(groups, 0, 1))
 
 
@@ -193,11 +217,22 @@
     arrived_count = devices_wide * capacity
 
     ids = expert_ids.T
-    packed = pl.pallas_call(
-        lambda *refs: pack_kernel(2, *refs),
-        out_shape=jax.ShapeDtypeStruct((devices_wide, capacity, width), BF16),
+    rings, wide = groups // CORES, CORES * width
+    gate_up = (gate_weight[0], up_weight[0])
+    part = jax.ShapeDtypeStruct((2 * units, wide), BF16)
+    whole, held = pl.BlockSpec(memory_space=pl.ANY), pl.BlockSpec(memory_space=pltpu.VMEM)
+    packed, across = pl.pallas_call(
+        lambda *refs: pack_kernel(2, 2, *refs),
+        out_shape=[jax.ShapeDtypeStruct((devices_wide, capacity, width), BF16), part],
+        in_specs=[held, held, whole, whole],
+        out_specs=[held, whole],
+        scratch_shapes=[
+            pltpu.VMEM(part.shape, BF16),
+            pltpu.SemaphoreType.DMA((2,)),
+            pltpu.SemaphoreType.DMA,
+        ],
         name="pack",
-    )(ids, tokens)
+    )(ids, tokens, *gate_up)
     mix = pl.pallas_call(
         lambda *refs: mix_kernel(capacity, 2, *refs),
         out_shape=jax.ShapeDtypeStruct((arrived_count, tok_count), F32),
@@ -205,13 +240,17 @@
         name="mix",
     )(ids, route_weights.T)
 
-    blocks = chip_blocks(gate_weight[0], up_weight[0], width, groups)
+    ahead, behind, own = cut((1, 3, 0), gate_up, wide)
+    blocks = [own, ahead, across, behind]
+    for ring in range(1, rings):
+        blocks[ring] = lax.ppermute(
+            blocks[ring], "tensor", shift_pairs(groups, ring, 0)
+        )
     arrived = lax.all_to_all(packed, "expert", 0, 0, tiled=True)
     arrived = arrived.reshape(arrived_count, width)
     down_near, down_far = down_columns(down_weight[0], width, groups)
 
     partner = lax.ppermute(arrived, "tensor", shift_pairs(groups, 0, 1))
-    rings = groups // CORES
     near = pl.pallas_call(
         near_kernel,
         out_shape=jax.ShapeDtypeStruct((rings, 2 * units, arrived_count), F32),

time: 139 us -> 140 us (level)
  no operation moved by 1% of the time
where the time goes in v3:
time: 140 us; the launch traced here: 139 us
  starting transfers between devices  52.5 us (38%)
  blocking collectives  43.2 us (31%)
  waiting for transfers between devices  29.9 us (21%)
  Pallas kernels  13.1 us (9%)
    all_to_all x1, blocking collectives, body(): lax.all_to_all(half_out.reshape(devices_wide, capacity, width), 'expert',...  43.2 us
    all_to_all x1, starting transfers between devices, body(): arrived = lax.all_to_all(packed, 'expert', 0, 0, tiled=True)  18.8 us
    ppermute x3, starting transfers between devices, down_columns(): lax.ppermute(blocks[ring], 'tensor', shift_pairs(groups, ring, 0))  13.3 us
    ppermute x3, starting transfers between devices, body(): lax.ppermute(blocks[ring], 'tensor', shift_pairs(groups, ring, 0))  9.12 us
    ppermute x3, waiting for transfers between devices, down_columns(): lax.ppermute(blocks[ring], 'tensor', shift_pairs(groups, ring, 0))  8.62 us
    all_to_all x1, waiting for transfers between devices, body(): hidden = lax.all_to_all(hidden, 'tensor', 0, 0, tiled=True)  7.42 us
    all_to_all x1, waiting for transfers between devices, body(): lax.all_to_all(partial, 'tensor', 0, 0, axis_index_groups=same_core, tile...  7.05 us
    all_to_all x1, waiting for transfers between devices, body(): arrived = lax.all_to_all(packed, 'expert', 0, 0, tiled=True)  6.77 us
  transfers between devices with their start and end apart: 11, of which 4 were waited for; matrix products, arithmetic and copies ran while one was open for 0% of the time, Pallas kernels for 6%

profile of v3, /device:TPU:6, one launch (start us, length us, event | category | flops | bytes accessed | tf_op | source)
XLA Modules:
  0.0 139.3 jit_solution(12966019923343790990)
XLA Ops:
  0.0 3.4 %pack.1 = (bf16[64,4,896]{2,1,0:T(4,128)(2,1)}, bf16[128,1792]{1,0:T(8,128)(2,1)}) custom-call(s32[8,16]{1,0:T(8,128)} %bitcast.5, bf16[16,896]{1,0:T(8,128)(2,1)} %refs_1_.1, bf16[64,7168]{1,0:T(8,128)(2,1)} %bitcast.8, bf16[64,7168]{1,0:T(8,128)(2,1)} %bitcast.10), custom_call_target="tpu_custom_call" | custom-call | tf_op jit(solution)/shard_map/pack/pallas_call | solution.py:224
  3.4 18.8 %all-to-all-start = ((bf16[64,4,896]{2,1,0:T(4,128)(2,1)}), bf16[64,4,896]{2,1,0:T(4,128)(2,1)S(1)}, u32[]{:S(2)}, u32[]{:S(2)}) async-start(bf16[64,4,896]{2,1,0:T(4,128)(2,1)} %get-tuple-element.18), calls=%async_computation | async-start | bytes 917504 | tf_op jit(solution)/shard_map/all_to_all | solution.py:249
  22.2 2.1 %cut.3 = (bf16[64,1792]{1,0:T(8,128)(2,1)}, bf16[64,1792]{1,0:T(8,128)(2,1)}, bf16[64,1792]{1,0:T(8,128)(2,1)}, bf16[64,1792]{1,0:T(8,128)(2,1)}) custom-call(bf16[64,7168]{1,0:T(8,128)(2,1)} %bitcast.12), custom_call_target="tpu_custom_call" | custom-call | tf_op jit(solution)/shard_map/cut/pallas_call | solution.py:117
  24.3 3.5 %collective-permute-start.4 = (bf16[64,1792]{1,0:T(8,128)(2,1)}, bf16[64,1792]{1,0:T(8,128)(2,1)S(1)}, u32[]{:S(2)}, u32[]{:S(2)}) collective-permute-start(bf16[64,1792]{1,0:T(8,128)(2,1)} %get-tuple-element.26), channel_id=1, source_target_pairs={{0,2},{1,3},{2,4},{3,5},{4,6},{5,7},{6,0},{7,1},{8,10},{9,11},{10,... | collective-permute-start | bytes 688136 | tf_op jit(solution)/shard_map/ppermute | solution.py:184
  27.8 0.0 copy-start.4
  27.8 4.9 %collective-permute-start.5 = (bf16[64,1792]{1,0:T(8,128)(2,1)}, bf16[64,1792]{1,0:T(8,128)(2,1)S(1)}, u32[]{:S(2)}, u32[]{:S(2)}) collective-permute-start(bf16[64,1792]{1,0:T(8,128)(2,1)} %get-tuple-element.27), channel_id=1, source_target_pairs={{0,4},{1,5},{2,6},{3,7},{4,0},{5,1},{6,2},{7,3},{8,12},{9,13},{10,... | collective-permute-start | bytes 688136 | tf_op jit(solution)/shard_map/ppermute | solution.py:184
  32.7 2.3 %cut.2 = (bf16[128,1792]{1,0:T(8,128)(2,1)}, bf16[128,1792]{1,0:T(8,128)(2,1)}, bf16[128,1792]{1,0:T(8,128)(2,1)}) custom-call(bf16[64,7168]{1,0:T(8,128)(2,1)} %bitcast.9, bf16[64,7168]{1,0:T(8,128)(2,1)} %bitcast.11), custom_call_target="tpu_custom_call" | custom-call | tf_op jit(solution)/shard_map/cut/pallas_call | solution.py:117
  35.1 1.9 %collective-permute-start.1 = (bf16[128,1792]{1,0:T(8,128)(2,1)}, bf16[128,1792]{1,0:T(8,128)(2,1)S(1)}, u32[]{:S(2)}, u32[]{:S(2)}) collective-permute-start(bf16[128,1792]{1,0:T(8,128)(2,1)} %get-tuple-element.20), channel_id=1, source_target_pairs={{0,2},{1,3},{2,4},{3,5},{4,6},{5,7},{6,0},{7,1},{8,10},{9,11},{10,... | collective-permute-start | bytes 1376264 | tf_op jit(solution)/shard_map/ppermute | solution.py:246
  37.0 0.0 copy-done.4
  37.0 4.7 %collective-permute-start.2 = (bf16[128,1792]{1,0:T(8,128)(2,1)S(1)}, bf16[128,1792]{1,0:T(8,128)(2,1)S(1)}, u32[]{:S(2)}, u32[]{:S(2)}) collective-permute-start(bf16[128,1792]{1,0:T(8,128)(2,1)S(1)} %copy-done.4), channel_id=1, source_target_pairs={{0,4},{1,5},{2,6},{3,7},{4,0},{5,1},{6,2},{7,3},{8,12},{9,13},{10,... | collective-permute-start | bytes 1376264 | tf_op jit(solution)/shard_map/ppermute | solution.py:246
  41.7 0.0 copy-start.1
  41.7 2.5 %collective-permute-start.3 = (bf16[128,1792]{1,0:T(8,128)(2,1)}, bf16[128,1792]{1,0:T(8,128)(2,1)S(1)}, u32[]{:S(2)}, u32[]{:S(2)}) collective-permute-start(bf16[128,1792]{1,0:T(8,128)(2,1)} %get-tuple-element.22), channel_id=1, source_target_pairs={{0,6},{1,7},{2,0},{3,1},{4,2},{5,3},{6,4},{7,5},{8,14},{9,15},{10,... | collective-permute-start | bytes 1376264 | tf_op jit(solution)/shard_map/ppermute | solution.py:246
  44.2 6.8 %all-to-all-done = bf16[64,4,896]{2,1,0:T(4,128)(2,1)S(1)} async-done(((bf16[64,4,896]{2,1,0:T(4,128)(2,1)}), bf16[64,4,896]{2,1,0:T(4,128)(2,1)S(1)}, u32[]{:S(2)}, u32[]{:S(2)}) %all-to-all-start) | async-done | bytes 458784 | tf_op jit(solution)/shard_map/all_to_all | solution.py:249
  51.0 0.1 reshape.9.rows_ref
  51.1 0.0 collective-permute-done.4.refs_1_
  51.1 1.9 %collective-permute-start = (bf16[256,896]{1,0:T(8,128)(2,1)S(1)}, bf16[256,896]{1,0:T(8,128)(2,1)S(1)}, u32[]{:S(2)}, u32[]{:S(2)}) collective-permute-start(bf16[256,896]{1,0:T(8,128)(2,1)S(1)} %reshape.9.rows_ref), channel_id=1, source_target_pairs={{0,1},{1,0},{2,3},{3,2},{4,5},{5,4},{6,7},{7,6},{8,9},{9,8},{10,11... | collective-permute-start | bytes 1376264 | tf_op jit(solution)/shard_map/ppermute | solution.py:253
  53.1 0.0 collective-permute-done.5.refs_2_
  53.1 4.9 %collective-permute-start.6 = (bf16[64,1792]{1,0:T(8,128)(2,1)}, bf16[64,1792]{1,0:T(8,128)(2,1)S(1)}, u32[]{:S(2)}, u32[]{:S(2)}) collective-permute-start(bf16[64,1792]{1,0:T(8,128)(2,1)} %get-tuple-element.28), channel_id=1, source_target_pairs={{0,6},{1,7},{2,0},{3,1},{4,2},{5,3},{6,4},{7,5},{8,14},{9,15},{10,... | collective-permute-start | bytes 688136 | tf_op jit(solution)/shard_map/ppermute | solution.py:184
  58.0 8.6 %collective-permute-done.6.refs_3_ = bf16[64,1792]{1,0:T(8,128)(2,1)S(1)} collective-permute-done((bf16[64,1792]{1,0:T(8,128)(2,1)}, bf16[64,1792]{1,0:T(8,128)(2,1)S(1)}, u32[]{:S(2)}, u32[]{:S(2)}) %collective-permute-start.6) | collective-permute-done | bytes 229408 | tf_op jit(solution)/shard_map/ppermute | solution.py:184
  66.6 0.0 copy-done.1
  66.6 0.0 copy-start
  66.6 0.8 core_cut.1
  67.5 1.9 %collective-permute-start.7 = (bf16[256,896]{1,0:T(8,128)(2,1)}, bf16[256,896]{1,0:T(8,128)(2,1)S(1)}, u32[]{:S(2)}, u32[]{:S(2)}) collective-permute-start(bf16[256,896]{1,0:T(8,128)(2,1)} %get-tuple-element.30), channel_id=1, source_target_pairs={{0,1},{1,0},{2,3},{3,2},{4,5},{5,4},{6,7},{7,6},{8,9},{9,8},{10,11... | collective-permute-start | bytes 1376264 | tf_op jit(solution)/shard_map/ppermute | solution.py:193
  69.4 0.0 collective-permute-done.1.refs_1_
  69.4 0.0 collective-permute-done.2.refs_2_
  69.4 0.0 collective-permute-done.3.refs_3_
  69.4 0.0 copy-done
  69.4 0.7 near.1.near_ref
  70.1 0.0 collective-permute-done.rows_ref
  70.2 1.4 %far.1 = bf16[4,128,256]{2,1,0:T(8,128)(2,1)} custom-call(bf16[256,896]{1,0:T(8,128)(2,1)S(1)} %collective-permute-done.rows_ref, f32[4,128,256]{2,1,0:T(8,128)S(1)} %near.1.near_ref, bf16[128,1792]{1,0:T(8,128)(2,1)S(1)} %copy-done, bf16[128,1792]{1,0:T(8,128)(2,1)S(1)} %collective-permute-done.1.refs_1_, ...), custom_call_target="tpu_custom_call" | custom-call | tf_op jit(solution)/shard_map/far/pallas_call | solution.py:261
  71.6 0.0 copy-start.2
  71.6 0.0 copy-start.3
  71.6 4.0 %all-to-all-start.1 = ((bf16[4,128,256]{2,1,0:T(8,128)(2,1)}), bf16[4,128,256]{2,1,0:T(8,128)(2,1)S(1)}, u32[]{:S(2)}, u32[]{:S(2)}) async-start(bf16[4,128,256]{2,1,0:T(8,128)(2,1)} %far.1), calls=%async_computation.1 | async-start | bytes 524288 | tf_op jit(solution)/shard_map/all_to_all | solution.py:268
  75.6 0.0 copy-done.2
  75.6 0.0 copy-done.3
  75.6 0.2 mix.1.mix_ref
  75.9 7.1 %all-to-all-done.1.partial_ref = bf16[4,128,256]{2,1,0:T(8,128)(2,1)S(1)} async-done(((bf16[4,128,256]{2,1,0:T(8,128)(2,1)}), bf16[4,128,256]{2,1,0:T(8,128)(2,1)S(1)}, u32[]{:S(2)}, u32[]{:S(2)}) %all-to-all-start.1) | async-done | bytes 262176 | tf_op jit(solution)/shard_map/all_to_all | solution.py:268
  82.9 0.7 hidden.1
  83.7 3.4 %all-to-all-start.2 = ((bf16[8,64,256]{2,1,0:T(8,128)(2,1)}), bf16[8,64,256]{2,1,0:T(8,128)(2,1)S(1)}, u32[]{:S(2)}, u32[]{:S(2)}) async-start(bf16[8,64,256]{2,1,0:T(8,128)(2,1)} %hidden.1), calls=%async_computation.2 | async-start | bytes 524288 | tf_op jit(solution)/shard_map/all_to_all | solution.py:278
  87.1 0.0 collective-permute-done.7.far_ref
  87.1 7.4 %all-to-all-done.2.hidden_ref = bf16[8,64,256]{2,1,0:T(8,128)(2,1)S(1)} async-done(((bf16[8,64,256]{2,1,0:T(8,128)(2,1)}), bf16[8,64,256]{2,1,0:T(8,128)(2,1)S(1)}, u32[]{:S(2)}, u32[]{:S(2)}) %all-to-all-start.2) | async-done | bytes 262176 | tf_op jit(solution)/shard_map/all_to_all | solution.py:278
  94.5 0.5 down.1
  95.0 0.1 reshape.10
  95.1 43.2 %all_to_all.20 = bf16[64,4,896]{2,1,0:T(4,128)(2,1)S(1)} all-to-all(bf16[64,4,896]{2,1,0:T(4,128)(2,1)S(1)} %reshape.10), channel_id=1, replica_groups=mesh['expert'=64,'tensor'=8] {'expert'}, dimensions={0} | all-to-all | bytes 917504 | tf_op jit(solution)/shard_map/all_to_all | solution.py:286
  138.3 0.1 reshape.11.rows_ref
  138.4 0.9 combine.1
Async XLA Ops:
  3.4 47.6 %all-to-all-start = ((bf16[64,4,896]{2,1,0:T(4,128)(2,1)}), bf16[64,4,896]{2,1,0:T(4,128)(2,1)S(1)}, u32[]{:S(2)}, u32[]{:S(2)}) async-start(bf16[64,4,896]{2,1,0:T(4,128)(2,1)} %get-tuple-element.18), calls=%async_computation | async-start | bytes 917504 | tf_op jit(solution)/shard_map/all_to_all | solution.py:249
  24.3 26.8 %collective-permute-start.4 = (bf16[64,1792]{1,0:T(8,128)(2,1)}, bf16[64,1792]{1,0:T(8,128)(2,1)S(1)}, u32[]{:S(2)}, u32[]{:S(2)}) collective-permute-start(bf16[64,1792]{1,0:T(8,128)(2,1)} %get-tuple-element.26), channel_id=1, source_target_pairs={{0,2},{1,3},{2,4},{3,5},{4,6},{5,7},{6,0},{7,1},{8,10},{9,11},{10,... | collective-permute-start | bytes 688136 | tf_op jit(solution)/shard_map/ppermute | solution.py:184
  27.8 9.2 %copy-start.4 = (bf16[128,1792]{1,0:T(8,128)(2,1)S(1)}, bf16[128,1792]{1,0:T(8,128)(2,1)}, u32[]{:S(2)}) copy-start(bf16[128,1792]{1,0:T(8,128)(2,1)} %get-tuple-element.21) | copy-start | bytes 1376260
  27.8 25.3 %collective-permute-start.5 = (bf16[64,1792]{1,0:T(8,128)(2,1)}, bf16[64,1792]{1,0:T(8,128)(2,1)S(1)}, u32[]{:S(2)}, u32[]{:S(2)}) collective-permute-start(bf16[64,1792]{1,0:T(8,128)(2,1)} %get-tuple-element.27), channel_id=1, source_target_pairs={{0,4},{1,5},{2,6},{3,7},{4,0},{5,1},{6,2},{7,3},{8,12},{9,13},{10,... | collective-permute-start | bytes 688136 | tf_op jit(solution)/shard_map/ppermute | solution.py:184
  35.1 34.3 %collective-permute-start.1 = (bf16[128,1792]{1,0:T(8,128)(2,1)}, bf16[128,1792]{1,0:T(8,128)(2,1)S(1)}, u32[]{:S(2)}, u32[]{:S(2)}) collective-permute-start(bf16[128,1792]{1,0:T(8,128)(2,1)} %get-tuple-element.20), channel_id=1, source_target_pairs={{0,2},{1,3},{2,4},{3,5},{4,6},{5,7},{6,0},{7,1},{8,10},{9,11},{10,... | collective-permute-start | bytes 1376264 | tf_op jit(solution)/shard_map/ppermute | solution.py:246
  37.0 32.4 %collective-permute-start.2 = (bf16[128,1792]{1,0:T(8,128)(2,1)S(1)}, bf16[128,1792]{1,0:T(8,128)(2,1)S(1)}, u32[]{:S(2)}, u32[]{:S(2)}) collective-permute-start(bf16[128,1792]{1,0:T(8,128)(2,1)S(1)} %copy-done.4), channel_id=1, source_target_pairs={{0,4},{1,5},{2,6},{3,7},{4,0},{5,1},{6,2},{7,3},{8,12},{9,13},{10,... | collective-permute-start | bytes 1376264 | tf_op jit(solution)/shard_map/ppermute | solution.py:246
  41.7 24.9 %copy-start.1 = (bf16[64,1792]{1,0:T(8,128)(2,1)S(1)}, bf16[64,1792]{1,0:T(8,128)(2,1)}, u32[]{:S(2)}) copy-start(bf16[64,1792]{1,0:T(8,128)(2,1)} %get-tuple-element.25.refs_0_) | copy-start | bytes 688132
  41.7 27.7 %collective-permute-start.3 = (bf16[128,1792]{1,0:T(8,128)(2,1)}, bf16[128,1792]{1,0:T(8,128)(2,1)S(1)}, u32[]{:S(2)}, u32[]{:S(2)}) collective-permute-start(bf16[128,1792]{1,0:T(8,128)(2,1)} %get-tuple-element.22), channel_id=1, source_target_pairs={{0,6},{1,7},{2,0},{3,1},{4,2},{5,3},{6,4},{7,5},{8,14},{9,15},{10,... | collective-permute-start | bytes 1376264 | tf_op jit(solution)/shard_map/ppermute | solution.py:246
  51.1 19.0 %collective-permute-start = (bf16[256,896]{1,0:T(8,128)(2,1)S(1)}, bf16[256,896]{1,0:T(8,128)(2,1)S(1)}, u32[]{:S(2)}, u32[]{:S(2)}) collective-permute-start(bf16[256,896]{1,0:T(8,128)(2,1)S(1)} %reshape.9.rows_ref), channel_id=1, source_target_pairs={{0,1},{1,0},{2,3},{3,2},{4,5},{5,4},{6,7},{7,6},{8,9},{9,8},{10,11... | collective-permute-start | bytes 1376264 | tf_op jit(solution)/shard_map/ppermute | solution.py:253
  53.1 13.5 %collective-permute-start.6 = (bf16[64,1792]{1,0:T(8,128)(2,1)}, bf16[64,1792]{1,0:T(8,128)(2,1)S(1)}, u32[]{:S(2)}, u32[]{:S(2)}) collective-permute-start(bf16[64,1792]{1,0:T(8,128)(2,1)} %get-tuple-element.28), channel_id=1, source_target_pairs={{0,6},{1,7},{2,0},{3,1},{4,2},{5,3},{6,4},{7,5},{8,14},{9,15},{10,... | collective-permute-start | bytes 688136 | tf_op jit(solution)/shard_map/ppermute | solution.py:184
  66.6 2.8 %copy-start = (bf16[128,1792]{1,0:T(8,128)(2,1)S(1)}, bf16[128,1792]{1,0:T(8,128)(2,1)}, u32[]{:S(2)}) copy-start(bf16[128,1792]{1,0:T(8,128)(2,1)} %get-tuple-element.19.refs_0_) | copy-start | bytes 1376260
  67.5 19.6 %collective-permute-start.7 = (bf16[256,896]{1,0:T(8,128)(2,1)}, bf16[256,896]{1,0:T(8,128)(2,1)S(1)}, u32[]{:S(2)}, u32[]{:S(2)}) collective-permute-start(bf16[256,896]{1,0:T(8,128)(2,1)} %get-tuple-element.30), channel_id=1, source_target_pairs={{0,1},{1,0},{2,3},{3,2},{4,5},{5,4},{6,7},{7,6},{8,9},{9,8},{10,11... | collective-permute-start | bytes 1376264 | tf_op jit(solution)/shard_map/ppermute | solution.py:193
  71.6 4.0 %copy-start.2 = (s32[16,8]{0,1:T(8,128)S(1)}, s32[16,8]{0,1:T(8,128)}, u32[]{:S(2)}) copy-start(s32[16,8]{0,1:T(8,128)} %param.7) | copy-start | bytes 1540
  71.6 4.0 %copy-start.3 = (f32[16,8]{0,1:T(8,128)S(1)}, f32[16,8]{0,1:T(8,128)}, u32[]{:S(2)}) copy-start(f32[16,8]{0,1:T(8,128)} %param.8) | copy-start | bytes 1540
  71.6 11.3 %all-to-all-start.1 = ((bf16[4,128,256]{2,1,0:T(8,128)(2,1)}), bf16[4,128,256]{2,1,0:T(8,128)(2,1)S(1)}, u32[]{:S(2)}, u32[]{:S(2)}) async-start(bf16[4,128,256]{2,1,0:T(8,128)(2,1)} %far.1), calls=%async_computation.1 | async-start | bytes 524288 | tf_op jit(solution)/shard_map/all_to_all | solution.py:268
  83.7 10.8 %all-to-all-start.2 = ((bf16[8,64,256]{2,1,0:T(8,128)(2,1)}), bf16[8,64,256]{2,1,0:T(8,128)(2,1)S(1)}, u32[]{:S(2)}, u32[]{:S(2)}) async-start(bf16[8,64,256]{2,1,0:T(8,128)(2,1)} %hidden.1), calls=%async_computation.2 | async-start | bytes 524288 | tf_op jit(solution)/shard_map/all_to_all | solution.py:278

commit v4 on v3

--- a/solution.py
+++ b/solution.py
@@ -3,7 +3,7 @@
 from jax import lax
 from jax.experimental import pallas as pl
 from jax.experimental.pallas import tpu as pltpu
-from jax.sharding import PartitionSpec as P
+from jax.sharding import Mesh, PartitionSpec as P
 
 F32 = jnp.float32
 BF16 = jnp.bfloat16
@@ -48,18 +48,26 @@
     mix_ref[...] = select * weight
 
 
-def combine_kernel(mix_ref, rows_ref, out_ref):
-    mix = mix_ref[...]
-    high = mix.astype(BF16)
-    low = (mix - high.astype(F32)).astype(BF16)
-    rows = rows_ref[...]
-    dims = (((0,), (0,)), ((), ()))
-    total = lax.dot_general(high, rows, dims, preferred_element_type=F32)
-    total = total + lax.dot_general(low, rows, dims, preferred_element_type=F32)
-    out_ref[...] = total.astype(BF16)
+def combine_kernel(capacity, mix_ref, rows_ref, out_ref):
+    half = rows_ref.shape[1]
+    width = out_ref.shape[1]
+    row = lax.broadcasted_iota(jnp.int32, mix_ref.shape, 0)
+    first = lax.rem(row // capacity, 2) == 0
+    for place in range(2):
+        mix = jnp.where(first == (place == 0), mix_ref[...], 0.0)
+        high = mix.astype(BF16)
+        low = (mix - high.astype(F32)).astype(BF16)
+        rows = rows_ref[...] if place == 0 else rows_ref[:, 2 * half - width :]
+        dims = (((0,), (0,)), ((), ()))
+        total = lax.dot_general(high, rows, dims, preferred_element_type=F32)
+        total = total + lax.dot_general(low, rows, dims, preferred_element_type=F32)
+        cols = slice(0, half) if place == 0 else slice(half, width)
+        out_ref[:, cols] = total.astype(BF16)
 
 
 CORES = 2
+EXPERT = ("pair", "half")
+QUARTERS = [(0, 0), (0, 1), (1, 0), (1, 1)]
 VMEM_BYTES = 10 * 2**20
 
 
@@ -93,39 +101,39 @@
     return reads
 
 
-def cut_kernel(rings, parts, *refs):
-    weights, refs = refs[:parts], refs[parts:]
-    *outs, held, taken, given = refs
-    reads = [
-        cut_reads(ring, weights, held.at[place], taken.at[place])
-        for place, ring in enumerate(rings)
-    ]
+def cut_kernel(pieces, gate_ref, up_ref, down_ref, *refs):
+    outs, refs = refs[: len(pieces)], refs[len(pieces) :]
+    held, (taken, given) = refs[:-2], refs[-2:]
+    reads = []
+    for place, (which, ring) in enumerate(pieces):
+        weights = (gate_ref, up_ref) if which == "up" else (down_ref,)
+        reads.append(cut_reads(ring, weights, held[place], taken.at[place]))
     writes = []
     for place, out in enumerate(outs):
         for read in reads[place]:
             read.wait()
-        writes.append(pltpu.make_async_copy(held.at[place], out, given.at[place]))
+        writes.append(pltpu.make_async_copy(held[place], out, given.at[place]))
         writes[-1].start()
     for write in writes:
         write.wait()
 
 
-def cut(rings, weights, wide):
-    parts, units = len(weights), weights[0].shape[0]
-    shape = jax.ShapeDtypeStruct((parts * units, wide), BF16)
+def cut(pieces, gate, up, down, wide):
+    units = gate.shape[0]
+    shapes = [(2 * units if which == "up" else units, wide) for which, _ in pieces]
     whole = pl.BlockSpec(memory_space=pl.ANY)
     return pl.pallas_call(
-        lambda *refs: cut_kernel(rings, parts, *refs),
-        out_shape=[shape] * len(rings),
-        in_specs=[whole] * parts,
-        out_specs=[whole] * len(rings),
-        scratch_shapes=[
-            pltpu.VMEM((len(rings), *shape.shape), BF16),
-            pltpu.SemaphoreType.DMA((len(rings), parts)),
-            pltpu.SemaphoreType.DMA((len(rings),)),
+        lambda *refs: cut_kernel(pieces, *refs),
+        out_shape=[jax.ShapeDtypeStruct(shape, BF16) for shape in shapes],
+        in_specs=[whole] * 3,
+        out_specs=[whole] * len(pieces),
+        scratch_shapes=[pltpu.VMEM(shape, BF16) for shape in shapes]
+        + [
+            pltpu.SemaphoreType.DMA((len(pieces), 2)),
+            pltpu.SemaphoreType.DMA((len(pieces),)),
         ],
         name="cut",
-    )(*weights)
+    )(gate, up, down)
 
 
 def half_product(block_ref, rows_ref, half):
@@ -163,51 +171,61 @@
         out_ref[g] = hidden
 
 
-def core_cut_kernel(*refs):
-    *blocks, near_ref, far_ref = refs
-    core = lax.rem(lax.axis_index("tensor"), CORES)
-    units = blocks[0].shape[0]
-    width = near_ref.shape[1]
-    for ring, block in enumerate(blocks):
-        rows = pl.ds(ring * units, units)
-        near_ref[rows, :] = block[:, pl.ds(pl.multiple_of(core * width, 128), width)]
-        far_ref[rows, :] = block[:, pl.ds(pl.multiple_of((1 - core) * width, 128), width)]
-
-
-def down_columns(weight, width, groups):
-    units = weight.shape[0]
-    rings = groups // CORES
-    order = (1, 2, 3, 0)
-    cuts = cut(order, (weight,), CORES * width)
-    blocks = dict(zip(order, cuts))
-    for ring in range(1, rings):
-        blocks[ring] = lax.ppermute(
-            blocks[ring], "tensor", shift_pairs(groups, ring, 0)
+def quarter_kernel(*refs):
+    blocks, outs = refs[:-4], refs[-4:]
+    core, half = lax.rem(lax.axis_index("tensor"), CORES), lax.axis_index("half")
+    units, wide = blocks[0].shape
+    width, part = wide // CORES, outs[0].shape[1]
+    for (other_half, other_core), out in zip(QUARTERS, outs):
+        to_core = lax.rem(core + other_core, CORES)
+        to_half = lax.rem(half + other_half, 2)
+        start = to_core * width + to_half * (width - part)
+        cols = pl.ds(pl.multiple_of(start, 128), part)
+        for ring, block in enumerate(blocks):
+            out[pl.ds(ring * units, units), :] = block[:, cols]
+
+
+def down_quarters(blocks, part, groups):
+    units, rings = blocks[0].shape[0], len(blocks)
+    own, core, pair, both = pl.pallas_call(
+        quarter_kernel,
+        out_shape=[jax.ShapeDtypeStruct((rings * units, part), BF16)] * 4,
+        compiler_params=pltpu.CompilerParams(vmem_limit_bytes=VMEM_BYTES),
+        name="quarter",
+    )(*blocks)
+    swap = shift_pairs(groups, 0, 1)
+    across = [(i + h * groups, j + (1 - h) * groups) for h in range(2) for i, j in swap]
+    pair = lax.ppermute(pair, "half", [(0, 1), (1, 0)])
+    both = lax.ppermute(both, ("half", "tensor"), across)
+    core = lax.ppermute(core, "tensor", swap)
+    return own, core, pair, both
+
+
+def down_kernel(hidden_ref, *refs):
+    *blocks, out_ref, held = refs
+    members, units, _ = hidden_ref.shape
+    groups = members // 2
+    me, half = lax.axis_index("tensor"), lax.axis_index("half")
+    total = None
+    for place, (other_half, other_core) in enumerate(QUARTERS):
+        from_half = lax.rem(half + other_half, 2)
+        for ring in range(groups // CORES):
+            source = moved_by(me, groups, ring, other_core, sign=-1)
+            held[place, pl.ds(ring * units, units), :] = hidden_ref[
+                from_half * groups + source
+            ]
+        term = lax.dot_general(
+            held[place],
+            blocks[place][...],
+            (((0,), (0,)), ((), ())),
+            preferred_element_type=F32,
         )
-    near, far = pl.pallas_call(
-        core_cut_kernel,
-        out_shape=[jax.ShapeDtypeStruct((rings * units, width), BF16)] * 2,
-        compiler_params=pltpu.CompilerParams(vmem_limit_bytes=VMEM_BYTES),
-        name="core_cut",
-    )(*[blocks[ring] for ring in range(rings)])
-    return near, lax.ppermute(far, "tensor", shift_pairs(groups, 0, 1))
-
-
-def down_kernel(hidden_ref, near_ref, far_ref, out_ref, held):
-    groups, units, _ = hidden_ref.shape
-    me = lax.axis_index("tensor")
-    for core in range(CORES):
-        for ring in range(groups // CORES):
-            source = moved_by(me, groups, ring, core, sign=-1)
-            held[core, pl.ds(ring * units, units), :] = hidden_ref[source]
-    dims = (((0,), (0,)), ((), ()))
-    total = lax.dot_general(held[0], near_ref[...], dims, preferred_element_type=F32)
-    total = total + lax.dot_general(held[1], far_ref[...], dims, preferred_element_type=F32)
+        total = term if total is None else total + term
     out_ref[...] = total.astype(BF16)
 
 
 def body(tokens, expert_ids, route_weights, gate_weight, up_weight, down_weight):
-    devices_wide = lax.axis_size("expert")
+    devices_wide = lax.axis_size(EXPERT)
     groups = lax.axis_size("tensor")
     experts = devices_wide // 2
     tok_count, per_token = expert_ids.shape
@@ -219,15 +237,15 @@
     ids = expert_ids.T
     rings, wide = groups // CORES, CORES * width
     gate_up = (gate_weight[0], up_weight[0])
-    part = jax.ShapeDtypeStruct((2 * units, wide), BF16)
+    block = jax.ShapeDtypeStruct((2 * units, wide), BF16)
     whole, held = pl.BlockSpec(memory_space=pl.ANY), pl.BlockSpec(memory_space=pltpu.VMEM)
     packed, across = pl.pallas_call(
         lambda *refs: pack_kernel(2, 2, *refs),
-        out_shape=[jax.ShapeDtypeStruct((devices_wide, capacity, width), BF16), part],
+        out_shape=[jax.ShapeDtypeStruct((devices_wide, capacity, width), BF16), block],
         in_specs=[held, held, whole, whole],
         out_specs=[held, whole],
         scratch_shapes=[
-            pltpu.VMEM(part.shape, BF16),
+            pltpu.VMEM(block.shape, BF16),
             pltpu.SemaphoreType.DMA((2,)),
             pltpu.SemaphoreType.DMA,
         ],
@@ -240,15 +258,20 @@
         name="mix",
     )(ids, route_weights.T)
 
-    ahead, behind, own = cut((1, 3, 0), gate_up, wide)
+    pieces = [("up", 1), ("up", 3)] + [("down", ring) for ring in (1, 2, 3)]
+    pieces += [("up", 0), ("down", 0)]
+    ahead, behind, *down, own, down_own = cut(pieces, *gate_up, down_weight[0], wide)
     blocks = [own, ahead, across, behind]
+    down = [down_own, *down]
     for ring in range(1, rings):
         blocks[ring] = lax.ppermute(
             blocks[ring], "tensor", shift_pairs(groups, ring, 0)
         )
-    arrived = lax.all_to_all(packed, "expert", 0, 0, tiled=True)
+        down[ring] = lax.ppermute(down[ring], "tensor", shift_pairs(groups, ring, 0))
+    arrived = lax.all_to_all(packed, EXPERT, 0, 0, tiled=True)
     arrived = arrived.reshape(arrived_count, width)
-    down_near, down_far = down_columns(down_weight[0], width, groups)
+    part = -(-width // 256) * 128
+    quarters = down_quarters(down, part, groups)
 
     partner = lax.ppermute(arrived, "tensor", shift_pairs(groups, 0, 1))
     near = pl.pallas_call(
@@ -270,24 +293,24 @@
     )
     hidden = pl.pallas_call(
         hidden_kernel,
-        out_shape=jax.ShapeDtypeStruct((groups, units, arrived_count), BF16),
+        out_shape=jax.ShapeDtypeStruct((2 * groups, units, arrived_count), BF16),
         compiler_params=pltpu.CompilerParams(vmem_limit_bytes=VMEM_BYTES),
         name="hidden",
     )(partial)
     hidden, mix = lax.optimization_barrier((hidden, mix))
-    hidden = lax.all_to_all(hidden, "tensor", 0, 0, tiled=True)
+    hidden = lax.all_to_all(hidden, ("half", "tensor"), 0, 0, tiled=True)
     half_out = pl.pallas_call(
         down_kernel,
-        out_shape=jax.ShapeDtypeStruct((arrived_count, width), BF16),
-        scratch_shapes=[pltpu.VMEM((2, groups // 2 * units, arrived_count), BF16)],
+        out_shape=jax.ShapeDtypeStruct((arrived_count, part), BF16),
+        scratch_shapes=[pltpu.VMEM((4, rings * units, arrived_count), BF16)],
         compiler_params=pltpu.CompilerParams(vmem_limit_bytes=VMEM_BYTES),
         name="down",
-    )(hidden, down_near, down_far)
+    )(hidden, *quarters)
     returned = lax.all_to_all(
-        half_out.reshape(devices_wide, capacity, width), "expert", 0, 0, tiled=True
-    ).reshape(arrived_count, width)
+        half_out.reshape(devices_wide, capacity, part), EXPERT, 0, 0, tiled=True
+    ).reshape(arrived_count, part)
     return pl.pallas_call(
-        combine_kernel,
+        lambda *refs: combine_kernel(capacity, *refs),
         out_shape=jax.ShapeDtypeStruct((tok_count, width), BF16),
         compiler_params=pltpu.CompilerParams(vmem_limit_bytes=VMEM_BYTES),
         name="combine",
@@ -295,18 +318,21 @@
 
 
 def solution(mesh):
+    wide, groups = mesh.devices.shape
+    mesh = Mesh(mesh.devices.reshape(wide // 2, 2, groups), (*EXPERT, "tensor"))
     placed = (
-        P("expert", "tensor"),
-        P("expert", None),
-        P("expert", None),
-        P("expert", "tensor", None),
-        P("expert", "tensor", None),
-        P("expert", "tensor", None),
+        P(EXPERT, "tensor"),
+        P(EXPERT, None),
+        P(EXPERT, None),
+        P(EXPERT, "tensor", None),
+        P(EXPERT, "tensor", None),
+        P(EXPERT, "tensor", None),
     )
+
     def step(*args):
         return body(*args)
 
     step = jax.shard_map(
-        step, mesh=mesh, in_specs=placed, out_specs=P("expert", "tensor"), check_vma=False
+        step, mesh=mesh, in_specs=placed, out_specs=P(EXPERT, "tensor"), check_vma=False
     )
     return step

time: 140 us -> 147 us (1.050)
  waiting for transfers between devices: 29.9 us -> 40.3 us
  blocking collectives: 43.2 us -> 34 us
  starting transfers between devices: 52.5 us -> 60 us
  Pallas kernels: 13.1 us -> 10.9 us
    ppermute x4 -> x6, waiting for transfers between devices: 8.62 us -> 18.3 us  [the longest x3 8.22 us: body(): lax.ppermute(down[ring], 'tensor', shift_pairs(groups, ring, 0))]
    all_to_all x1, blocking collectives: 43.2 us -> 34 us  [body(): lax.all_to_all(half_out.reshape(devices_wide, capacity, part), EXPERT, 0,...]
    ppermute x4 -> x6, starting transfers between devices: 15.3 us -> 19.3 us  [the longest x3 11.7 us: body(): lax.ppermute(down[ring], 'tensor', shift_pairs(groups, ring, 0))]
    ppermute x3, starting transfers between devices: 9.12 us -> 11.7 us  [body(): lax.ppermute(blocks[ring], 'tensor', shift_pairs(groups, ring, 0))]
    pallas_call x5 -> x4, Pallas kernels: 6.87 us -> 4.59 us  [the longest x1 2.74 us: cut(): pl.pallas_call(lambda *refs: cut_kernel(pieces, *refs), out_shape=[jax.Sh...]
  transfers between devices with their start and end apart: 11 -> 13, of which waited for: 4 -> 7; matrix products, arithmetic and copies ran while one was open for 0% -> 0% of each run, Pallas kernels for 6% -> 3%
where the time goes in v4:
time: 147 us; the launch traced here: 146 us
  starting transfers between devices  60 us (41%)
  waiting for transfers between devices  40.3 us (27%)
  blocking collectives  34 us (23%)
  Pallas kernels  10.9 us (7%)
    all_to_all x1, blocking collectives, body(): lax.all_to_all(half_out.reshape(devices_wide, capacity, part), EXPERT, 0,...  34 us
    all_to_all x1, starting transfers between devices, body(): arrived = lax.all_to_all(packed, EXPERT, 0, 0, tiled=True)  18.8 us
    all_to_all x1, waiting for transfers between devices, body(): arrived = lax.all_to_all(packed, EXPERT, 0, 0, tiled=True)  14.3 us
    ppermute x3, starting transfers between devices, body(): lax.ppermute(down[ring], 'tensor', shift_pairs(groups, ring, 0))  11.7 us
    ppermute x3, starting transfers between devices, body(): lax.ppermute(blocks[ring], 'tensor', shift_pairs(groups, ring, 0))  11.7 us
    ppermute x3, waiting for transfers between devices, body(): lax.ppermute(down[ring], 'tensor', shift_pairs(groups, ring, 0))  8.22 us
    all_to_all x1, waiting for transfers between devices, body(): lax.all_to_all(partial, 'tensor', 0, 0, axis_index_groups=same_core, tile...  6.69 us
    ppermute x1, waiting for transfers between devices, down_quarters(): pair = lax.ppermute(pair, 'half', [(0, 1), (1, 0)])  5.38 us
  transfers between devices with their start and end apart: 13, of which 7 were waited for; matrix products, arithmetic and copies ran while one was open for 0% of the time, Pallas kernels for 3%

profile of v4, /device:TPU:6, one launch (start us, length us, event | category | flops | bytes accessed | tf_op | source)
XLA Modules:
  0.0 145.7 jit_solution(3801857129268147888)
XLA Ops:
  0.0 3.4 %pack.1 = (bf16[64,4,896]{2,1,0:T(4,128)(2,1)}, bf16[128,1792]{1,0:T(8,128)(2,1)}) custom-call(s32[8,16]{1,0:T(8,128)} %bitcast.5, bf16[16,896]{1,0:T(8,128)(2,1)} %refs_1_.1, bf16[64,7168]{1,0:T(8,128)(2,1)} %bitcast.8, bf16[64,7168]{1,0:T(8,128)(2,1)} %bitcast.10), custom_call_target="tpu_custom_call" | custom-call | tf_op jit(solution)/shard_map/pack/pallas_call | solution.py:242
  3.4 18.8 %all-to-all-start = ((bf16[64,4,896]{2,1,0:T(4,128)(2,1)}), bf16[64,4,896]{2,1,0:T(4,128)(2,1)S(1)}, u32[]{:S(2)}, u32[]{:S(2)}) async-start(bf16[64,4,896]{2,1,0:T(4,128)(2,1)} %get-tuple-element.20), calls=%async_computation | async-start | bytes 917504 | tf_op jit(solution)/shard_map/all_to_all | solution.py:271
  22.2 0.0 copy-start.4
  22.3 2.7 %cut.1 = (bf16[128,1792]{1,0:T(8,128)(2,1)}, bf16[128,1792]{1,0:T(8,128)(2,1)}, bf16[64,1792]{1,0:T(8,128)(2,1)}, bf16[64,1792]{1,0:T(8,128)(2,1)}, bf16[64,1792...) custom-call(bf16[64,7168]{1,0:T(8,128)(2,1)} %bitcast.9, bf16[64,7168]{1,0:T(8,128)(2,1)} %bitcast.11, ...), custom_call_target="tpu_custom_call" | custom-call | tf_op jit(solution)/shard_map/cut/pallas_call | solution.py:125
  25.0 3.5 %collective-permute-start.1 = (bf16[128,1792]{1,0:T(8,128)(2,1)}, bf16[128,1792]{1,0:T(8,128)(2,1)S(1)}, u32[]{:S(2)}, u32[]{:S(2)}) collective-permute-start(bf16[128,1792]{1,0:T(8,128)(2,1)} %get-tuple-element.22), channel_id=1, source_target_pairs={{0,2},{1,3},{2,4},{3,5},{4,6},{5,7},{6,0},{7,1},{8,10},{9,11},{10,... | collective-permute-start | bytes 1376264 | tf_op jit(solution)/shard_map/ppermute | solution.py:267
  28.5 0.0 copy-done.4
  28.5 4.8 %collective-permute-start.2 = (bf16[128,1792]{1,0:T(8,128)(2,1)S(1)}, bf16[128,1792]{1,0:T(8,128)(2,1)S(1)}, u32[]{:S(2)}, u32[]{:S(2)}) collective-permute-start(bf16[128,1792]{1,0:T(8,128)(2,1)S(1)} %copy-done.4), channel_id=1, source_target_pairs={{0,4},{1,5},{2,6},{3,7},{4,0},{5,1},{6,2},{7,3},{8,12},{9,13},{10,... | collective-permute-start | bytes 1376264 | tf_op jit(solution)/shard_map/ppermute | solution.py:267
  33.3 0.0 copy-start
  33.3 3.4 %collective-permute-start.3 = (bf16[128,1792]{1,0:T(8,128)(2,1)}, bf16[128,1792]{1,0:T(8,128)(2,1)S(1)}, u32[]{:S(2)}, u32[]{:S(2)}) collective-permute-start(bf16[128,1792]{1,0:T(8,128)(2,1)} %get-tuple-element.24), channel_id=1, source_target_pairs={{0,6},{1,7},{2,0},{3,1},{4,2},{5,3},{6,4},{7,5},{8,14},{9,15},{10,... | collective-permute-start | bytes 1376264 | tf_op jit(solution)/shard_map/ppermute | solution.py:267
  36.7 14.3 %all-to-all-done = bf16[64,4,896]{2,1,0:T(4,128)(2,1)S(1)} async-done(((bf16[64,4,896]{2,1,0:T(4,128)(2,1)}), bf16[64,4,896]{2,1,0:T(4,128)(2,1)S(1)}, u32[]{:S(2)}, u32[]{:S(2)}) %all-to-all-start) | async-done | bytes 458784 | tf_op jit(solution)/shard_map/all_to_all | solution.py:271
  51.0 0.1 reshape.9.rows_ref
  51.1 1.9 %collective-permute-start = (bf16[256,896]{1,0:T(8,128)(2,1)S(1)}, bf16[256,896]{1,0:T(8,128)(2,1)S(1)}, u32[]{:S(2)}, u32[]{:S(2)}) collective-permute-start(bf16[256,896]{1,0:T(8,128)(2,1)S(1)} %reshape.9.rows_ref), channel_id=1, source_target_pairs={{0,1},{1,0},{2,3},{3,2},{4,5},{5,4},{6,7},{7,6},{8,9},{9,8},{10,11... | collective-permute-start | bytes 1376264 | tf_op jit(solution)/shard_map/ppermute | solution.py:276
  53.1 0.0 collective-permute-done.1.refs_1_
  53.1 0.0 collective-permute-done.2.refs_2_
  53.1 0.0 collective-permute-done.3.refs_3_
  53.1 0.0 copy-done
  53.1 0.7 near.1.near_ref
  53.8 1.0 collective-permute-done.rows_ref
  54.9 1.4 far.1
  56.3 4.6 %all-to-all-start.1 = ((bf16[4,128,256]{2,1,0:T(8,128)(2,1)}), bf16[4,128,256]{2,1,0:T(8,128)(2,1)S(1)}, u32[]{:S(2)}, u32[]{:S(2)}) async-start(bf16[4,128,256]{2,1,0:T(8,128)(2,1)} %far.1), calls=%async_computation.1 | async-start | bytes 524288 | tf_op jit(solution)/shard_map/all_to_all | solution.py:291
  60.9 0.0 copy-done.2
  60.9 0.0 copy-done.3
  60.9 0.2 mix.1.refs_0_
  61.1 6.7 %all-to-all-done.1.partial_ref = bf16[4,128,256]{2,1,0:T(8,128)(2,1)S(1)} async-done(((bf16[4,128,256]{2,1,0:T(8,128)(2,1)}), bf16[4,128,256]{2,1,0:T(8,128)(2,1)S(1)}, u32[]{:S(2)}, u32[]{:S(2)}) %all-to-all-start.1) | async-done | bytes 262176 | tf_op jit(solution)/shard_map/all_to_all | solution.py:291
  67.8 0.9 hidden.1
  68.7 3.7 %all-to-all-start.2 = ((bf16[16,64,256]{2,1,0:T(8,128)(2,1)}), bf16[16,64,256]{2,1,0:T(8,128)(2,1)S(1)}, u32[]{:S(2)}, u32[]{:S(2)}) async-start(bf16[16,64,256]{2,1,0:T(8,128)(2,1)} %hidden.1), calls=%async_computation.2 | async-start | bytes 1048576 | tf_op jit(solution)/shard_map/all_to_all | solution.py:301
  72.4 0.0 copy-done.7
  72.5 3.7 %collective-permute-start.4 = (bf16[64,1792]{1,0:T(8,128)(2,1)S(1)}, bf16[64,1792]{1,0:T(8,128)(2,1)S(1)}, u32[]{:S(2)}, u32[]{:S(2)}) collective-permute-start(bf16[64,1792]{1,0:T(8,128)(2,1)S(1)} %copy-done.7), channel_id=1, source_target_pairs={{0,2},{1,3},{2,4},{3,5},{4,6},{5,7},{6,0},{7,1},{8,10},{9,11},{10,... | collective-permute-start | bytes 688136 | tf_op jit(solution)/shard_map/ppermute | solution.py:270
  76.2 0.0 copy-done.6
  76.2 4.6 %collective-permute-start.5 = (bf16[64,1792]{1,0:T(8,128)(2,1)S(1)}, bf16[64,1792]{1,0:T(8,128)(2,1)S(1)}, u32[]{:S(2)}, u32[]{:S(2)}) collective-permute-start(bf16[64,1792]{1,0:T(8,128)(2,1)S(1)} %copy-done.6), channel_id=1, source_target_pairs={{0,4},{1,5},{2,6},{3,7},{4,0},{5,1},{6,2},{7,3},{8,12},{9,13},{10,... | collective-permute-start | bytes 688136 | tf_op jit(solution)/shard_map/ppermute | solution.py:270
  80.8 0.0 copy-done.5
  80.8 3.4 %collective-permute-start.6 = (bf16[64,1792]{1,0:T(8,128)(2,1)S(1)}, bf16[64,1792]{1,0:T(8,128)(2,1)S(1)}, u32[]{:S(2)}, u32[]{:S(2)}) collective-permute-start(bf16[64,1792]{1,0:T(8,128)(2,1)S(1)} %copy-done.5), channel_id=1, source_target_pairs={{0,6},{1,7},{2,0},{3,1},{4,2},{5,3},{6,4},{7,5},{8,14},{9,15},{10,... | collective-permute-start | bytes 688136 | tf_op jit(solution)/shard_map/ppermute | solution.py:270
  84.2 3.3 %collective-permute-done.4.refs_1_ = bf16[64,1792]{1,0:T(8,128)(2,1)S(1)} collective-permute-done((bf16[64,1792]{1,0:T(8,128)(2,1)S(1)}, bf16[64,1792]{1,0:T(8,128)(2,1)S(1)}, u32[]{:S(2)}, u32[]{:S(2)}) %collective-permute-start.4) | collective-permute-done | bytes 229408 | tf_op jit(solution)/shard_map/ppermute | solution.py:270
  87.5 4.9 %collective-permute-done.5.refs_2_ = bf16[64,1792]{1,0:T(8,128)(2,1)S(1)} collective-permute-done((bf16[64,1792]{1,0:T(8,128)(2,1)S(1)}, bf16[64,1792]{1,0:T(8,128)(2,1)S(1)}, u32[]{:S(2)}, u32[]{:S(2)}) %collective-permute-start.5) | collective-permute-done | bytes 229408 | tf_op jit(solution)/shard_map/ppermute | solution.py:270
  92.4 0.0 collective-permute-done.6.refs_3_
  92.4 0.1 quarter.1
  92.5 1.9 %collective-permute-start.7 = (bf16[256,512]{1,0:T(8,128)(2,1)S(1)}, bf16[256,512]{1,0:T(8,128)(2,1)S(1)}, u32[]{:S(2)}, u32[]{:S(2)}) collective-permute-start(bf16[256,512]{1,0:T(8,128)(2,1)S(1)} %get-tuple-element.32), channel_id=1, source_target_pairs={{0,1},{1,0},{2,3},{3,2},{4,5},{5,4},{6,7},{7,6},{8,9},{9,8},{10,11... | collective-permute-start | bytes 786440 | tf_op jit(solution)/shard_map/ppermute | solution.py:200
  94.4 3.4 %collective-permute-start.8 = (bf16[256,512]{1,0:T(8,128)(2,1)S(1)}, bf16[256,512]{1,0:T(8,128)(2,1)S(1)}, u32[]{:S(2)}, u32[]{:S(2)}) collective-permute-start(bf16[256,512]{1,0:T(8,128)(2,1)S(1)} %get-tuple-element.33), channel_id=1, source_target_pairs={{0,8},{8,0},{1,9},{9,1},{2,10},{10,2},{3,11},{11,3},{4,12},{12,4},... | collective-permute-start | bytes 786440 | tf_op jit(solution)/shard_map/ppermute | solution.py:198
  97.8 2.3 %collective-permute-start.9 = (bf16[256,512]{1,0:T(8,128)(2,1)S(1)}, bf16[256,512]{1,0:T(8,128)(2,1)S(1)}, u32[]{:S(2)}, u32[]{:S(2)}) collective-permute-start(bf16[256,512]{1,0:T(8,128)(2,1)S(1)} %get-tuple-element.34), channel_id=1, source_target_pairs={{0,9},{1,8},{2,11},{3,10},{4,13},{5,12},{6,15},{7,14},{8,1},{9,0},... | collective-permute-start | bytes 786440 | tf_op jit(solution)/shard_map/ppermute | solution.py:199
  100.1 0.0 collective-permute-done.7.refs_1_
  100.1 5.4 %collective-permute-done.8.refs_2_ = bf16[256,512]{1,0:T(8,128)(2,1)S(1)} collective-permute-done((bf16[256,512]{1,0:T(8,128)(2,1)S(1)}, bf16[256,512]{1,0:T(8,128)(2,1)S(1)}, u32[]{:S(2)}, u32[]{:S(2)}) %collective-permute-start.8) | collective-permute-done | bytes 262176 | tf_op jit(solution)/shard_map/ppermute | solution.py:198
  105.5 4.7 %collective-permute-done.9.refs_3_ = bf16[256,512]{1,0:T(8,128)(2,1)S(1)} collective-permute-done((bf16[256,512]{1,0:T(8,128)(2,1)S(1)}, bf16[256,512]{1,0:T(8,128)(2,1)S(1)}, u32[]{:S(2)}, u32[]{:S(2)}) %collective-permute-start.9) | collective-permute-done | bytes 262176 | tf_op jit(solution)/shard_map/ppermute | solution.py:199
  110.1 0.0 all-to-all-done.2.hidden_ref
  110.2 0.5 down.1
  110.6 0.1 reshape.10
  110.7 34.0 %all_to_all.20 = bf16[64,4,512]{2,1,0:T(4,128)(2,1)S(1)} all-to-all(bf16[64,4,512]{2,1,0:T(4,128)(2,1)S(1)} %reshape.10), channel_id=1, replica_groups=mesh['pair'=32,'half'=2,'tensor'=8] {'pair','half'}, dimensions={0} | all-to-all | bytes 524288 | tf_op jit(solution)/shard_map/all_to_all | solution.py:309
  144.7 0.1 reshape.11.refs_1_
  144.8 0.9 combine.1
  (7 shorter events, 0.0 us)
Async XLA Ops:
  3.4 47.6 %all-to-all-start = ((bf16[64,4,896]{2,1,0:T(4,128)(2,1)}), bf16[64,4,896]{2,1,0:T(4,128)(2,1)S(1)}, u32[]{:S(2)}, u32[]{:S(2)}) async-start(bf16[64,4,896]{2,1,0:T(4,128)(2,1)} %get-tuple-element.20), calls=%async_computation | async-start | bytes 917504 | tf_op jit(solution)/shard_map/all_to_all | solution.py:271
  22.2 6.3 %copy-start.4 = (bf16[128,1792]{1,0:T(8,128)(2,1)S(1)}, bf16[128,1792]{1,0:T(8,128)(2,1)}, u32[]{:S(2)}) copy-start(bf16[128,1792]{1,0:T(8,128)(2,1)} %get-tuple-element.23) | copy-start | bytes 1376260
  25.0 28.1 %collective-permute-start.1 = (bf16[128,1792]{1,0:T(8,128)(2,1)}, bf16[128,1792]{1,0:T(8,128)(2,1)S(1)}, u32[]{:S(2)}, u32[]{:S(2)}) collective-permute-start(bf16[128,1792]{1,0:T(8,128)(2,1)} %get-tuple-element.22), channel_id=1, source_target_pairs={{0,2},{1,3},{2,4},{3,5},{4,6},{5,7},{6,0},{7,1},{8,10},{9,11},{10,... | collective-permute-start | bytes 1376264 | tf_op jit(solution)/shard_map/ppermute | solution.py:267
  28.5 24.6 %collective-permute-start.2 = (bf16[128,1792]{1,0:T(8,128)(2,1)S(1)}, bf16[128,1792]{1,0:T(8,128)(2,1)S(1)}, u32[]{:S(2)}, u32[]{:S(2)}) collective-permute-start(bf16[128,1792]{1,0:T(8,128)(2,1)S(1)} %copy-done.4), channel_id=1, source_target_pairs={{0,4},{1,5},{2,6},{3,7},{4,0},{5,1},{6,2},{7,3},{8,12},{9,13},{10,... | collective-permute-start | bytes 1376264 | tf_op jit(solution)/shard_map/ppermute | solution.py:267
  33.3 19.8 %copy-start = (bf16[128,1792]{1,0:T(8,128)(2,1)S(1)}, bf16[128,1792]{1,0:T(8,128)(2,1)}, u32[]{:S(2)}) copy-start(bf16[128,1792]{1,0:T(8,128)(2,1)} %get-tuple-element.21.refs_0_) | copy-start | bytes 1376260
  33.3 19.8 %collective-permute-start.3 = (bf16[128,1792]{1,0:T(8,128)(2,1)}, bf16[128,1792]{1,0:T(8,128)(2,1)S(1)}, u32[]{:S(2)}, u32[]{:S(2)}) collective-permute-start(bf16[128,1792]{1,0:T(8,128)(2,1)} %get-tuple-element.24), channel_id=1, source_target_pairs={{0,6},{1,7},{2,0},{3,1},{4,2},{5,3},{6,4},{7,5},{8,14},{9,15},{10,... | collective-permute-start | bytes 1376264 | tf_op jit(solution)/shard_map/ppermute | solution.py:267
  51.1 3.7 %collective-permute-start = (bf16[256,896]{1,0:T(8,128)(2,1)S(1)}, bf16[256,896]{1,0:T(8,128)(2,1)S(1)}, u32[]{:S(2)}, u32[]{:S(2)}) collective-permute-start(bf16[256,896]{1,0:T(8,128)(2,1)S(1)} %reshape.9.rows_ref), channel_id=1, source_target_pairs={{0,1},{1,0},{2,3},{3,2},{4,5},{5,4},{6,7},{7,6},{8,9},{9,8},{10,11... | collective-permute-start | bytes 1376264 | tf_op jit(solution)/shard_map/ppermute | solution.py:276
  56.3 4.6 %copy-start.2 = (s32[16,8]{0,1:T(8,128)S(1)}, s32[16,8]{0,1:T(8,128)}, u32[]{:S(2)}) copy-start(s32[16,8]{0,1:T(8,128)} %param.7) | copy-start | bytes 1540
  56.3 4.6 %copy-start.3 = (f32[16,8]{0,1:T(8,128)S(1)}, f32[16,8]{0,1:T(8,128)}, u32[]{:S(2)}) copy-start(f32[16,8]{0,1:T(8,128)} %param.8) | copy-start | bytes 1540
  56.3 11.5 %all-to-all-start.1 = ((bf16[4,128,256]{2,1,0:T(8,128)(2,1)}), bf16[4,128,256]{2,1,0:T(8,128)(2,1)S(1)}, u32[]{:S(2)}, u32[]{:S(2)}) async-start(bf16[4,128,256]{2,1,0:T(8,128)(2,1)} %far.1), calls=%async_computation.1 | async-start | bytes 524288 | tf_op jit(solution)/shard_map/all_to_all | solution.py:291
  68.7 3.7 %copy-start.7 = (bf16[64,1792]{1,0:T(8,128)(2,1)S(1)}, bf16[64,1792]{1,0:T(8,128)(2,1)}, u32[]{:S(2)}) copy-start(bf16[64,1792]{1,0:T(8,128)(2,1)} %get-tuple-element.28) | copy-start | bytes 688132
  68.7 7.5 %copy-start.6 = (bf16[64,1792]{1,0:T(8,128)(2,1)S(1)}, bf16[64,1792]{1,0:T(8,128)(2,1)}, u32[]{:S(2)}) copy-start(bf16[64,1792]{1,0:T(8,128)(2,1)} %get-tuple-element.29) | copy-start | bytes 688132
  68.7 12.1 %copy-start.5 = (bf16[64,1792]{1,0:T(8,128)(2,1)S(1)}, bf16[64,1792]{1,0:T(8,128)(2,1)}, u32[]{:S(2)}) copy-start(bf16[64,1792]{1,0:T(8,128)(2,1)} %get-tuple-element.30) | copy-start | bytes 688132
  68.7 23.7 %copy-start.1 = (bf16[64,1792]{1,0:T(8,128)(2,1)S(1)}, bf16[64,1792]{1,0:T(8,128)(2,1)}, u32[]{:S(2)}) copy-start(bf16[64,1792]{1,0:T(8,128)(2,1)} %get-tuple-element.27.refs_0_) | copy-start | bytes 688132
  68.7 41.4 %all-to-all-start.2 = ((bf16[16,64,256]{2,1,0:T(8,128)(2,1)}), bf16[16,64,256]{2,1,0:T(8,128)(2,1)S(1)}, u32[]{:S(2)}, u32[]{:S(2)}) async-start(bf16[16,64,256]{2,1,0:T(8,128)(2,1)} %hidden.1), calls=%async_computation.2 | async-start | bytes 1048576 | tf_op jit(solution)/shard_map/all_to_all | solution.py:301
  72.5 15.0 %collective-permute-start.4 = (bf16[64,1792]{1,0:T(8,128)(2,1)S(1)}, bf16[64,1792]{1,0:T(8,128)(2,1)S(1)}, u32[]{:S(2)}, u32[]{:S(2)}) collective-permute-start(bf16[64,1792]{1,0:T(8,128)(2,1)S(1)} %copy-done.7), channel_id=1, source_target_pairs={{0,2},{1,3},{2,4},{3,5},{4,6},{5,7},{6,0},{7,1},{8,10},{9,11},{10,... | collective-permute-start | bytes 688136 | tf_op jit(solution)/shard_map/ppermute | solution.py:270
  76.2 16.2 %collective-permute-start.5 = (bf16[64,1792]{1,0:T(8,128)(2,1)S(1)}, bf16[64,1792]{1,0:T(8,128)(2,1)S(1)}, u32[]{:S(2)}, u32[]{:S(2)}) collective-permute-start(bf16[64,1792]{1,0:T(8,128)(2,1)S(1)} %copy-done.6), channel_id=1, source_target_pairs={{0,4},{1,5},{2,6},{3,7},{4,0},{5,1},{6,2},{7,3},{8,12},{9,13},{10,... | collective-permute-start | bytes 688136 | tf_op jit(solution)/shard_map/ppermute | solution.py:270
  80.8 11.6 %collective-permute-start.6 = (bf16[64,1792]{1,0:T(8,128)(2,1)S(1)}, bf16[64,1792]{1,0:T(8,128)(2,1)S(1)}, u32[]{:S(2)}, u32[]{:S(2)}) collective-permute-start(bf16[64,1792]{1,0:T(8,128)(2,1)S(1)} %copy-done.5), channel_id=1, source_target_pairs={{0,6},{1,7},{2,0},{3,1},{4,2},{5,3},{6,4},{7,5},{8,14},{9,15},{10,... | collective-permute-start | bytes 688136 | tf_op jit(solution)/shard_map/ppermute | solution.py:270
  92.5 7.6 %collective-permute-start.7 = (bf16[256,512]{1,0:T(8,128)(2,1)S(1)}, bf16[256,512]{1,0:T(8,128)(2,1)S(1)}, u32[]{:S(2)}, u32[]{:S(2)}) collective-permute-start(bf16[256,512]{1,0:T(8,128)(2,1)S(1)} %get-tuple-element.32), channel_id=1, source_target_pairs={{0,1},{1,0},{2,3},{3,2},{4,5},{5,4},{6,7},{7,6},{8,9},{9,8},{10,11... | collective-permute-start | bytes 786440 | tf_op jit(solution)/shard_map/ppermute | solution.py:200
  94.4 11.1 %collective-permute-start.8 = (bf16[256,512]{1,0:T(8,128)(2,1)S(1)}, bf16[256,512]{1,0:T(8,128)(2,1)S(1)}, u32[]{:S(2)}, u32[]{:S(2)}) collective-permute-start(bf16[256,512]{1,0:T(8,128)(2,1)S(1)} %get-tuple-element.33), channel_id=1, source_target_pairs={{0,8},{8,0},{1,9},{9,1},{2,10},{10,2},{3,11},{11,3},{4,12},{12,4},... | collective-permute-start | bytes 786440 | tf_op jit(solution)/shard_map/ppermute | solution.py:198
  97.8 12.3 %collective-permute-start.9 = (bf16[256,512]{1,0:T(8,128)(2,1)S(1)}, bf16[256,512]{1,0:T(8,128)(2,1)S(1)}, u32[]{:S(2)}, u32[]{:S(2)}) collective-permute-start(bf16[256,512]{1,0:T(8,128)(2,1)S(1)} %get-tuple-element.34), channel_id=1, source_target_pairs={{0,9},{1,8},{2,11},{3,10},{4,13},{5,12},{6,15},{7,14},{8,1},{9,0},... | collective-permute-start | bytes 786440 | tf_op jit(solution)/shard_map/ppermute | solution.py:199

commit v5 on v3

--- a/solution.py
+++ b/solution.py
@@ -25,17 +25,30 @@
 
 
 def pack_kernel(copies, ring, ids_ref, tok_ref, gate_ref, up_ref, out_ref, block_ref, *refs):
-    held, taken, given = refs
+    ids, tok, packed, held, taken, given, small = refs
+    fetches = [
+        pltpu.make_async_copy(ids_ref, ids, small.at[0]),
+        pltpu.make_async_copy(tok_ref, tok, small.at[1]),
+    ]
+    for fetch in fetches:
+        fetch.start()
     reads = cut_reads(ring, (gate_ref, up_ref), held, taken)
-    peers, capacity, width = out_ref.shape
-    select, _ = slot_onehot(ids_ref[...], peers * capacity, capacity, copies)
-    packed = jnp.dot(select.astype(BF16), tok_ref[...], preferred_element_type=F32)
+    peers, capacity, width = packed.shape
+    for fetch in fetches:
+        fetch.wait()
+    select, _ = slot_onehot(ids[...], peers * capacity, capacity, copies)
+    rows = jnp.dot(select.astype(BF16), tok[...], preferred_element_type=F32)
+    packed[...] = rows.reshape(peers, capacity, width).astype(BF16)
     for read in reads:
         read.wait()
-    write = pltpu.make_async_copy(held, block_ref, given)
-    write.start()
-    out_ref[...] = packed.reshape(peers, capacity, width).astype(BF16)
-    write.wait()
+    writes = [
+        pltpu.make_async_copy(held, block_ref, given.at[0]),
+        pltpu.make_async_copy(packed, out_ref, given.at[1]),
+    ]
+    for write in writes:
+        write.start()
+    for write in writes:
+        write.wait()
 
 
 def mix_kernel(capacity, copies, ids_ref, route_ref, mix_ref):
@@ -128,28 +141,22 @@
     )(*weights)
 
 
-def half_product(block_ref, rows_ref, half):
-    width = rows_ref.shape[1]
-    cols = pl.ds(pl.multiple_of(half * width, 128), width)
-    return lax.dot_general(
-        block_ref[:, cols], rows_ref[...], (((1,), (1,)), ((), ())), preferred_element_type=F32
-    )
-
-
-def near_kernel(rows_ref, *refs):
+def gate_up_kernel(rows_ref, *refs):
     *blocks, out_ref = refs
-    chip, core = lax.axis_index("tensor") // CORES, lax.rem(lax.axis_index("tensor"), CORES)
+    rings, width = len(blocks), rows_ref.shape[2]
+    chip = lax.axis_index("tensor") // CORES
+    dims = (((1,), (1,)), ((), ()))
     for ring, block in enumerate(blocks):
-        source = lax.rem(chip - ring + len(blocks), len(blocks))
-        out_ref[source] = half_product(block, rows_ref, core)
-
-
-def far_kernel(rows_ref, near_ref, *refs):
-    *blocks, out_ref = refs
-    chip, core = lax.axis_index("tensor") // CORES, lax.rem(lax.axis_index("tensor"), CORES)
-    for ring, block in enumerate(blocks):
-        source = lax.rem(chip - ring + len(blocks), len(blocks))
-        out_ref[source] = (near_ref[source] + half_product(block, rows_ref, 1 - core)).astype(BF16)
+        total = None
+        for core in range(CORES):
+            term = lax.dot_general(
+                block[:, core * width : (core + 1) * width],
+                rows_ref[core],
+                dims,
+                preferred_element_type=F32,
+            )
+            total = term if total is None else total + term
+        out_ref[lax.rem(chip - ring + rings, rings)] = total.astype(BF16)
 
 
 def hidden_kernel(partial_ref, out_ref):
@@ -193,7 +200,7 @@
     return near, lax.ppermute(far, "tensor", shift_pairs(groups, 0, 1))
 
 
-def down_kernel(hidden_ref, near_ref, far_ref, out_ref, held):
+def down_kernel(hidden_ref, near_ref, far_ref, keep_ref, give_ref, held, rows):
     groups, units, _ = hidden_ref.shape
     me = lax.axis_index("tensor")
     for core in range(CORES):
@@ -203,7 +210,12 @@
     dims = (((0,), (0,)), ((), ()))
     total = lax.dot_general(held[0], near_ref[...], dims, preferred_element_type=F32)
     total = total + lax.dot_general(held[1], far_ref[...], dims, preferred_element_type=F32)
-    out_ref[...] = total.astype(BF16)
+    rows[...] = total.reshape(rows.shape)
+    slots = keep_ref.shape[1]
+    half = lax.rem(lax.axis_index("expert"), 2)
+    low, high = rows[:, :slots, :], rows[:, slots:, :]
+    keep_ref[...] = jnp.where(half == 0, low, high).astype(BF16)
+    give_ref[...] = jnp.where(half == 0, high, low).astype(BF16)
 
 
 def body(tokens, expert_ids, route_weights, gate_weight, up_weight, down_weight):
@@ -220,22 +232,26 @@
     rings, wide = groups // CORES, CORES * width
     gate_up = (gate_weight[0], up_weight[0])
     part = jax.ShapeDtypeStruct((2 * units, wide), BF16)
-    whole, held = pl.BlockSpec(memory_space=pl.ANY), pl.BlockSpec(memory_space=pltpu.VMEM)
+    whole = pl.BlockSpec(memory_space=pl.ANY)
     packed, across = pl.pallas_call(
         lambda *refs: pack_kernel(2, 2, *refs),
         out_shape=[jax.ShapeDtypeStruct((devices_wide, capacity, width), BF16), part],
-        in_specs=[held, held, whole, whole],
-        out_specs=[held, whole],
+        in_specs=[whole] * 4,
+        out_specs=[whole] * 2,
         scratch_shapes=[
+            pltpu.VMEM(ids.shape, jnp.int32),
+            pltpu.VMEM(tokens.shape, BF16),
+            pltpu.VMEM((devices_wide, capacity, width), BF16),
             pltpu.VMEM(part.shape, BF16),
             pltpu.SemaphoreType.DMA((2,)),
-            pltpu.SemaphoreType.DMA,
+            pltpu.SemaphoreType.DMA((2,)),
+            pltpu.SemaphoreType.DMA((2,)),
         ],
         name="pack",
     )(ids, tokens, *gate_up)
     mix = pl.pallas_call(
-        lambda *refs: mix_kernel(capacity, 2, *refs),
-        out_shape=jax.ShapeDtypeStruct((arrived_count, tok_count), F32),
+        lambda *refs: mix_kernel(capacity, 1, *refs),
+        out_shape=jax.ShapeDtypeStruct((experts * capacity, tok_count), F32),
         compiler_params=pltpu.CompilerParams(vmem_limit_bytes=VMEM_BYTES),
         name="mix",
     )(ids, route_weights.T)
@@ -250,20 +266,22 @@
     arrived = arrived.reshape(arrived_count, width)
     down_near, down_far = down_columns(down_weight[0], width, groups)
 
-    partner = lax.ppermute(arrived, "tensor", shift_pairs(groups, 0, 1))
-    near = pl.pallas_call(
-        near_kernel,
-        out_shape=jax.ShapeDtypeStruct((rings, 2 * units, arrived_count), F32),
-        compiler_params=pltpu.CompilerParams(vmem_limit_bytes=VMEM_BYTES),
-        cost_estimate=pl.CostEstimate(flops=10**9, bytes_accessed=10**6, transcendentals=0),
-        name="near",
-    )(arrived, *blocks)
+    arrived, *blocks = lax.optimization_barrier((arrived, *blocks))
+    one_chip = [[chip * CORES + core for core in range(CORES)] for chip in range(rings)]
+    rows = lax.all_to_all(
+        jnp.broadcast_to(arrived, (CORES, *arrived.shape)),
+        "tensor",
+        0,
+        0,
+        axis_index_groups=one_chip,
+        tiled=True,
+    )
     partial = pl.pallas_call(
-        far_kernel,
+        gate_up_kernel,
         out_shape=jax.ShapeDtypeStruct((rings, 2 * units, arrived_count), BF16),
         compiler_params=pltpu.CompilerParams(vmem_limit_bytes=VMEM_BYTES),
-        name="far",
-    )(partner, near, *blocks)
+        name="gate_up",
+    )(rows, *blocks)
     same_core = [list(range(core, groups, CORES)) for core in range(CORES)]
     partial = lax.all_to_all(
         partial, "tensor", 0, 0, axis_index_groups=same_core, tiled=True
@@ -276,16 +294,22 @@
     )(partial)
     hidden, mix = lax.optimization_barrier((hidden, mix))
     hidden = lax.all_to_all(hidden, "tensor", 0, 0, tiled=True)
-    half_out = pl.pallas_call(
+    slots = capacity // 2
+    kept, given = pl.pallas_call(
         down_kernel,
-        out_shape=jax.ShapeDtypeStruct((arrived_count, width), BF16),
-        scratch_shapes=[pltpu.VMEM((2, groups // 2 * units, arrived_count), BF16)],
+        out_shape=[jax.ShapeDtypeStruct((devices_wide, slots, width), BF16)] * 2,
+        scratch_shapes=[
+            pltpu.VMEM((2, groups // 2 * units, arrived_count), BF16),
+            pltpu.VMEM((devices_wide, capacity, width), F32),
+        ],
         compiler_params=pltpu.CompilerParams(vmem_limit_bytes=VMEM_BYTES),
         name="down",
     )(hidden, down_near, down_far)
-    returned = lax.all_to_all(
-        half_out.reshape(devices_wide, capacity, width), "expert", 0, 0, tiled=True
-    ).reshape(arrived_count, width)
+    pairs = [(i, i + 1 - 2 * (i % 2)) for i in range(devices_wide)]
+    taken = lax.ppermute(given, "expert", pairs)
+    both = (kept.astype(F32) + taken.astype(F32)).astype(BF16)
+    returned = lax.all_to_all(both, "expert", 0, 0, tiled=True)
+    returned = returned.reshape(devices_wide * slots, width)
     return pl.pallas_call(
         combine_kernel,
         out_shape=jax.ShapeDtypeStruct((tok_count, width), BF16),

time: 140 us -> 144 us (1.029)
  waiting for transfers between devices: 29.9 us -> 39.3 us
  blocking collectives: 43.2 us -> 37.8 us
  Pallas kernels: 13.1 us -> 11.3 us
  local copies, waits for them, and re-layouts: 0.34 us -> 2.09 us
    ppermute x3, waiting for transfers between devices: 8.62 us -> 19.6 us  [down_columns(): lax.ppermute(blocks[ring], 'tensor', shift_pairs(groups, ring, 0))]
    all_to_all x1, waiting for transfers between devices: 6.77 us -> 0.01 us  [body(): arrived = lax.all_to_all(packed, 'expert', 0, 0, tiled=True)]
    ppermute x1, waiting for transfers between devices: 0.01 us -> 5.5 us  [body(): taken = lax.ppermute(given, 'expert', pairs)]
    all_to_all x1 -> x2, blocking collectives: 43.2 us -> 37.8 us  [the longest x1 33.2 us: body(): returned = lax.all_to_all(both, 'expert', 0, 0, tiled=True)]
    ppermute x3, starting transfers between devices: 13.3 us -> 9.72 us  [down_columns(): lax.ppermute(blocks[ring], 'tensor', shift_pairs(groups, ring, 0))]
    ppermute x3, starting transfers between devices: 9.12 us -> 10.7 us  [body(): lax.ppermute(blocks[ring], 'tensor', shift_pairs(groups, ring, 0))]
    ppermute x1, starting transfers between devices: 1.92 us -> 3.37 us  [body(): taken = lax.ppermute(given, 'expert', pairs)]
    pallas_call x4 -> x3, Pallas kernels: 2.87 us -> 3.04 us  [the longest x1 2 us: body(): pl.pallas_call(gate_up_kernel, out_shape=jax.ShapeDtypeStruct((rings, 2 *...]
  transfers between devices with their start and end apart: 11 -> 11, of which waited for: 4 -> 5; matrix products, arithmetic and copies ran while one was open for 0% -> 1% of each run, Pallas kernels for 6% -> 5%
where the time goes in v5:
time: 144 us; the launch traced here: 143 us
  starting transfers between devices  52.1 us (36%)
  waiting for transfers between devices  39.3 us (27%)
  blocking collectives  37.8 us (26%)
  Pallas kernels  11.3 us (8%)
  local copies, waits for them, and re-layouts  2.09 us (1%)
    all_to_all x1, blocking collectives, body(): returned = lax.all_to_all(both, 'expert', 0, 0, tiled=True)  33.2 us
    ppermute x3, waiting for transfers between devices, down_columns(): lax.ppermute(blocks[ring], 'tensor', shift_pairs(groups, ring, 0))  19.6 us
    all_to_all x1, starting transfers between devices, body(): arrived = lax.all_to_all(packed, 'expert', 0, 0, tiled=True)  18.8 us
    ppermute x3, starting transfers between devices, body(): lax.ppermute(blocks[ring], 'tensor', shift_pairs(groups, ring, 0))  10.7 us
    ppermute x3, starting transfers between devices, down_columns(): lax.ppermute(blocks[ring], 'tensor', shift_pairs(groups, ring, 0))  9.72 us
    all_to_all x1, waiting for transfers between devices, body(): hidden = lax.all_to_all(hidden, 'tensor', 0, 0, tiled=True)  7.42 us
    all_to_all x1, waiting for transfers between devices, body(): lax.all_to_all(partial, 'tensor', 0, 0, axis_index_groups=same_core, tile...  6.78 us
    ppermute x1, waiting for transfers between devices, body(): taken = lax.ppermute(given, 'expert', pairs)  5.5 us
  transfers between devices with their start and end apart: 11, of which 5 were waited for; matrix products, arithmetic and copies ran while one was open for 1% of the time, Pallas kernels for 5%

profile of v5, /device:TPU:6, one launch (start us, length us, event | category | flops | bytes accessed | tf_op | source)
XLA Modules:
  0.0 143.0 jit_solution(8046140392430729119)
XLA Ops:
  0.0 2.2 %pack.1 = (bf16[64,4,896]{2,1,0:T(4,128)(2,1)}, bf16[128,1792]{1,0:T(8,128)(2,1)}) custom-call(s32[8,16]{1,0:T(8,128)} %bitcast.5, bf16[16,896]{1,0:T(8,128)(2,1)} %refs_1_.1, bf16[64,7168]{1,0:T(8,128)(2,1)} %bitcast.8, bf16[64,7168]{1,0:T(8,128)(2,1)} %bitcast.10), custom_call_target="tpu_custom_call" | custom-call | tf_op jit(solution)/shard_map/pack/pallas_call | solution.py:236
  2.2 18.8 %all-to-all-start = ((bf16[64,4,896]{2,1,0:T(4,128)(2,1)}), bf16[64,4,896]{2,1,0:T(4,128)(2,1)S(1)}, u32[]{:S(2)}, u32[]{:S(2)}) async-start(bf16[64,4,896]{2,1,0:T(4,128)(2,1)} %get-tuple-element.25), calls=%async_computation | async-start | bytes 917504 | tf_op jit(solution)/shard_map/all_to_all | solution.py:265
  21.0 2.1 %cut.3 = (bf16[64,1792]{1,0:T(8,128)(2,1)}, bf16[64,1792]{1,0:T(8,128)(2,1)}, bf16[64,1792]{1,0:T(8,128)(2,1)}, bf16[64,1792]{1,0:T(8,128)(2,1)}) custom-call(bf16[64,7168]{1,0:T(8,128)(2,1)} %bitcast.12), custom_call_target="tpu_custom_call" | custom-call | tf_op jit(solution)/shard_map/cut/pallas_call | solution.py:130
  23.1 0.0 copy-start.5
  23.1 0.0 copy-start.4
  23.1 0.0 copy-start.1
  23.1 3.6 %collective-permute-start.3 = (bf16[64,1792]{1,0:T(8,128)(2,1)}, bf16[64,1792]{1,0:T(8,128)(2,1)S(1)}, u32[]{:S(2)}, u32[]{:S(2)}) collective-permute-start(bf16[64,1792]{1,0:T(8,128)(2,1)} %get-tuple-element.38), channel_id=1, source_target_pairs={{0,2},{1,3},{2,4},{3,5},{4,6},{5,7},{6,0},{7,1},{8,10},{9,11},{10,... | collective-permute-start | bytes 688136 | tf_op jit(solution)/shard_map/ppermute | solution.py:191
  26.7 2.3 %cut.2 = (bf16[128,1792]{1,0:T(8,128)(2,1)}, bf16[128,1792]{1,0:T(8,128)(2,1)}, bf16[128,1792]{1,0:T(8,128)(2,1)}) custom-call(bf16[64,7168]{1,0:T(8,128)(2,1)} %bitcast.9, bf16[64,7168]{1,0:T(8,128)(2,1)} %bitcast.11), custom_call_target="tpu_custom_call" | custom-call | tf_op jit(solution)/shard_map/cut/pallas_call | solution.py:130
  29.1 3.5 %collective-permute-start = (bf16[128,1792]{1,0:T(8,128)(2,1)}, bf16[128,1792]{1,0:T(8,128)(2,1)S(1)}, u32[]{:S(2)}, u32[]{:S(2)}) collective-permute-start(bf16[128,1792]{1,0:T(8,128)(2,1)} %get-tuple-element.27), channel_id=1, source_target_pairs={{0,2},{1,3},{2,4},{3,5},{4,6},{5,7},{6,0},{7,1},{8,10},{9,11},{10,... | collective-permute-start | bytes 1376264 | tf_op jit(solution)/shard_map/ppermute | solution.py:262
  32.5 3.6 %collective-permute-start.2 = (bf16[128,1792]{1,0:T(8,128)(2,1)}, bf16[128,1792]{1,0:T(8,128)(2,1)S(1)}, u32[]{:S(2)}, u32[]{:S(2)}) collective-permute-start(bf16[128,1792]{1,0:T(8,128)(2,1)} %get-tuple-element.29), channel_id=1, source_target_pairs={{0,6},{1,7},{2,0},{3,1},{4,2},{5,3},{6,4},{7,5},{8,14},{9,15},{10,... | collective-permute-start | bytes 1376264 | tf_op jit(solution)/shard_map/ppermute | solution.py:262
  36.1 3.6 %collective-permute-start.1 = (bf16[128,1792]{1,0:T(8,128)(2,1)}, bf16[128,1792]{1,0:T(8,128)(2,1)S(1)}, u32[]{:S(2)}, u32[]{:S(2)}) collective-permute-start(bf16[128,1792]{1,0:T(8,128)(2,1)} %get-tuple-element.28), channel_id=1, source_target_pairs={{0,4},{1,5},{2,6},{3,7},{4,0},{5,1},{6,2},{7,3},{8,12},{9,13},{10,... | collective-permute-start | bytes 1376264 | tf_op jit(solution)/shard_map/ppermute | solution.py:262
  39.7 0.0 copy-done.5
  39.7 3.7 %collective-permute-start.4 = (bf16[64,1792]{1,0:T(8,128)(2,1)S(1)}, bf16[64,1792]{1,0:T(8,128)(2,1)S(1)}, u32[]{:S(2)}, u32[]{:S(2)}) collective-permute-start(bf16[64,1792]{1,0:T(8,128)(2,1)S(1)} %copy-done.5), channel_id=1, source_target_pairs={{0,4},{1,5},{2,6},{3,7},{4,0},{5,1},{6,2},{7,3},{8,12},{9,13},{10,... | collective-permute-start | bytes 688136 | tf_op jit(solution)/shard_map/ppermute | solution.py:191
  43.5 0.0 collective-permute-done.3.refs_1_
  43.5 0.0 copy-done.4
  43.5 2.4 %collective-permute-start.5 = (bf16[64,1792]{1,0:T(8,128)(2,1)S(1)}, bf16[64,1792]{1,0:T(8,128)(2,1)S(1)}, u32[]{:S(2)}, u32[]{:S(2)}) collective-permute-start(bf16[64,1792]{1,0:T(8,128)(2,1)S(1)} %copy-done.4), channel_id=1, source_target_pairs={{0,6},{1,7},{2,0},{3,1},{4,2},{5,3},{6,4},{7,5},{8,14},{9,15},{10,... | collective-permute-start | bytes 688136 | tf_op jit(solution)/shard_map/ppermute | solution.py:191
  45.9 13.3 %collective-permute-done.4.refs_2_ = bf16[64,1792]{1,0:T(8,128)(2,1)S(1)} collective-permute-done((bf16[64,1792]{1,0:T(8,128)(2,1)S(1)}, bf16[64,1792]{1,0:T(8,128)(2,1)S(1)}, u32[]{:S(2)}, u32[]{:S(2)}) %collective-permute-start.4) | collective-permute-done | bytes 229408 | tf_op jit(solution)/shard_map/ppermute | solution.py:191
  59.2 6.3 %collective-permute-done.5.refs_3_ = bf16[64,1792]{1,0:T(8,128)(2,1)S(1)} collective-permute-done((bf16[64,1792]{1,0:T(8,128)(2,1)S(1)}, bf16[64,1792]{1,0:T(8,128)(2,1)S(1)}, u32[]{:S(2)}, u32[]{:S(2)}) %collective-permute-start.5) | collective-permute-done | bytes 229408 | tf_op jit(solution)/shard_map/ppermute | solution.py:191
  65.5 0.0 copy-done.1
  65.5 0.1 core_cut.1
  65.6 1.9 %collective-permute-start.6 = (bf16[256,896]{1,0:T(8,128)(2,1)S(1)}, bf16[256,896]{1,0:T(8,128)(2,1)S(1)}, u32[]{:S(2)}, u32[]{:S(2)}) collective-permute-start(bf16[256,896]{1,0:T(8,128)(2,1)S(1)} %get-tuple-element.42), channel_id=1, source_target_pairs={{0,1},{1,0},{2,3},{3,2},{4,5},{5,4},{6,7},{7,6},{8,9},{9,8},{10,11... | collective-permute-start | bytes 1376264 | tf_op jit(solution)/shard_map/ppermute | solution.py:200
  67.5 0.0 all-to-all-done
  67.5 0.9 reshape.6
  68.4 0.0 collective-permute-done.refs_1_
  68.4 0.0 collective-permute-done.2.refs_3_
  68.4 0.0 collective-permute-done.1.refs_2_
  68.4 1.1 broadcast_in_dim.3
  69.5 0.0 copy-start
  69.5 4.6 %all_to_all.25.rows_ref = bf16[2,256,896]{2,1,0:T(8,128)(2,1)S(1)} all-to-all(bf16[2,256,896]{2,1,0:T(8,128)(2,1)S(1)} %broadcast_in_dim.3), channel_id=1, replica_groups={{0,1},{2,3},{4,5},{6,7},{8,9},{10,11},{12,13},{14,15},{16,17},{18,19},{..., dimensions={0} | all-to-all | bytes 1835008 | tf_op jit(solution)/shard_map/all_to_all | solution.py:271
  74.1 0.0 copy-done
  74.1 2.0 %gate_up.1 = bf16[4,128,256]{2,1,0:T(8,128)(2,1)} custom-call(bf16[2,256,896]{2,1,0:T(8,128)(2,1)S(1)} %all_to_all.25.rows_ref, bf16[128,1792]{1,0:T(8,128)(2,1)S(1)} %copy-done, bf16[128,1792]{1,0:T(8,128)(2,1)S(1)} %collective-permute-done.refs_1_, bf16[128,1792]{1,0:T(8,128)(2,1)S(1)} %collective-permute-done.1.refs_2_, ...), custom_call_target="tpu_custom_call" | custom-call | tf_op jit(solution)/shard_map/gate_up/pallas_call | solution.py:279
  76.1 0.0 copy-start.2
  76.1 4.2 %all-to-all-start.2 = ((bf16[4,128,256]{2,1,0:T(8,128)(2,1)}), bf16[4,128,256]{2,1,0:T(8,128)(2,1)S(1)}, u32[]{:S(2)}, u32[]{:S(2)}) async-start(bf16[4,128,256]{2,1,0:T(8,128)(2,1)} %gate_up.1), calls=%async_computation.2 | async-start | bytes 524288 | tf_op jit(solution)/shard_map/all_to_all | solution.py:286
  80.4 0.0 copy-done.2
  80.4 0.0 copy-done.3
  80.4 0.2 mix.1.mix_ref
  80.5 6.8 %all-to-all-done.2.partial_ref = bf16[4,128,256]{2,1,0:T(8,128)(2,1)S(1)} async-done(((bf16[4,128,256]{2,1,0:T(8,128)(2,1)}), bf16[4,128,256]{2,1,0:T(8,128)(2,1)S(1)}, u32[]{:S(2)}, u32[]{:S(2)}) %all-to-all-start.2) | async-done | bytes 262176 | tf_op jit(solution)/shard_map/all_to_all | solution.py:286
  87.3 0.8 hidden.1
  88.1 3.4 %all-to-all-start.3 = ((bf16[8,64,256]{2,1,0:T(8,128)(2,1)}), bf16[8,64,256]{2,1,0:T(8,128)(2,1)S(1)}, u32[]{:S(2)}, u32[]{:S(2)}) async-start(bf16[8,64,256]{2,1,0:T(8,128)(2,1)} %hidden.1), calls=%async_computation.3 | async-start | bytes 524288 | tf_op jit(solution)/shard_map/all_to_all | solution.py:296
  91.5 0.0 collective-permute-done.6.far_ref
  91.5 7.4 %all-to-all-done.3.hidden_ref = bf16[8,64,256]{2,1,0:T(8,128)(2,1)S(1)} async-done(((bf16[8,64,256]{2,1,0:T(8,128)(2,1)}), bf16[8,64,256]{2,1,0:T(8,128)(2,1)S(1)}, u32[]{:S(2)}, u32[]{:S(2)}) %all-to-all-start.3) | async-done | bytes 262176 | tf_op jit(solution)/shard_map/all_to_all | solution.py:296
  98.9 0.9 down.1
  99.8 3.4 %collective-permute-start.7 = (bf16[64,2,896]{2,1,0:T(2,128)(2,1)S(1)}, bf16[64,2,896]{2,1,0:T(2,128)(2,1)S(1)}, u32[]{:S(2)}, u32[]{:S(2)}) collective-permute-start(bf16[64,2,896]{2,1,0:T(2,128)(2,1)S(1)} %get-tuple-element.44), channel_id=1, source_target_pairs={{0,8},{8,0},{16,24},{24,16},{32,40},{40,32},{48,56},{56,48},{64,72... | collective-permute-start | bytes 688136 | tf_op jit(solution)/shard_map/ppermute | solution.py:309
  103.2 5.5 %collective-permute-done.7 = bf16[64,2,896]{2,1,0:T(2,128)(2,1)S(1)} collective-permute-done((bf16[64,2,896]{2,1,0:T(2,128)(2,1)S(1)}, bf16[64,2,896]{2,1,0:T(2,128)(2,1)S(1)}, u32[]{:S(2)}, u32[]{:S(2)}) %collective-permute-start.7) | collective-permute-done | bytes 229408 | tf_op jit(solution)/shard_map/ppermute | solution.py:309
  108.7 0.2 add_convert_fusion
  108.9 33.2 %all_to_all.26 = bf16[64,2,896]{2,1,0:T(2,128)(2,1)S(1)} all-to-all(bf16[64,2,896]{2,1,0:T(2,128)(2,1)S(1)} %add_convert_fusion), channel_id=1, replica_groups=mesh['expert'=64,'tensor'=8] {'expert'}, dimensions={0} | all-to-all | bytes 458752 | tf_op jit(solution)/shard_map/all_to_all | solution.py:311
  142.1 0.1 reshape.7.rows_ref
  142.2 0.8 combine.1
  (1 shorter events, 0.0 us)
Async XLA Ops:
  2.2 65.3 %all-to-all-start = ((bf16[64,4,896]{2,1,0:T(4,128)(2,1)}), bf16[64,4,896]{2,1,0:T(4,128)(2,1)S(1)}, u32[]{:S(2)}, u32[]{:S(2)}) async-start(bf16[64,4,896]{2,1,0:T(4,128)(2,1)} %get-tuple-element.25), calls=%async_computation | async-start | bytes 917504 | tf_op jit(solution)/shard_map/all_to_all | solution.py:265
  23.1 16.7 %copy-start.5 = (bf16[64,1792]{1,0:T(8,128)(2,1)S(1)}, bf16[64,1792]{1,0:T(8,128)(2,1)}, u32[]{:S(2)}) copy-start(bf16[64,1792]{1,0:T(8,128)(2,1)} %get-tuple-element.39) | copy-start | bytes 688132
  23.1 20.4 %copy-start.4 = (bf16[64,1792]{1,0:T(8,128)(2,1)S(1)}, bf16[64,1792]{1,0:T(8,128)(2,1)}, u32[]{:S(2)}) copy-start(bf16[64,1792]{1,0:T(8,128)(2,1)} %get-tuple-element.40) | copy-start | bytes 688132
  23.1 42.4 %copy-start.1 = (bf16[64,1792]{1,0:T(8,128)(2,1)S(1)}, bf16[64,1792]{1,0:T(8,128)(2,1)}, u32[]{:S(2)}) copy-start(bf16[64,1792]{1,0:T(8,128)(2,1)} %get-tuple-element.37.refs_0_) | copy-start | bytes 688132
  23.1 20.4 %collective-permute-start.3 = (bf16[64,1792]{1,0:T(8,128)(2,1)}, bf16[64,1792]{1,0:T(8,128)(2,1)S(1)}, u32[]{:S(2)}, u32[]{:S(2)}) collective-permute-start(bf16[64,1792]{1,0:T(8,128)(2,1)} %get-tuple-element.38), channel_id=1, source_target_pairs={{0,2},{1,3},{2,4},{3,5},{4,6},{5,7},{6,0},{7,1},{8,10},{9,11},{10,... | collective-permute-start | bytes 688136 | tf_op jit(solution)/shard_map/ppermute | solution.py:191
  29.1 39.4 %collective-permute-start = (bf16[128,1792]{1,0:T(8,128)(2,1)}, bf16[128,1792]{1,0:T(8,128)(2,1)S(1)}, u32[]{:S(2)}, u32[]{:S(2)}) collective-permute-start(bf16[128,1792]{1,0:T(8,128)(2,1)} %get-tuple-element.27), channel_id=1, source_target_pairs={{0,2},{1,3},{2,4},{3,5},{4,6},{5,7},{6,0},{7,1},{8,10},{9,11},{10,... | collective-permute-start | bytes 1376264 | tf_op jit(solution)/shard_map/ppermute | solution.py:262
  32.5 35.9 %collective-permute-start.2 = (bf16[128,1792]{1,0:T(8,128)(2,1)}, bf16[128,1792]{1,0:T(8,128)(2,1)S(1)}, u32[]{:S(2)}, u32[]{:S(2)}) collective-permute-start(bf16[128,1792]{1,0:T(8,128)(2,1)} %get-tuple-element.29), channel_id=1, source_target_pairs={{0,6},{1,7},{2,0},{3,1},{4,2},{5,3},{6,4},{7,5},{8,14},{9,15},{10,... | collective-permute-start | bytes 1376264 | tf_op jit(solution)/shard_map/ppermute | solution.py:262
  36.1 32.3 %collective-permute-start.1 = (bf16[128,1792]{1,0:T(8,128)(2,1)}, bf16[128,1792]{1,0:T(8,128)(2,1)S(1)}, u32[]{:S(2)}, u32[]{:S(2)}) collective-permute-start(bf16[128,1792]{1,0:T(8,128)(2,1)} %get-tuple-element.28), channel_id=1, source_target_pairs={{0,4},{1,5},{2,6},{3,7},{4,0},{5,1},{6,2},{7,3},{8,12},{9,13},{10,... | collective-permute-start | bytes 1376264 | tf_op jit(solution)/shard_map/ppermute | solution.py:262
  39.7 19.4 %collective-permute-start.4 = (bf16[64,1792]{1,0:T(8,128)(2,1)S(1)}, bf16[64,1792]{1,0:T(8,128)(2,1)S(1)}, u32[]{:S(2)}, u32[]{:S(2)}) collective-permute-start(bf16[64,1792]{1,0:T(8,128)(2,1)S(1)} %copy-done.5), channel_id=1, source_target_pairs={{0,4},{1,5},{2,6},{3,7},{4,0},{5,1},{6,2},{7,3},{8,12},{9,13},{10,... | collective-permute-start | bytes 688136 | tf_op jit(solution)/shard_map/ppermute | solution.py:191
  43.5 22.0 %collective-permute-start.5 = (bf16[64,1792]{1,0:T(8,128)(2,1)S(1)}, bf16[64,1792]{1,0:T(8,128)(2,1)S(1)}, u32[]{:S(2)}, u32[]{:S(2)}) collective-permute-start(bf16[64,1792]{1,0:T(8,128)(2,1)S(1)} %copy-done.4), channel_id=1, source_target_pairs={{0,6},{1,7},{2,0},{3,1},{4,2},{5,3},{6,4},{7,5},{8,14},{9,15},{10,... | collective-permute-start | bytes 688136 | tf_op jit(solution)/shard_map/ppermute | solution.py:191
  65.6 25.9 %collective-permute-start.6 = (bf16[256,896]{1,0:T(8,128)(2,1)S(1)}, bf16[256,896]{1,0:T(8,128)(2,1)S(1)}, u32[]{:S(2)}, u32[]{:S(2)}) collective-permute-start(bf16[256,896]{1,0:T(8,128)(2,1)S(1)} %get-tuple-element.42), channel_id=1, source_target_pairs={{0,1},{1,0},{2,3},{3,2},{4,5},{5,4},{6,7},{7,6},{8,9},{9,8},{10,11... | collective-permute-start | bytes 1376264 | tf_op jit(solution)/shard_map/ppermute | solution.py:200
  69.5 4.6 %copy-start = (bf16[128,1792]{1,0:T(8,128)(2,1)S(1)}, bf16[128,1792]{1,0:T(8,128)(2,1)}, u32[]{:S(2)}) copy-start(bf16[128,1792]{1,0:T(8,128)(2,1)} %get-tuple-element.31.refs_0_) | copy-start | bytes 1376260
  76.1 4.2 %copy-start.2 = (s32[16,8]{0,1:T(8,128)S(1)}, s32[16,8]{0,1:T(8,128)}, u32[]{:S(2)}) copy-start(s32[16,8]{0,1:T(8,128)} %param.7) | copy-start | bytes 1540
  76.1 4.2 %copy-start.3 = (f32[16,8]{0,1:T(8,128)S(1)}, f32[16,8]{0,1:T(8,128)}, u32[]{:S(2)}) copy-start(f32[16,8]{0,1:T(8,128)} %param.8) | copy-start | bytes 1540
  76.1 11.2 %all-to-all-start.2 = ((bf16[4,128,256]{2,1,0:T(8,128)(2,1)}), bf16[4,128,256]{2,1,0:T(8,128)(2,1)S(1)}, u32[]{:S(2)}, u32[]{:S(2)}) async-start(bf16[4,128,256]{2,1,0:T(8,128)(2,1)} %gate_up.1), calls=%async_computation.2 | async-start | bytes 524288 | tf_op jit(solution)/shard_map/all_to_all | solution.py:286
  88.1 10.8 %all-to-all-start.3 = ((bf16[8,64,256]{2,1,0:T(8,128)(2,1)}), bf16[8,64,256]{2,1,0:T(8,128)(2,1)S(1)}, u32[]{:S(2)}, u32[]{:S(2)}) async-start(bf16[8,64,256]{2,1,0:T(8,128)(2,1)} %hidden.1), calls=%async_computation.3 | async-start | bytes 524288 | tf_op jit(solution)/shard_map/all_to_all | solution.py:296
  99.8 8.9 %collective-permute-start.7 = (bf16[64,2,896]{2,1,0:T(2,128)(2,1)S(1)}, bf16[64,2,896]{2,1,0:T(2,128)(2,1)S(1)}, u32[]{:S(2)}, u32[]{:S(2)}) collective-permute-start(bf16[64,2,896]{2,1,0:T(2,128)(2,1)S(1)} %get-tuple-element.44), channel_id=1, source_target_pairs={{0,8},{8,0},{16,24},{24,16},{32,40},{40,32},{48,56},{56,48},{64,72... | collective-permute-start | bytes 688136 | tf_op jit(solution)/shard_map/ppermute | solution.py:309
